TPU v7x, 32 devices: a whole 2x2x4 slice. The times are simulated.
32 devices in a mesh: dp: 4 (over z), pipe: 4 (over x, core), ctx: 2 (over y).
Axes of the slice: x: 2, y: 2, z: 4, core: 2. Of those that a mesh axis runs over, the one named last changes fastest.
Arguments:
- projected: bfloat16 [4, 4, 256, 2304], P('pipe', 'dp', 'ctx'), may hold values from -40 to 40
- gated_input: bfloat16 [4, 4, 256, 1536], P('pipe', 'dp', 'ctx'), may hold values from -6 to 6
- upstream: bfloat16 [4, 4, 256, 2304], P('pipe', 'dp', 'ctx'), may hold values from -6 to 6
- lengths: int32 [4, 4], P('pipe', 'dp'), may hold values from 64 to 256, as said below
- depth_kernel: float32 [4, 31, 1536], P('pipe'), may hold values from -1 to 1
- depth_bias: float32 [4, 1536], P('pipe'), may hold values from -3 to 3
Outputs:
- attention_out: bfloat16 [4, 4, 256, 768], P('pipe', 'dp', 'ctx')
- depth_out: bfloat16 [4, 4, 256, 1536], P('pipe', 'dp', 'ctx')
- projected_grad: bfloat16 [4, 4, 256, 2304], P('pipe', 'dp', 'ctx')
- gated_grad: bfloat16 [4, 4, 256, 1536], P('pipe', 'dp', 'ctx')
- kernel_grad: float32 [4, 31, 1536], P('pipe')
- bias_grad: float32 [4, 1536], P('pipe')
Inputs may be any that keep to these rules, and one draw needn't show every extreme that they name: `lengths`: frames after a recording's length are padding; in every draw some recording has all 256 frames.
All inputs are finite; a program needn't handle non-finite values.
Results may differ from a plain program's by a relative error of at most 0.0069.
Values may be sent and summed in bfloat16 or wider, within the bound.
No kernel may reach another device: no remote copies, remote signals or barrier semaphores. Data moves between devices by JAX's collectives and lax.ppermute only.
A program may use at most 64 MiB of HBM per device.

v0:
```python
import math

import jax
import jax.numpy as jnp
from jax import lax
from jax.sharding import PartitionSpec as P

HEADS = 8
HD = 96
KSIZE = 31


def shifted(value, axis, by):
    count = lax.axis_size(axis)
    return lax.ppermute(value, axis, [(i, (i + by) % count) for i in range(count)])


def padded_2(block, sides, width):
    for axis, dim in sides:
        count = lax.axis_size(axis)
        forward = [(i, i + 1) for i in range(count - 1)]
        backward = [(target, source) for source, target in forward]
        low = lax.ppermute(
            lax.slice_in_dim(block, block.shape[dim] - width, None, axis=dim), axis, forward
        )
        high = lax.ppermute(lax.slice_in_dim(block, 0, width, axis=dim), axis, backward)
        block = jnp.concatenate([low, block, high], axis=dim)
    return block


def head_pass(queries, grad_out, keys_in, values_in, valid_keys):
    query_rows, head_dim = queries.shape
    score_scale = 1.0 / math.sqrt(head_dim)
    block_rows = min(512, query_rows)
    block_count = query_rows // block_rows
    frame_count = keys_in.shape[0]
    across = (((1,), (1,)), ((), ()))
    downward = (((0,), (0,)), ((), ()))

    def advance(totals, blocks):
        query_block, grad_block = blocks
        scores = (
            lax.dot_general(query_block, keys_in, across, preferred_element_type=jnp.float32)
            * score_scale
        )
        scores = jnp.where(valid_keys[None, :], scores, -1e30)
        row_top = jnp.max(scores, axis=1, keepdims=True)
        row_total = jnp.sum(jnp.exp(scores - row_top), axis=1, keepdims=True)
        probs_bf = (jnp.exp(scores - row_top) / row_total).astype(jnp.bfloat16)
        attended_full = jnp.dot(probs_bf, values_in, preferred_element_type=jnp.float32)
        attended = attended_full.astype(jnp.bfloat16)
        grad_probs = lax.dot_general(
            grad_block, values_in, across, preferred_element_type=jnp.float32
        )
        centre = jnp.sum(grad_block.astype(jnp.float32) * attended_full, axis=1, keepdims=True)
        grad_scores = (probs_bf.astype(jnp.float32) * (grad_probs - centre) * score_scale).astype(
            jnp.bfloat16
        )
        grad_query = jnp.dot(grad_scores, keys_in, preferred_element_type=jnp.float32).astype(
            jnp.bfloat16
        )
        key_total = totals[0] + lax.dot_general(
            grad_scores, query_block, downward, preferred_element_type=jnp.float32
        )
        value_total = totals[1] + lax.dot_general(
            probs_bf, grad_block, downward, preferred_element_type=jnp.float32
        )
        return ((key_total, value_total), (attended, grad_query))

    zero_grads = jnp.zeros((frame_count, head_dim), jnp.float32)
    blocked = (
        queries.reshape(block_count, block_rows, head_dim),
        grad_out.reshape(block_count, block_rows, head_dim),
    )
    totals, results = lax.scan(advance, (zero_grads, zero_grads), blocked)
    attended = results[0].reshape(query_rows, head_dim)
    grad_query = results[1].reshape(query_rows, head_dim)
    return (attended, grad_query, totals[0], totals[1])


def attend_block(query_part, grad_part, key_value, valid_keys, heads_dev):
    block_width = heads_dev * HD

    def split_heads(matrix):
        return matrix.reshape(matrix.shape[0], heads_dev, HD).transpose(1, 0, 2)

    def join_heads(matrix):
        return matrix.transpose(1, 0, 2).reshape(matrix.shape[1], block_width)

    def one_head(items):
        return head_pass(items[0], items[1], items[2], items[3], valid_keys)

    stacked = (
        split_heads(query_part),
        split_heads(grad_part),
        split_heads(key_value[:, :block_width]),
        split_heads(key_value[:, block_width:]),
    )
    attended, grad_query, key_grad, value_grad = lax.map(one_head, stacked)
    key_grads = jnp.concatenate([join_heads(key_grad), join_heads(value_grad)], axis=1)
    return (join_heads(attended), join_heads(grad_query), key_grads)


def depthwise(source, taps, bias, count):
    total = jnp.zeros((count, source.shape[1]), jnp.float32) + bias[None, :]
    for offset in range(KSIZE):
        total = total + taps[offset][None, :] * source[offset : offset + count].astype(jnp.float32)
    return total


def slope(pre_act):
    sigmoid_pre = jax.nn.sigmoid(pre_act)
    return sigmoid_pre + pre_act * sigmoid_pre * (1.0 - sigmoid_pre)


def local(projected, gated_input, upstream, lengths, depth_kernel, depth_bias):
    arriving = shifted(upstream, "pipe", -1)[0, 0]
    rows_here = projected.shape[2]
    devices_ctx = lax.axis_size("ctx")
    frames_all = rows_here * devices_ctx
    embed = HEADS * HD
    part_count = max(devices_ctx // HEADS, 1)
    heads_dev = max(HEADS // devices_ctx, 1)
    block_heads = HEADS // heads_dev
    part_rows = rows_here // part_count
    block_width = heads_dev * HD
    my_index = lax.axis_index("ctx")
    length = lengths[0, 0]
    valid_keys = jnp.arange(frames_all) < length
    frame_mask = my_index * rows_here + jnp.arange(rows_here) < length
    mixed = projected[0, 0]
    queries = mixed[:, :embed]
    keys_in = mixed[:, embed : 2 * embed]
    values_in = mixed[:, 2 * embed :]
    grad_attn = arriving[:, :embed]
    grad_depth = arriving[:, embed:]

    def by_part(matrix):
        split = matrix.reshape(part_count, part_rows, block_heads, block_width).transpose(
            2, 0, 1, 3
        )
        return split.reshape(devices_ctx, part_rows, block_width)

    key_value = jnp.concatenate(
        [
            keys_in.reshape(rows_here, block_heads, block_width),
            values_in.reshape(rows_here, block_heads, block_width),
        ],
        axis=2,
    )
    key_value = jnp.repeat(key_value.transpose(1, 0, 2), part_count, axis=0)
    query_part, grad_part, key_value = (
        lax.all_to_all(by_part(queries), "ctx", split_axis=0, concat_axis=1, tiled=True),
        lax.all_to_all(by_part(grad_attn), "ctx", split_axis=0, concat_axis=1, tiled=True),
        lax.all_to_all(key_value, "ctx", split_axis=0, concat_axis=1, tiled=True),
    )
    query_part = query_part[0]
    grad_part = grad_part[0]
    key_value = key_value[0]
    attended, grad_query, key_grads = attend_block(
        query_part, grad_part, key_value, valid_keys, heads_dev
    )
    outgoing = jnp.concatenate([attended, grad_query], axis=1).reshape(
        devices_ctx, part_rows, 2 * block_width
    )
    returned = lax.all_to_all(outgoing, "ctx", split_axis=0, concat_axis=0, tiled=True)
    key_returned = lax.all_to_all(
        key_grads.reshape(devices_ctx, rows_here, 2 * block_width).astype(jnp.bfloat16),
        "ctx",
        split_axis=0,
        concat_axis=0,
        tiled=True,
    ).astype(jnp.float32)
    columns = 2 * block_width
    split = returned.reshape(block_heads, part_count, part_rows, columns).transpose(1, 2, 0, 3)
    returned = split.reshape(rows_here, block_heads, columns)
    attention_out = returned[:, :, :block_width].reshape(rows_here, embed)
    grad_q = returned[:, :, block_width:].reshape(rows_here, embed)
    summed = jnp.sum(
        key_returned.reshape(block_heads, part_count, rows_here, 2 * block_width), axis=1
    )
    summed = summed.astype(jnp.bfloat16).transpose(1, 0, 2)
    grad_k = summed[:, :, :block_width].reshape(rows_here, embed)
    grad_v = summed[:, :, block_width:].reshape(rows_here, embed)
    half_width = KSIZE // 2
    taps = depth_kernel[0]
    bias = depth_bias[0]
    gated = gated_input[0, 0]
    masked = jnp.where(frame_mask[:, None], gated, jnp.zeros((), jnp.bfloat16))
    padded = padded_2(masked, (("ctx", 0),), half_width)
    pre_act = depthwise(padded, taps, bias, rows_here)
    grad_pre = grad_depth.astype(jnp.float32) * slope(pre_act)
    grad_pad = padded_2(grad_pre, (("ctx", 0),), half_width)
    depth_out = (pre_act * jax.nn.sigmoid(pre_act)).astype(jnp.bfloat16)
    back = jnp.zeros((rows_here, taps.shape[1]), jnp.float32)
    for offset in range(KSIZE):
        start = 2 * half_width - offset
        back = back + taps[offset][None, :] * grad_pad[start : start + rows_here]
    gated_grad = jnp.where(frame_mask[:, None], back, 0.0).astype(jnp.bfloat16)
    kernel_local = jnp.stack(
        [
            jnp.sum(padded[offset : offset + rows_here].astype(jnp.float32) * grad_pre, axis=0)
            for offset in range(KSIZE)
        ]
    )
    bias_local = jnp.sum(grad_pre, axis=0)
    kernel_grad, bias_grad = lax.psum((kernel_local, bias_local), ("dp", "ctx"))
    projected_grad = jnp.concatenate([grad_q, grad_k, grad_v], axis=1)
    return (
        attention_out[None, None],
        depth_out[None, None],
        projected_grad[None, None],
        gated_grad[None, None],
        kernel_grad[None],
        bias_grad[None],
    )


def solution(mesh):
    placed = (
        P("pipe", "dp", "ctx", None),
        P("pipe", "dp", "ctx", None),
        P("pipe", "dp", "ctx", None),
        P("pipe", "dp"),
        P("pipe", None, None),
        P("pipe", None),
    )
    return jax.shard_map(
        local,
        mesh=mesh,
        in_specs=placed,
        out_specs=(
            P("pipe", "dp", "ctx", None),
            P("pipe", "dp", "ctx", None),
            P("pipe", "dp", "ctx", None),
            P("pipe", "dp", "ctx", None),
            P("pipe", None, None),
            P("pipe", None),
        ),
        check_vma=False,
    )
```

profile of v0, /device:TPU:0, one launch (start us, length us, event | category | flops | bytes accessed | tf_op | source)
XLA Modules:
  0.0 200.0 jit_solution(13303225998379243030)
XLA Ops:
  7.2 1.4 copy.80
  9.3 4.4 %all-to-all-start = ((bf16[2,128,384]{1,2,0:T(8,128)(2,1)}), bf16[2,128,384]{1,2,0:T(8,128)(2,1)S(1)}, u32[]{:S(2)}, u32[]{:S(2)}) async-start(bf16[2,128,384]{1,2,0:T(8,128)(2,1)} %bitcast.3), calls=%async_computation | async-start | bytes 393216 | tf_op jit(solution)/shard_map/all_to_all | solution.py:153
  14.7 1.6 collective-permute-start
  18.7 3.6 %collective-permute-start.1 = (bf16[15,1536]{0,1:T(8,128)(2,1)}, bf16[15,1536]{0,1:T(8,128)(2,1)S(1)}, u32[]{:S(2)}, u32[]{:S(2)}) collective-permute-start(bf16[15,1536]{0,1:T(8,128)(2,1)} %get-tuple-element.278), channel_id=1, source_target_pairs={{0,1},{2,3},{4,5},{6,7},{8,9},{10,11},{12,13},{14,15},{16,17},{18,... | collective-permute-start | bytes 138248 | tf_op jit(solution)/shard_map/ppermute | solution.py:23
  22.4 1.3 collective-permute-start.2
  24.5 3.9 %all-to-all-start.1 = ((bf16[2,128,768]{1,2,0:T(8,128)(2,1)}), bf16[2,128,768]{1,2,0:T(8,128)(2,1)S(1)}, u32[]{:S(2)}, u32[]{:S(2)}) async-start(bf16[2,128,768]{1,2,0:T(8,128)(2,1)} %maximum_bitcast_fusion.1), calls=%async_computation.1 | async-start | bytes 786432 | tf_op jit(solution)/shard_map/all_to_all | solution.py:155
  29.6 9.0 %all-to-all-done.1 = bf16[2,128,768]{1,2,0:T(8,128)(2,1)S(1)} async-done(((bf16[2,128,768]{1,2,0:T(8,128)(2,1)}), bf16[2,128,768]{1,2,0:T(8,128)(2,1)S(1)}, u32[]{:S(2)}, u32[]{:S(2)}) %all-to-all-start.1) | async-done | bytes 393248 | tf_op jit(solution)/shard_map/all_to_all | solution.py:155
  41.6 4.1 %all-to-all-start.2 = ((bf16[2,128,384]{2,1,0:T(8,128)(2,1)}), bf16[2,128,384]{2,1,0:T(8,128)(2,1)}, u32[]{:S(2)}, u32[]{:S(2)}) async-start(bf16[2,128,384]{2,1,0:T(8,128)(2,1)} %copy.86), calls=%async_computation.2 | async-start | bytes 393216 | tf_op jit(solution)/shard_map/all_to_all | solution.py:154
  46.2 18.7 %fusion.95 = (f32[1536]{0:T(1024)S(1)}, f32[1536]{0:T(1024)S(1)}, f32[1536]{0:T(1024)S(1)}, f32[1536]{0:T(1024)S(1)}, f32[1536]{0:T(1024)S(1)}, /*index=5*/f32[1...) fusion(bf16[15,1536]{0,1:T(8,128)(2,1)S(1)} %collective-permute, ...), kind=kLoop, calls=%fused_computation.278 | loop fusion | flops 47565312 | bytes 2703360 | tf_op jit(solution)/shard_map/reduce_sum | solution.py:202
  65.0 1.1 fusion.220
  66.1 3.0 %fusion.80 = (f32[1536]{0:T(1024)S(1)}, f32[1536]{0:T(1024)S(1)}, f32[1536]{0:T(1024)S(1)}, f32[1536]{0:T(1024)S(1)}, f32[1536]{0:T(1024)S(1)}, /*index=5*/f32[1536]{0:T(1024)S(1)}, f32[1536]{0:T(1024)S(1)}, f32[1536]{0:T(1024)S(1)}) fusion(f32[128,1536]{0,1:T(8,128)S(1)} %get-tuple-element.263, bf16[15,1536]{0,1:T(8,128)(2,1)S(1)} %copy-done.2, ...), kind=kLoop, calls=%fused_computation.263 | loop fusion | flops 7852032 | bytes 1274880 | tf_op jit(solution)/shard_map/reduce_sum | solution.py:202
  79.3 3.8 %fusion.73 = (f32[1536]{0:T(1024)S(1)}, f32[1536]{0:T(1024)S(1)}, f32[1536]{0:T(1024)S(1)}, f32[1536]{0:T(1024)S(1)}, f32[1536]{0:T(1024)S(1)}, /*index=5*/f32[1...) fusion(f32[128,1536]{0,1:T(8,128)S(1)} %get-tuple-element.263, ...), kind=kLoop, calls=%fused_computation.256 | loop fusion | flops 10603008 | bytes 1281024 | tf_op jit(solution)/shard_map/reduce_sum | solution.py:202
  83.7 2.5 %fusion.64 = (f32[1536]{0:T(1024)S(1)}, f32[1536]{0:T(1024)S(1)}, f32[1536]{0:T(1024)S(1)}, f32[1536]{0:T(1024)S(1)}, f32[1536]{0:T(1024)S(1)}, /*index=5*/f32[1536]{0:T(1024)S(1)}) fusion(f32[128,1536]{0,1:T(8,128)S(1)} %get-tuple-element.263, bf16[128,1536]{0,1:T(8,128)(2,1)S(1)} %bitcast_select_fusion, bf16[15,1536]{0,1:T(8,128)(2,1)S(1)} %collective-permute-done.1), kind=kLoop, calls=%fused_computation.247 | loop fusion | flops 7068672 | bytes 1262592 | tf_op jit(solution)/shard_map/reduce_sum | solution.py:202
  94.6 6.0 %stack.127 = f32[31,1536]{1,0:T(8,128)} concatenate(f32[1,1536]{1,0:T(1,128)} %stack.96, f32[1,1536]{1,0:T(1,128)} %stack.97, f32[1,1536]{1,0:T(1,128)} %stack.98, f32[1,1536]{1,0:T(1,128)} %stack.99, f32[1,1536]{1,0:T(1,128)} %stack.100, f32[1,1536]{1,0:T(1,128)} %stack.101, f32[1,1536]{1,0:T(1,128)} %stack.102, f32[1,1536]{1,0:T(1,128)} %stack.103, f32[1,1536]{1,0:T(1,128)} %stack.104, ...), dimensions={0} | concatenate | bytes 380928 | tf_op jit(solution)/shard_map/stack | solution.py:200
  100.5 1.7 broadcast_in_dim.88
  104.1 3.7 %collective-permute-start.4 = (f32[15,1536]{1,0:T(8,128)}, f32[15,1536]{1,0:T(8,128)S(1)}, u32[]{:S(2)}, u32[]{:S(2)}) collective-permute-start(f32[15,1536]{1,0:T(8,128)} %copy.98), channel_id=1, source_target_pairs={{0,1},{2,3},{4,5},{6,7},{8,9},{10,11},{12,13},{14,15},{16,17},{18,... | collective-permute-start | bytes 276488 | tf_op jit(solution)/shard_map/ppermute | solution.py:23
  107.8 1.3 collective-permute-start.3
  110.2 24.2 %psum.15 = f32[1,1536]{1,0:T(1,128)} all-reduce(f32[1,1536]{1,0:T(1,128)S(1)} %copy-done.65), channel_id=1, replica_groups=mesh['dp'=4,'pipe'=4,'ctx'=2] {'dp','ctx'}, use_global_device_ids=true, to_apply=%region_38.39 | all-reduce | flops 1536 | bytes 12288 | tf_op jit(solution)/shard_map/psum | solution.py:207
  136.3 13.2 %while.17 = (s32[]{:T(128)}, bf16[4,256,96]{1,2,0:T(8,128)(2,1)}, bf16[4,256,96]{1,2,0:T(8,128)(2,1)}, bf16[4,256,96]{1,2,0:T(8,128)(2,1)}, bf16[4,256,96]{1,2,0...) while((s32[]{:T(128)}, bf16[4,256,96]{1,2,0:T(8,128)(2,1)}, ...), condition=%wide.region_4.5_spmd.clone, body=%wide.region_0.4_spmd.clone.sunk | while | flops 76471808 | bytes 4224949 | solution.py:99
  153.3 3.7 %all-to-all-start.3 = ((bf16[2,128,768]{2,1,0:T(8,128)(2,1)}), bf16[2,128,768]{2,1,0:T(8,128)(2,1)S(1)}, u32[]{:S(2)}, u32[]{:S(2)}) async-start(bf16[2,128,768]{2,1,0:T(8,128)(2,1)} %copy.91), calls=%async_computation.3 | async-start | bytes 786432 | tf_op jit(solution)/shard_map/all_to_all | solution.py:166
  157.2 21.0 %fusion.217 = bf16[1,1,128,1536]{2,3,1,0:T(8,128)(2,1)S(1)} fusion(f32[128,1536]{0,1:T(8,128)S(1)} %get-tuple-element.263, f32[15,1536]{0,1:T(8,128)S(1)} %copy.99, f32[1536]{0:T(1024)} %copy-done.63, f32[1536]{0:T(1024)} %copy-done.64, f32[1536]{0:T(1024)S(1)} %get-tuple-element.213, f32[1536]{0:T(1024)S(1)} %copy-done.13, f32[1536]{0:T(1024)S(1)} %copy-done.15, ...), kind=kLoop, calls=%fused_computation.411 | loop fusion | flops 18284544 | bytes 1554560 | tf_op jit(solution)/shard_map/broadcast_in_dim | solution.py:213
  180.9 3.5 %all-to-all-start.4 = ((bf16[2,128,768]{2,1,0:T(8,128)(2,1)}), bf16[2,128,768]{2,1,0:T(8,128)(2,1)S(1)}, u32[]{:S(2)}, u32[]{:S(2)}) async-start(bf16[2,128,768]{2,1,0:T(8,128)(2,1)} %copy.94), calls=%async_computation.4 | async-start | bytes 786432 | tf_op jit(solution)/shard_map/all_to_all | solution.py:167
  185.4 4.8 %all-to-all-done.4 = bf16[2,128,768]{2,1,0:T(8,128)(2,1)S(1)} async-done(((bf16[2,128,768]{2,1,0:T(8,128)(2,1)}), bf16[2,128,768]{2,1,0:T(8,128)(2,1)S(1)}, u32[]{:S(2)}, u32[]{:S(2)}) %all-to-all-start.4) | async-done | bytes 393248 | tf_op jit(solution)/shard_map/all_to_all | solution.py:167
  191.6 1.6 copy.131
  (277 shorter events, 53.8 us)
Async XLA Ops:
  9.3 15.3 %all-to-all-start = ((bf16[2,128,384]{1,2,0:T(8,128)(2,1)}), bf16[2,128,384]{1,2,0:T(8,128)(2,1)S(1)}, u32[]{:S(2)}, u32[]{:S(2)}) async-start(bf16[2,128,384]{1,2,0:T(8,128)(2,1)} %bitcast.3), calls=%async_computation | async-start | bytes 393216 | tf_op jit(solution)/shard_map/all_to_all | solution.py:153
  14.7 25.1 %collective-permute-start = (bf16[1,1,128,2304]{2,3,1,0:T(8,128)(2,1)}, bf16[1,1,128,2304]{2,3,1,0:T(8,128)(2,1)}, u32[]{:S(2)}, u32[]{:S(2)}) collective-permute-start(bf16[1,1,128,2304]{2,3,1,0:T(8,128)(2,1)} %copy.85), channel_id=1, source_target_pairs={{0,6},{2,0},{4,2},{6,4},{1,7},{3,1},{5,3},{7,5},{8,14},{10,8},{12,... | collective-permute-start | bytes 1769480 | tf_op jit(solution)/shard_map/ppermute | solution.py:15
  18.7 27.2 %collective-permute-start.1 = (bf16[15,1536]{0,1:T(8,128)(2,1)}, bf16[15,1536]{0,1:T(8,128)(2,1)S(1)}, u32[]{:S(2)}, u32[]{:S(2)}) collective-permute-start(bf16[15,1536]{0,1:T(8,128)(2,1)} %get-tuple-element.278), channel_id=1, source_target_pairs={{0,1},{2,3},{4,5},{6,7},{8,9},{10,11},{12,13},{14,15},{16,17},{18,... | collective-permute-start | bytes 138248 | tf_op jit(solution)/shard_map/ppermute | solution.py:23
  22.4 23.5 %collective-permute-start.2 = (bf16[15,1536]{0,1:T(8,128)(2,1)S(1)}, bf16[15,1536]{0,1:T(8,128)(2,1)S(1)}, u32[]{:S(2)}, u32[]{:S(2)}) collective-permute-start(bf16[15,1536]{0,1:T(8,128)(2,1)S(1)} %get-tuple-element.279), channel_id=1, source_target_pairs={{1,0},{3,2},{5,4},{7,6},{9,8},{11,10},{13,12},{15,14},{17,16},{19,... | collective-permute-start | bytes 138248 | tf_op jit(solution)/shard_map/ppermute | solution.py:26
  24.5 14.1 %all-to-all-start.1 = ((bf16[2,128,768]{1,2,0:T(8,128)(2,1)}), bf16[2,128,768]{1,2,0:T(8,128)(2,1)S(1)}, u32[]{:S(2)}, u32[]{:S(2)}) async-start(bf16[2,128,768]{1,2,0:T(8,128)(2,1)} %maximum_bitcast_fusion.1), calls=%async_computation.1 | async-start | bytes 786432 | tf_op jit(solution)/shard_map/all_to_all | solution.py:155
  28.6 17.3 %copy-start.46 = (f32[1536]{0:T(1024)}, f32[1536]{0:T(1024)S(1)}, u32[]{:S(2)}) copy-start(f32[1536]{0:T(1024)S(1)} %get-tuple-element.231) | copy-start | bytes 18436
  28.7 17.3 %copy-start.48 = (f32[1536]{0:T(1024)}, f32[1536]{0:T(1024)S(1)}, u32[]{:S(2)}) copy-start(f32[1536]{0:T(1024)S(1)} %get-tuple-element.232) | copy-start | bytes 18436
  28.7 17.3 %copy-start.50 = (f32[1536]{0:T(1024)}, f32[1536]{0:T(1024)S(1)}, u32[]{:S(2)}) copy-start(f32[1536]{0:T(1024)S(1)} %get-tuple-element.233) | copy-start | bytes 18436
  28.7 17.3 %copy-start.52 = (f32[1536]{0:T(1024)}, f32[1536]{0:T(1024)S(1)}, u32[]{:S(2)}) copy-start(f32[1536]{0:T(1024)S(1)} %get-tuple-element.234) | copy-start | bytes 18436
  28.7 17.3 %copy-start.54 = (f32[1536]{0:T(1024)}, f32[1536]{0:T(1024)S(1)}, u32[]{:S(2)}) copy-start(f32[1536]{0:T(1024)S(1)} %get-tuple-element.235) | copy-start | bytes 18436
  28.7 17.3 %copy-start.56 = (f32[1536]{0:T(1024)}, f32[1536]{0:T(1024)S(1)}, u32[]{:S(2)}) copy-start(f32[1536]{0:T(1024)S(1)} %get-tuple-element.236) | copy-start | bytes 18436
  28.7 17.3 %copy-start.58 = (f32[1536]{0:T(1024)}, f32[1536]{0:T(1024)S(1)}, u32[]{:S(2)}) copy-start(f32[1536]{0:T(1024)S(1)} %get-tuple-element.237) | copy-start | bytes 18436
  28.7 17.3 %copy-start.60 = (f32[1536]{0:T(1024)}, f32[1536]{0:T(1024)S(1)}, u32[]{:S(2)}) copy-start(f32[1536]{0:T(1024)S(1)} %get-tuple-element.238) | copy-start | bytes 18436
  28.7 17.3 %copy-start.61 = (f32[1536]{0:T(1024)}, f32[1536]{0:T(1024)S(1)}, u32[]{:S(2)}) copy-start(f32[1536]{0:T(1024)S(1)} %get-tuple-element.239) | copy-start | bytes 18436
  28.7 17.3 %copy-start.62 = (f32[1536]{0:T(1024)}, f32[1536]{0:T(1024)S(1)}, u32[]{:S(2)}) copy-start(f32[1536]{0:T(1024)S(1)} %get-tuple-element.240) | copy-start | bytes 18436
  28.7 17.3 %copy-start.63 = (f32[1536]{0:T(1024)}, f32[1536]{0:T(1024)S(1)}, u32[]{:S(2)}) copy-start(f32[1536]{0:T(1024)S(1)} %get-tuple-element.241) | copy-start | bytes 18436
  28.8 17.3 %copy-start.64 = (f32[1536]{0:T(1024)}, f32[1536]{0:T(1024)S(1)}, u32[]{:S(2)}) copy-start(f32[1536]{0:T(1024)S(1)} %get-tuple-element.242) | copy-start | bytes 18436
  41.6 93.5 %all-to-all-start.2 = ((bf16[2,128,384]{2,1,0:T(8,128)(2,1)}), bf16[2,128,384]{2,1,0:T(8,128)(2,1)}, u32[]{:S(2)}, u32[]{:S(2)}) async-start(bf16[2,128,384]{2,1,0:T(8,128)(2,1)} %copy.86), calls=%async_computation.2 | async-start | bytes 393216 | tf_op jit(solution)/shard_map/all_to_all | solution.py:154
  45.7 145.9 %all-reduce.2.cloned.1.call-start = ((), (), s32[]{:S(2)}) async-start(), calls=%async_computation.5 | async-start | bytes 380928 | tf_op jit(solution)/shard_map/psum | solution.py:207
  45.9 19.1 %copy-start.1 = (bf16[15,1536]{0,1:T(8,128)(2,1)}, bf16[15,1536]{0,1:T(8,128)(2,1)S(1)}, u32[]{:S(2)}) copy-start(bf16[15,1536]{0,1:T(8,128)(2,1)S(1)} %collective-permute-done.2) | copy-start | bytes 138244
  104.1 30.7 %collective-permute-start.4 = (f32[15,1536]{1,0:T(8,128)}, f32[15,1536]{1,0:T(8,128)S(1)}, u32[]{:S(2)}, u32[]{:S(2)}) collective-permute-start(f32[15,1536]{1,0:T(8,128)} %copy.98), channel_id=1, source_target_pairs={{0,1},{2,3},{4,5},{6,7},{8,9},{10,11},{12,13},{14,15},{16,17},{18,... | collective-permute-start | bytes 276488 | tf_op jit(solution)/shard_map/ppermute | solution.py:23
  107.8 26.7 %collective-permute-start.3 = (f32[15,1536]{1,0:T(8,128)S(1)}, f32[15,1536]{1,0:T(8,128)S(1)}, u32[]{:S(2)}, u32[]{:S(2)}) collective-permute-start(f32[15,1536]{1,0:T(8,128)S(1)} %copy-done.11), channel_id=1, source_target_pairs={{1,0},{3,2},{5,4},{7,6},{9,8},{11,10},{13,12},{15,14},{17,16},{19,... | collective-permute-start | bytes 276488 | tf_op jit(solution)/shard_map/ppermute | solution.py:26
  153.3 27.6 %all-to-all-start.3 = ((bf16[2,128,768]{2,1,0:T(8,128)(2,1)}), bf16[2,128,768]{2,1,0:T(8,128)(2,1)S(1)}, u32[]{:S(2)}, u32[]{:S(2)}) async-start(bf16[2,128,768]{2,1,0:T(8,128)(2,1)} %copy.91), calls=%async_computation.3 | async-start | bytes 786432 | tf_op jit(solution)/shard_map/all_to_all | solution.py:166
  180.9 9.3 %all-to-all-start.4 = ((bf16[2,128,768]{2,1,0:T(8,128)(2,1)}), bf16[2,128,768]{2,1,0:T(8,128)(2,1)S(1)}, u32[]{:S(2)}, u32[]{:S(2)}) async-start(bf16[2,128,768]{2,1,0:T(8,128)(2,1)} %copy.94), calls=%async_computation.4 | async-start | bytes 786432 | tf_op jit(solution)/shard_map/all_to_all | solution.py:167
  (61 other events, 467.5 us)
Sparse Core Ops, SparseCore 0:
  102.4 72.1 all-reduce.1
where the time goes:
time: 201 us; the launch traced here: 200 us
  other arithmetic  54.4 us (27%)
  local copies, waits for them, and re-layouts  50.4 us (25%)
  starting transfers between devices  31.2 us (16%)
  blocking collectives  24.2 us (12%)
  between operations  16 us (8%)
  waiting for transfers between devices  13.8 us (7%)
  matrix products  9.53 us (5%)
    reduce_sum x4, other arithmetic, local(): jnp.sum(padded[offset:offset + rows_here].astype(jnp.float32) * grad_pre,...  28.1 us
    another operation x32, local copies, waits for them, and re-layouts, local(): jnp.stack([jnp.sum(padded[offset:offset + rows_here].astype(jnp.float32)...  24.4 us
    psum x1, blocking collectives, local(): kernel_grad, bias_grad = lax.psum((kernel_local, bias_local), ('dp', 'ctx'))  24.2 us
    broadcast_in_dim x1, other arithmetic, local(): gated_grad[None, None]  21 us
    all_to_all x1, waiting for transfers between devices, local(): lax.all_to_all(key_value, 'ctx', split_axis=0, concat_axis=1, tiled=True)  8.99 us
    unnamed x140, local copies, waits for them, and re-layouts  8.85 us
    ppermute x2, starting transfers between devices, padded_2(): lax.ppermute(lax.slice_in_dim(block, block.shape[dim] - width, None, axis...  7.3 us
    all_to_all x1, waiting for transfers between devices, local(): lax.all_to_all(key_grads.reshape(devices_ctx, rows_here, 2 * block_width)...  4.77 us
  transfers between devices with their start and end apart: 11, of which 2 were waited for; matrix products, arithmetic and copies ran while one was open for 55% of the time, Pallas kernels for 0%

commit v1 on v0

v1 whole, which is shorter than its diff:
```python
import math

import jax
import jax.numpy as jnp
from jax import lax
from jax.experimental import pallas as pl
from jax.experimental.pallas import tpu as pltpu
from jax.sharding import PartitionSpec as P

HEADS = 8
HD = 96
KSIZE = 31
HALF = KSIZE // 2
LANES = 128
EDGE = 32
SLIM = 16
GROUP = 4
F32 = jnp.float32
BF16 = jnp.bfloat16


def conv_kernel(
    place_ref, gated_ref, gated_low, gated_high, cot_ref, cot_low, cot_high, taps_ref, bias_ref,
    out_ref, grad_ref, sums_ref, source, slopes, partial,
):
    rows, width = gated_ref.shape
    first, length, frames = place_ref[0], place_ref[1], place_ref[2]

    def frame_of(start, count):
        return first + start + lax.broadcasted_iota(jnp.int32, (count, LANES), 0)

    for column in range(width // LANES):
        lanes = pl.ds(column * LANES, LANES)

        def fill(value, start):
            count = value.shape[0]
            frame = frame_of(start, count)
            keep = (frame >= 0) & (frame < length)
            source[pl.ds(start + EDGE, count), :] = jnp.where(keep, value.astype(F32), 0.0)

        def fill_cot(value, start):
            count = value.shape[0]
            frame = frame_of(start, count)
            keep = (frame >= 0) & (frame < frames)
            slopes[pl.ds(start + SLIM, count), :] = jnp.where(keep, value.astype(F32), 0.0)

        fill(gated_low[:, lanes], -EDGE)
        fill(gated_high[:, lanes], rows)
        fill_cot(cot_low[:, lanes], -SLIM)
        fill_cot(cot_high[:, lanes], rows)

        @pl.loop(0, rows // EDGE)
        def _(step):
            at = pl.multiple_of(step * EDGE, EDGE)
            fill(gated_ref[pl.ds(at, EDGE), lanes], at)
            slopes[pl.ds(at + SLIM, EDGE), :] = cot_ref[pl.ds(at, EDGE), lanes].astype(F32)

        taps = [
            jnp.broadcast_to(taps_ref[k : k + 1, lanes], (8, LANES)) for k in range(KSIZE)
        ]
        bias = jnp.broadcast_to(bias_ref[:, lanes], (8, LANES))

        def weighted(read, order, base):
            parts = [base, None, None, None]
            for k in range(KSIZE):
                term = taps[k] * read(order(k))
                slot = k % 4
                parts[slot] = term if parts[slot] is None else parts[slot] + term
            return (parts[0] + parts[1]) + (parts[2] + parts[3])

        def pre_tile(at):
            pre = weighted(lambda k: source[pl.ds(at + 1 + k, 8), :], lambda k: k, bias)
            gate = jax.nn.sigmoid(pre)
            swish = pre * gate
            where = pl.ds(at, 8)
            slopes[where, :] = slopes[where, :] * (gate + swish * (1.0 - gate))
            return swish

        for at in range(0, SLIM, 8):
            pre_tile(at)
            pre_tile(rows + SLIM + at)

        @pl.loop(0, rows // 16)
        def _(step):
            at = pl.multiple_of(step * 16, 16)
            swish = [pre_tile(SLIM + at), pre_tile(SLIM + at + 8)]
            out_ref[pl.ds(at, 16), lanes] = jnp.concatenate(swish, axis=0).astype(BF16)

        zero = jnp.zeros((8, LANES), F32)

        def gather(step, totals):
            at = pl.multiple_of(step * 8, 8)
            grad = slopes[pl.ds(at + SLIM, 8), :]
            sums = [
                totals[k] + grad * source[pl.ds(at + SLIM + 1 + k, 8), :] for k in range(KSIZE)
            ]
            return (*sums, totals[KSIZE] + grad)

        totals = lax.fori_loop(0, rows // 8, gather, (zero,) * (KSIZE + 1))
        for k in range(KSIZE + 1):
            partial[8 * k : 8 * k + 8, :] = totals[k]
        summed = partial[pl.ds(0, KSIZE + 1, stride=8), :]
        for sublane in range(1, 8):
            summed = summed + partial[pl.ds(sublane, KSIZE + 1, stride=8), :]
        sums_ref[:, lanes] = summed.astype(sums_ref.dtype)

        @pl.loop(0, rows // 16)
        def _(step):
            at = pl.multiple_of(step * 16, 16)
            back = [
                weighted(
                    lambda k: slopes[pl.ds(at + shift + SLIM + HALF - k, 8), :],
                    lambda k: k,
                    zero,
                )
                for shift in (0, 8)
            ]
            keep = frame_of(at, 16) < length
            whole = jnp.where(keep, jnp.concatenate(back, axis=0), 0.0)
            grad_ref[pl.ds(at, 16), lanes] = whole.astype(BF16)


def conv_call(place, gated, gated_low, gated_high, arriving, cot_low, cot_high, taps, bias):
    rows, channels = gated.shape
    width = 2 * LANES
    offset = (arriving.shape[1] - channels) // width

    def columns(count, shift=0):
        return pl.BlockSpec((count, width), lambda i: (0, i + shift))

    work = 3 * 2 * KSIZE * rows * channels
    return pl.pallas_call(
        conv_kernel,
        grid=(channels // width,),
        in_specs=[
            pl.BlockSpec(memory_space=pltpu.SMEM),
            columns(rows),
            columns(EDGE),
            columns(EDGE),
            columns(rows, offset),
            columns(SLIM),
            columns(SLIM),
            columns(KSIZE),
            columns(1),
        ],
        out_specs=[columns(rows), columns(rows), columns(KSIZE + 1)],
        out_shape=[
            jax.ShapeDtypeStruct((rows, channels), BF16),
            jax.ShapeDtypeStruct((rows, channels), BF16),
            jax.ShapeDtypeStruct((KSIZE + 1, channels), BF16),
        ],
        scratch_shapes=[
            pltpu.VMEM((rows + 2 * EDGE, LANES), F32),
            pltpu.VMEM((rows + 2 * SLIM, LANES), F32),
            pltpu.VMEM((8 * (KSIZE + 1), LANES), F32),
        ],
        cost_estimate=pl.CostEstimate(
            flops=work, bytes_accessed=10 * rows * channels, transcendentals=rows * channels
        ),
        name="conv",
    )(place, gated, gated_low, gated_high, arriving, cot_low, cot_high, taps, bias)


def attention_kernel(
    place_ref, mine_ref, peer_ref, cot_ref, cot_peer_ref, out_ref, grad_ref
):
    rows = mine_ref.shape[0]
    embed = HEADS * HD
    scale = 1.0 / math.sqrt(HD)
    first, first_peer, length = place_ref[0], place_ref[1], place_ref[2]
    row = lax.broadcasted_iota(jnp.int32, (2 * rows, 2 * rows), 0)
    frame = jnp.where(row < rows, row + first, row - rows + first_peer)
    valid = frame < length
    across = (((1,), (1,)), ((), ()))
    downward = (((0,), (0,)), ((), ()))

    def both(a_ref, b_ref, start, width):
        return jnp.concatenate(
            [a_ref[:, start : start + width], b_ref[:, start : start + width]], axis=0
        )

    for group in range(HEADS // GROUP):
        tiles = GROUP * HD // LANES
        totals = [[None] * tiles for _ in range(4)]
        for head in range(GROUP):
            low = head * HD
            tile = low // LANES
            count = (low + HD - 1) // LANES - tile + 1
            width = count * LANES
            start = group * GROUP * HD + tile * LANES
            lane = lax.broadcasted_iota(jnp.int32, (2 * rows, width), 1) + tile * LANES
            here = (lane >= low) & (lane < low + HD)

            def own(value):
                return jnp.where(here, value, jnp.zeros((), BF16))

            query = both(mine_ref, peer_ref, start, width)
            key = own(both(mine_ref, peer_ref, embed + start, width))
            value = own(both(mine_ref, peer_ref, 2 * embed + start, width))
            cot = both(cot_ref, cot_peer_ref, start, width)
            scores = lax.dot_general(key, query, across, preferred_element_type=F32) * scale
            scores = jnp.where(valid, scores, -1e30)
            top = jnp.max(scores, axis=0, keepdims=True)
            raised = jnp.exp(scores - top)
            total = jnp.sum(raised, axis=0, keepdims=True)
            probs_bf = (raised * (1.0 / total)).astype(BF16)
            probs = probs_bf.astype(F32)
            grad_probs = lax.dot_general(value, cot, across, preferred_element_type=F32)
            centre = jnp.sum(probs * grad_probs, axis=0, keepdims=True)
            grad_scores = (probs * (grad_probs - centre) * scale).astype(BF16)
            results = (
                lax.dot_general(probs_bf[:, :rows], value, downward, preferred_element_type=F32),
                lax.dot_general(grad_scores[:, :rows], key, downward, preferred_element_type=F32),
                jnp.dot(grad_scores[:rows], own(query), preferred_element_type=F32),
                jnp.dot(probs_bf[:rows], own(cot), preferred_element_type=F32),
            )
            for result, kept in zip(results, totals):
                for index in range(count):
                    piece = result[:, index * LANES : (index + 1) * LANES]
                    held = kept[tile + index]
                    kept[tile + index] = piece if held is None else held + piece
        for index in range(tiles):
            start = group * GROUP * HD + index * LANES
            out_ref[:, start : start + LANES] = totals[0][index].astype(BF16)
            for block in range(3):
                at = block * embed + start
                grad_ref[:, at : at + LANES] = totals[block + 1][index].astype(BF16)


def attention_call(place, mine, peer, arriving, cot_peer):
    rows, columns = mine.shape
    embed = HEADS * HD
    whole = pl.BlockSpec((rows, columns), lambda i: (0, 0))
    third = pl.BlockSpec((rows, embed), lambda i: (0, 0))
    return pl.pallas_call(
        attention_kernel,
        grid=(1,),
        in_specs=[pl.BlockSpec(memory_space=pltpu.SMEM), whole, whole, third, third],
        out_specs=[third, whole],
        out_shape=[
            jax.ShapeDtypeStruct((rows, embed), BF16),
            jax.ShapeDtypeStruct((rows, columns), BF16),
        ],
        cost_estimate=pl.CostEstimate(
            flops=6 * 2 * HEADS * 4 * rows * rows * HD,
            bytes_accessed=2 * rows * (3 * columns + 3 * embed),
            transcendentals=HEADS * 4 * rows * rows,
        ),
        compiler_params=pltpu.CompilerParams(vmem_limit_bytes=40 * 1024 * 1024),
        name="attention",
    )(place, mine, peer, arriving, cot_peer)


def head_pass(queries, grad_out, keys_in, values_in, valid_keys):
    query_rows, head_dim = queries.shape
    score_scale = 1.0 / math.sqrt(head_dim)
    block_rows = min(512, query_rows)
    block_count = query_rows // block_rows
    frame_count = keys_in.shape[0]
    across = (((1,), (1,)), ((), ()))
    downward = (((0,), (0,)), ((), ()))

    def advance(totals, blocks):
        query_block, grad_block = blocks
        scores = (
            lax.dot_general(query_block, keys_in, across, preferred_element_type=jnp.float32)
            * score_scale
        )
        scores = jnp.where(valid_keys[None, :], scores, -1e30)
        row_top = jnp.max(scores, axis=1, keepdims=True)
        row_total = jnp.sum(jnp.exp(scores - row_top), axis=1, keepdims=True)
        probs_bf = (jnp.exp(scores - row_top) / row_total).astype(jnp.bfloat16)
        attended_full = jnp.dot(probs_bf, values_in, preferred_element_type=jnp.float32)
        attended = attended_full.astype(jnp.bfloat16)
        grad_probs = lax.dot_general(
            grad_block, values_in, across, preferred_element_type=jnp.float32
        )
        centre = jnp.sum(grad_block.astype(jnp.float32) * attended_full, axis=1, keepdims=True)
        grad_scores = (probs_bf.astype(jnp.float32) * (grad_probs - centre) * score_scale).astype(
            jnp.bfloat16
        )
        grad_query = jnp.dot(grad_scores, keys_in, preferred_element_type=jnp.float32).astype(
            jnp.bfloat16
        )
        key_total = totals[0] + lax.dot_general(
            grad_scores, query_block, downward, preferred_element_type=jnp.float32
        )
        value_total = totals[1] + lax.dot_general(
            probs_bf, grad_block, downward, preferred_element_type=jnp.float32
        )
        return ((key_total, value_total), (attended, grad_query))

    zero_grads = jnp.zeros((frame_count, head_dim), jnp.float32)
    blocked = (
        queries.reshape(block_count, block_rows, head_dim),
        grad_out.reshape(block_count, block_rows, head_dim),
    )
    totals, results = lax.scan(advance, (zero_grads, zero_grads), blocked)
    attended = results[0].reshape(query_rows, head_dim)
    grad_query = results[1].reshape(query_rows, head_dim)
    return (attended, grad_query, totals[0], totals[1])


def attend_block(query_part, grad_part, key_value, valid_keys, heads_dev):
    block_width = heads_dev * HD

    def split_heads(matrix):
        return matrix.reshape(matrix.shape[0], heads_dev, HD).transpose(1, 0, 2)

    def join_heads(matrix):
        return matrix.transpose(1, 0, 2).reshape(matrix.shape[1], block_width)

    def one_head(items):
        return head_pass(items[0], items[1], items[2], items[3], valid_keys)

    stacked = (
        split_heads(query_part),
        split_heads(grad_part),
        split_heads(key_value[:, :block_width]),
        split_heads(key_value[:, block_width:]),
    )
    attended, grad_query, key_grad, value_grad = lax.map(one_head, stacked)
    key_grads = jnp.concatenate([join_heads(key_grad), join_heads(value_grad)], axis=1)
    return (join_heads(attended), join_heads(grad_query), key_grads)


def attend_by_heads(mixed, grad_attn, valid_keys):
    rows_here = mixed.shape[0]
    devices_ctx = lax.axis_size("ctx")
    embed = HEADS * HD
    part_count = max(devices_ctx // HEADS, 1)
    heads_dev = max(HEADS // devices_ctx, 1)
    block_heads = HEADS // heads_dev
    part_rows = rows_here // part_count
    block_width = heads_dev * HD
    queries = mixed[:, :embed]
    keys_in = mixed[:, embed : 2 * embed]
    values_in = mixed[:, 2 * embed :]

    def by_part(matrix):
        split = matrix.reshape(part_count, part_rows, block_heads, block_width).transpose(
            2, 0, 1, 3
        )
        return split.reshape(devices_ctx, part_rows, block_width)

    def swap(value, concat):
        return lax.all_to_all(value, "ctx", split_axis=0, concat_axis=concat, tiled=True)

    key_value = jnp.concatenate(
        [
            keys_in.reshape(rows_here, block_heads, block_width),
            values_in.reshape(rows_here, block_heads, block_width),
        ],
        axis=2,
    )
    key_value = jnp.repeat(key_value.transpose(1, 0, 2), part_count, axis=0)
    query_part = swap(by_part(queries), 1)[0]
    grad_part = swap(by_part(grad_attn), 1)[0]
    key_value = swap(key_value, 1)[0]
    attended, grad_query, key_grads = attend_block(
        query_part, grad_part, key_value, valid_keys, heads_dev
    )
    outgoing = jnp.concatenate([attended, grad_query], axis=1).reshape(
        devices_ctx, part_rows, 2 * block_width
    )
    returned = swap(outgoing, 0)
    key_returned = swap(
        key_grads.reshape(devices_ctx, rows_here, 2 * block_width).astype(BF16), 0
    ).astype(F32)
    columns = 2 * block_width
    split = returned.reshape(block_heads, part_count, part_rows, columns).transpose(1, 2, 0, 3)
    returned = split.reshape(rows_here, block_heads, columns)
    attention_out = returned[:, :, :block_width].reshape(rows_here, embed)
    grad_q = returned[:, :, block_width:].reshape(rows_here, embed)
    summed = jnp.sum(
        key_returned.reshape(block_heads, part_count, rows_here, 2 * block_width), axis=1
    )
    summed = summed.astype(BF16).transpose(1, 0, 2)
    grad_k = summed[:, :, :block_width].reshape(rows_here, embed)
    grad_v = summed[:, :, block_width:].reshape(rows_here, embed)
    return attention_out, jnp.concatenate([grad_q, grad_k, grad_v], axis=1)


def summed_over(value, axes):
    for axis in axes:
        count = lax.axis_size(axis)
        step = 1
        while step < count:
            other = lax.ppermute(value, axis, [(i, i ^ step) for i in range(count)])
            total = value.astype(F32) + other.astype(F32)
            value = total.astype(BF16)
            step *= 2
    return total


def edges(block, count, pipe_shift):
    rows = block.shape[0]
    sections, devices = lax.axis_size("pipe"), lax.axis_size("ctx")
    me = lax.axis_index("ctx")

    def route(ctx_pairs):
        return [
            (s * devices + a, ((s - pipe_shift) % sections) * devices + b)
            for s in range(sections)
            for a, b in ctx_pairs
        ]

    if devices == 2:
        start = jnp.where(me == 0, rows - count, 0)
        piece = lax.dynamic_slice_in_dim(block, start, count, axis=0)
        got = lax.ppermute(piece, ("pipe", "ctx"), route([(0, 1), (1, 0)]))
        return got, got
    upward = [(i, i + 1) for i in range(devices - 1)]
    low = lax.ppermute(block[rows - count :], ("pipe", "ctx"), route(upward))
    high = lax.ppermute(block[:count], ("pipe", "ctx"), route([(b, a) for a, b in upward]))
    return low, high


def local(projected, gated_input, upstream, lengths, depth_kernel, depth_bias):
    embed = HEADS * HD
    sections, devices = lax.axis_size("pipe"), lax.axis_size("ctx")
    me = lax.axis_index("ctx")
    mixed, gated, sent = projected[0, 0], gated_input[0, 0], upstream[0, 0]
    rows = mixed.shape[0]
    frames = rows * devices
    length = lengths[0, 0]
    first = me * rows
    gated_low, gated_high = edges(gated, EDGE, 0)
    cot_low, cot_high = edges(sent[:, embed:], SLIM, 1)
    arriving = lax.ppermute(sent, "pipe", [(i, (i - 1) % sections) for i in range(sections)])
    if devices == 2:
        crossed = [
            (s * 2 + c, ((s - 1) % sections) * 2 + 1 - c)
            for s in range(sections)
            for c in range(2)
        ]
        cot_peer = lax.ppermute(sent[:, :embed], ("pipe", "ctx"), crossed)
        peer = lax.ppermute(mixed, "ctx", [(0, 1), (1, 0)])
    place = jnp.stack([first, length, jnp.int32(frames)])
    depth_out, gated_grad, sums = conv_call(
        place,
        gated,
        gated_low,
        gated_high,
        arriving,
        cot_low,
        cot_high,
        depth_kernel[0],
        depth_bias,
    )
    sums = summed_over(sums, ("dp", "ctx"))
    if devices == 2:
        place = jnp.stack([first, (1 - me) * rows, length])
        attention_out, projected_grad = attention_call(place, mixed, peer, arriving, cot_peer)
    else:
        attention_out, projected_grad = attend_by_heads(
            mixed, arriving[:, :embed], jnp.arange(frames) < length
        )
    return (
        attention_out[None, None],
        depth_out[None, None],
        projected_grad[None, None],
        gated_grad[None, None],
        sums[None, :KSIZE],
        sums[KSIZE:],
    )


def solution(mesh):
    by_frame = P("pipe", "dp", "ctx", None)
    return jax.shard_map(
        local,
        mesh=mesh,
        in_specs=(
            by_frame,
            by_frame,
            by_frame,
            P("pipe", "dp"),
            P("pipe", None, None),
            P("pipe", None),
        ),
        out_specs=(
            by_frame,
            by_frame,
            by_frame,
            by_frame,
            P("pipe", None, None),
            P("pipe", None),
        ),
        check_vma=False,
    )
```

time: 201 us -> 62.1 us (0.31)
  other arithmetic: 54.4 us -> 1.71 us
  local copies, waits for them, and re-layouts: 50.4 us -> 5.95 us
  blocking collectives: 24.2 us -> 0 us
  Pallas kernels: 0 us -> 18.7 us
  starting transfers between devices: 31.2 us -> 12.6 us
  between operations: 16 us -> 1.36 us
  matrix products: 9.53 us -> 0 us
  waiting for transfers between devices: 13.8 us -> 21.6 us
    reduce_sum x12 -> x0, other arithmetic: 28.5 us -> none  [the longest x4 28.1 us: local(): jnp.sum(padded[offset:offset + rows_here].astype(jnp.float32) * grad_pre,...]
    another operation x34 -> x0, local copies, waits for them, and re-layouts: 24.7 us -> none  [the longest x32 24.4 us: local(): jnp.stack([jnp.sum(padded[offset:offset + rows_here].astype(jnp.float32)...]
    psum x1 -> x0, blocking collectives: 24.2 us -> none  [local(): kernel_grad, bias_grad = lax.psum((kernel_local, bias_local), ('dp', 'ctx'))]
    ppermute x5 -> x8, waiting for transfers between devices: 0.01 us -> 21.6 us  [the longest x1 13.5 us: local(): cot_peer = lax.ppermute(sent[:, :embed], ('pipe', 'ctx'), crossed)]
    broadcast_in_dim x3 -> x0, other arithmetic: 21.3 us -> none  [the longest x1 21 us: local(): gated_grad[None, None]]
    all_to_all x5 -> x0, starting transfers between devices: 19.5 us -> none  [the longest x1 4.37 us: local(): lax.all_to_all(by_part(queries), 'ctx', split_axis=0, concat_axis=1, tile...]
    pallas_call x0 -> x2, Pallas kernels: none -> 18.7 us  [the longest x1 14.3 us: conv_call(): pl.pallas_call(conv_kernel, grid=(channels // width,), in_specs=[pl.Block...]
    all_to_all x5 -> x0, waiting for transfers between devices: 13.8 us -> none  [the longest x1 8.99 us: local(): lax.all_to_all(key_value, 'ctx', split_axis=0, concat_axis=1, tiled=True)]
  transfers between devices with their start and end apart: 11 -> 8, of which waited for: 2 -> 4; matrix products, arithmetic and copies ran while one was open for 55% -> 7% of each run, Pallas kernels for 0% -> 7%
where the time goes in v1:
time: 62.1 us; the launch traced here: 61.9 us
  waiting for transfers between devices  21.6 us (35%)
  Pallas kernels  18.7 us (30%)
  starting transfers between devices  12.6 us (20%)
  local copies, waits for them, and re-layouts  5.95 us (10%)
  other arithmetic  1.71 us (3%)
  between operations  1.36 us (2%)
    pallas_call x1, Pallas kernels, conv_call(): pl.pallas_call(conv_kernel, grid=(channels // width,), in_specs=[pl.Block...  14.3 us
    ppermute x1, waiting for transfers between devices, local(): cot_peer = lax.ppermute(sent[:, :embed], ('pipe', 'ctx'), crossed)  13.5 us
    ppermute x3, waiting for transfers between devices, summed_over(): other = lax.ppermute(value, axis, [(i, i ^ step) for i in range(count)])  5.88 us
    ppermute x3, starting transfers between devices, summed_over(): other = lax.ppermute(value, axis, [(i, i ^ step) for i in range(count)])  5.81 us
    pallas_call x1, Pallas kernels, attention_call(): pl.pallas_call(attention_kernel, grid=(1,), in_specs=[pl.BlockSpec(memory...  4.38 us
    ppermute x1, starting transfers between devices, local(): lax.ppermute(sent, 'pipe', [(i, (i - 1) % sections) for i in range(sectio...  2.43 us
    unnamed x14, local copies, waits for them, and re-layouts  2.42 us
    ppermute x2, waiting for transfers between devices, edges(): got = lax.ppermute(piece, ('pipe', 'ctx'), route([(0, 1), (1, 0)]))  2.22 us
  transfers between devices with their start and end apart: 8, of which 4 were waited for; matrix products, arithmetic and copies ran while one was open for 7% of the time, Pallas kernels for 7%

profile of v1, /device:TPU:0, one launch (start us, length us, event | category | flops | bytes accessed | tf_op | source)
XLA Modules:
  0.0 61.9 jit_solution(15301759632467825277)
XLA Ops:
  0.6 2.4 %collective-permute-start.1 = (bf16[128,2304]{1,0:T(8,128)(2,1)}, bf16[128,2304]{1,0:T(8,128)(2,1)S(1)}, u32[]{:S(2)}, u32[]{:S(2)}) collective-permute-start(bf16[128,2304]{1,0:T(8,128)(2,1)} %bitcast.23), channel_id=1, source_target_pairs={{0,6},{2,0},{4,2},{6,4},{1,7},{3,1},{5,3},{7,5},{8,14},{10,8},{12,... | collective-permute-start | bytes 1769480 | tf_op jit(solution)/shard_map/ppermute | solution.py:430
  3.1 0.9 %dynamic-slice_bitcast_fusion = bf16[32,1536]{1,0:T(8,128)(2,1)S(1)} fusion(bf16[1,1,128,1536]{3,2,1,0:T(8,128)(2,1)} %param.7, s32[]{:T(128)S(6)} %select_n.9), kind=kLoop, calls=%fused_computation.5 | loop fusion | bytes 196612 | tf_op jit(solution)/shard_map/dynamic_slice | solution.py:410
  4.0 1.5 %collective-permute-start.3 = (bf16[32,1536]{1,0:T(8,128)(2,1)S(1)}, bf16[32,1536]{1,0:T(8,128)(2,1)S(1)}, u32[]{:S(2)}, u32[]{:S(2)}) collective-permute-start(bf16[32,1536]{1,0:T(8,128)(2,1)S(1)} %dynamic-slice_bitcast_fusion), channel_id=1, source_target_pairs={{0,1},{1,0},{2,3},{3,2},{4,5},{5,4},{6,7},{7,6},{8,9},{9,8},{10,11... | collective-permute-start | bytes 294920 | tf_op jit(solution)/shard_map/ppermute | solution.py:411
  5.5 1.1 %slice.17 = bf16[128,1536]{1,0:T(8,128)(2,1)S(1)} slice(bf16[128,2304]{1,0:T(8,128)(2,1)} %bitcast.24), slice={[0:128], [768:2304]} | slice | bytes 786432 | tf_op jit(solution)/shard_map/slice | solution.py:429
  6.6 0.4 collective-permute-start.4
  7.6 0.7 %pad_add_fusion.1.place_ref = s32[3]{0:T(128)} fusion(s32[1]{0:T(128)} %constant.6.clone.1, s32[1]{0:T(128)} %bitcast.18, s32[1]{0:T(128)} %bitcast), kind=kLoop, calls=%fused_computation.7 | loop fusion | flops 6 | bytes 24 | tf_op jit(solution)/shard_map/stack | solution.py:439
  8.3 0.7 %copy.15 = f32[1,31,1536]{2,1,0:T(8,128)} copy(f32[1,31,1536]{2,0,1:T(1,128)S(1)} %copy-done.5) | data formatting | bytes 380928
  9.0 2.2 %collective-permute-done.4.cot_low.cot_high = bf16[16,1536]{1,0:T(8,128)(2,1)S(1)} collective-permute-done((bf16[16,1536]{1,0:T(8,128)(2,1)S(1)}, bf16[16,1536]{1,0:T(8,128)(2,1)S(1)}, u32[]{:S(2)}, u32[]{:S(2)}) %collective-permute-start.4) | collective-permute-done | bytes 49184 | tf_op jit(solution)/shard_map/ppermute | solution.py:411
  11.2 0.6 copy-done.4
  11.9 0.2 copy-done
  12.1 14.3 %conv.1 = (bf16[128,1536]{1,0:T(8,128)(2,1)}, bf16[128,1536]{1,0:T(8,128)(2,1)}, bf16[32,1536]{1,0:T(8,128)(2,1)}) custom-call(s32[3]{0:T(128)} %pad_add_fusion.1.place_ref, bf16[128,1536]{1,0:T(8,128)(2,1)} %bitcast.22, bf16[32,1536]{1,0:T(8,128)(2,1)} %copy-done.3, bf16[32,1536]{1,0:T(8,128)(2,1)} %copy-done.3, bf16[128,2304]{1,0:T(8,128)(2,1)} %copy-done, ...), custom_call_target="tpu_custom_call" | custom-call | flops 36569088 | bytes 1966080 | tf_op jit(solution)/shard_map/conv/pallas_call | solution.py:132
  26.4 1.6 %collective-permute-start.5 = (bf16[32,1536]{1,0:T(8,128)(2,1)}, bf16[32,1536]{1,0:T(8,128)(2,1)S(1)}, u32[]{:S(2)}, u32[]{:S(2)}) collective-permute-start(bf16[32,1536]{1,0:T(8,128)(2,1)} %get-tuple-element.15), channel_id=1, source_target_pairs={{0,8},{8,0},{16,24},{24,16},{1,9},{9,1},{17,25},{25,17},{2,10},{10... | collective-permute-start | bytes 294920 | tf_op jit(solution)/shard_map/ppermute | solution.py:389
  28.1 3.5 %collective-permute-done.5 = bf16[32,1536]{1,0:T(8,128)(2,1)S(1)} collective-permute-done((bf16[32,1536]{1,0:T(8,128)(2,1)}, bf16[32,1536]{1,0:T(8,128)(2,1)S(1)}, u32[]{:S(2)}, u32[]{:S(2)}) %collective-permute-start.5) | collective-permute-done | bytes 98336 | tf_op jit(solution)/shard_map/ppermute | solution.py:389
  31.6 0.9 %add_convert_fusion.1 = bf16[32,1536]{1,0:T(8,128)(2,1)S(1)} fusion(bf16[32,1536]{1,0:T(8,128)(2,1)S(1)} %collective-permute-done.5, bf16[32,1536]{1,0:T(8,128)(2,1)} %get-tuple-element.15), kind=kLoop, calls=%fused_computation.4 | loop fusion | flops 196608 | bytes 294912 | tf_op jit(solution)/shard_map/convert_element_type | solution.py:391
  32.5 2.7 %collective-permute-start.6 = (bf16[32,1536]{1,0:T(8,128)(2,1)S(1)}, bf16[32,1536]{1,0:T(8,128)(2,1)S(1)}, u32[]{:S(2)}, u32[]{:S(2)}) collective-permute-start(bf16[32,1536]{1,0:T(8,128)(2,1)S(1)} %add_convert_fusion.1), channel_id=1, source_target_pairs={{0,16},{8,24},{16,0},{24,8},{1,17},{9,25},{17,1},{25,9},{2,18},{10... | collective-permute-start | bytes 294920 | tf_op jit(solution)/shard_map/ppermute | solution.py:389
  35.1 2.1 %collective-permute-start = (bf16[128,2304]{1,0:T(8,128)(2,1)S(1)}, bf16[128,2304]{1,0:T(8,128)(2,1)S(1)}, u32[]{:S(2)}, u32[]{:S(2)}) collective-permute-start(bf16[128,2304]{1,0:T(8,128)(2,1)S(1)} %bitcast.19), channel_id=1, source_target_pairs={{0,1},{1,0},{2,3},{3,2},{4,5},{5,4},{6,7},{7,6},{8,9},{9,8},{10,11... | collective-permute-start | bytes 1769480 | tf_op jit(solution)/shard_map/ppermute | solution.py:438
  37.3 0.9 %slice.16 = bf16[128,768]{1,0:T(8,128)(2,1)S(1)} slice(bf16[128,2304]{1,0:T(8,128)(2,1)} %bitcast.25), slice={[0:128], [0:768]} | slice | bytes 393216 | tf_op jit(solution)/shard_map/slice | solution.py:437
  38.2 0.3 collective-permute-start.2
  38.5 2.4 %collective-permute-done.6 = bf16[32,1536]{1,0:T(8,128)(2,1)S(1)} collective-permute-done((bf16[32,1536]{1,0:T(8,128)(2,1)S(1)}, bf16[32,1536]{1,0:T(8,128)(2,1)S(1)}, u32[]{:S(2)}, u32[]{:S(2)}) %collective-permute-start.6) | collective-permute-done | bytes 98336 | tf_op jit(solution)/shard_map/ppermute | solution.py:389
  40.9 1.5 %collective-permute-start.7 = (bf16[32,1536]{1,0:T(8,128)(2,1)S(1)}, bf16[32,1536]{1,0:T(8,128)(2,1)S(1)}, u32[]{:S(2)}, u32[]{:S(2)}) collective-permute-start(bf16[32,1536]{1,0:T(8,128)(2,1)S(1)} %add_convert_fusion), channel_id=1, source_target_pairs={{0,1},{1,0},{2,3},{3,2},{4,5},{5,4},{6,7},{7,6},{8,9},{9,8},{10,11... | collective-permute-start | bytes 294920 | tf_op jit(solution)/shard_map/ppermute | solution.py:389
  42.5 13.5 %collective-permute-done.2.cot_peer_ref = bf16[128,768]{1,0:T(8,128)(2,1)S(1)} collective-permute-done((bf16[128,768]{1,0:T(8,128)(2,1)S(1)}, bf16[128,768]{1,0:T(8,128)(2,1)S(1)}, u32[]{:S(2)}, u32[]{:S(2)}) %collective-permute-start.2) | collective-permute-done | bytes 196640 | tf_op jit(solution)/shard_map/ppermute | solution.py:437
  56.0 4.4 %attention.1 = (bf16[128,768]{1,0:T(8,128)(2,1)}, bf16[128,2304]{1,0:T(8,128)(2,1)}) custom-call(s32[3]{0:T(128)S(1)} %pad_add_fusion.place_ref, bf16[128,2304]{1,0:T(8,128)(2,1)S(1)} %bitcast.20, bf16[128,2304]{1,0:T(8,128)(2,1)S(1)} %collective-permute-done.peer_ref, bf16[128,2304]{1,0:T(8,128)(2,1)S(1)} %copy-done.1, ...), custom_call_target="tpu_custom_call" | custom-call | flops 603979776 | bytes 2359296 | tf_op jit(solution)/shard_map/attention/pallas_call | solution.py:235
  60.4 0.6 slice.19
  61.0 0.9 %copy.12 = f32[1,31,1536]{2,0,1:T(1,128)} copy(f32[1,31,1536]{2,1,0:T(8,128)S(1)} %slice_bitcast_fusion) | data formatting | bytes 380928
  (19 shorter events, 0.2 us)
Async XLA Ops:
  0.6 10.6 %collective-permute-start.1 = (bf16[128,2304]{1,0:T(8,128)(2,1)}, bf16[128,2304]{1,0:T(8,128)(2,1)S(1)}, u32[]{:S(2)}, u32[]{:S(2)}) collective-permute-start(bf16[128,2304]{1,0:T(8,128)(2,1)} %bitcast.23), channel_id=1, source_target_pairs={{0,6},{2,0},{4,2},{6,4},{1,7},{3,1},{5,3},{7,5},{8,14},{10,8},{12,... | collective-permute-start | bytes 1769480 | tf_op jit(solution)/shard_map/ppermute | solution.py:430
  4.0 7.2 %collective-permute-start.3 = (bf16[32,1536]{1,0:T(8,128)(2,1)S(1)}, bf16[32,1536]{1,0:T(8,128)(2,1)S(1)}, u32[]{:S(2)}, u32[]{:S(2)}) collective-permute-start(bf16[32,1536]{1,0:T(8,128)(2,1)S(1)} %dynamic-slice_bitcast_fusion), channel_id=1, source_target_pairs={{0,1},{1,0},{2,3},{3,2},{4,5},{5,4},{6,7},{7,6},{8,9},{9,8},{10,11... | collective-permute-start | bytes 294920 | tf_op jit(solution)/shard_map/ppermute | solution.py:411
  5.5 2.8 %copy-start.5 = (f32[1,31,1536]{2,0,1:T(1,128)S(1)}, f32[1,31,1536]{2,0,1:T(1,128)}, u32[]{:S(2)}) copy-start(f32[1,31,1536]{2,0,1:T(1,128)} %param.10) | copy-start | bytes 571396
  6.6 4.6 %collective-permute-start.4 = (bf16[16,1536]{1,0:T(8,128)(2,1)S(1)}, bf16[16,1536]{1,0:T(8,128)(2,1)S(1)}, u32[]{:S(2)}, u32[]{:S(2)}) collective-permute-start(bf16[16,1536]{1,0:T(8,128)(2,1)S(1)} %constant_dynamic-slice_fusion), channel_id=1, source_target_pairs={{0,7},{1,6},{2,1},{3,0},{4,3},{5,2},{6,5},{7,4},{8,15},{9,14},{10,... | collective-permute-start | bytes 147464 | tf_op jit(solution)/shard_map/ppermute | solution.py:411
  11.2 0.6 copy-start.4
  11.2 0.7 %copy-start.3 = (bf16[32,1536]{1,0:T(8,128)(2,1)}, bf16[32,1536]{1,0:T(8,128)(2,1)S(1)}, u32[]{:S(2)}) copy-start(bf16[32,1536]{1,0:T(8,128)(2,1)S(1)} %collective-permute-done.3.gated_low.gated_high) | copy-start | bytes 294916
  11.2 0.8 %copy-start = (bf16[128,2304]{1,0:T(8,128)(2,1)}, bf16[128,2304]{1,0:T(8,128)(2,1)S(1)}, u32[]{:S(2)}) copy-start(bf16[128,2304]{1,0:T(8,128)(2,1)S(1)} %collective-permute-done.1.cot_ref) | copy-start | bytes 1769476
  12.1 23.1 %copy-start.2 = (bf16[1,1,128,2304]{3,2,1,0:T(8,128)(2,1)S(1)}, bf16[1,1,128,2304]{3,2,1,0:T(8,128)(2,1)}, u32[]{:S(2)}) copy-start(bf16[1,1,128,2304]{3,2,1,0:T(8,128)(2,1)} %param.6) | copy-start | bytes 1769476
  26.4 29.6 %copy-start.1 = (bf16[128,2304]{1,0:T(8,128)(2,1)S(1)}, bf16[128,2304]{1,0:T(8,128)(2,1)}, u32[]{:S(2)}) copy-start(bf16[128,2304]{1,0:T(8,128)(2,1)} %copy-done) | copy-start | bytes 1769476
  26.4 5.1 %collective-permute-start.5 = (bf16[32,1536]{1,0:T(8,128)(2,1)}, bf16[32,1536]{1,0:T(8,128)(2,1)S(1)}, u32[]{:S(2)}, u32[]{:S(2)}) collective-permute-start(bf16[32,1536]{1,0:T(8,128)(2,1)} %get-tuple-element.15), channel_id=1, source_target_pairs={{0,8},{8,0},{16,24},{24,16},{1,9},{9,1},{17,25},{25,17},{2,10},{10... | collective-permute-start | bytes 294920 | tf_op jit(solution)/shard_map/ppermute | solution.py:389
  32.5 8.4 %collective-permute-start.6 = (bf16[32,1536]{1,0:T(8,128)(2,1)S(1)}, bf16[32,1536]{1,0:T(8,128)(2,1)S(1)}, u32[]{:S(2)}, u32[]{:S(2)}) collective-permute-start(bf16[32,1536]{1,0:T(8,128)(2,1)S(1)} %add_convert_fusion.1), channel_id=1, source_target_pairs={{0,16},{8,24},{16,0},{24,8},{1,17},{9,25},{17,1},{25,9},{2,18},{10... | collective-permute-start | bytes 294920 | tf_op jit(solution)/shard_map/ppermute | solution.py:389
  35.1 20.9 %collective-permute-start = (bf16[128,2304]{1,0:T(8,128)(2,1)S(1)}, bf16[128,2304]{1,0:T(8,128)(2,1)S(1)}, u32[]{:S(2)}, u32[]{:S(2)}) collective-permute-start(bf16[128,2304]{1,0:T(8,128)(2,1)S(1)} %bitcast.19), channel_id=1, source_target_pairs={{0,1},{1,0},{2,3},{3,2},{4,5},{5,4},{6,7},{7,6},{8,9},{9,8},{10,11... | collective-permute-start | bytes 1769480 | tf_op jit(solution)/shard_map/ppermute | solution.py:438
  38.2 17.8 %collective-permute-start.2 = (bf16[128,768]{1,0:T(8,128)(2,1)S(1)}, bf16[128,768]{1,0:T(8,128)(2,1)S(1)}, u32[]{:S(2)}, u32[]{:S(2)}) collective-permute-start(bf16[128,768]{1,0:T(8,128)(2,1)S(1)} %slice.16), channel_id=1, source_target_pairs={{0,7},{1,6},{2,1},{3,0},{4,3},{5,2},{6,5},{7,4},{8,15},{9,14},{10,... | collective-permute-start | bytes 589832 | tf_op jit(solution)/shard_map/ppermute | solution.py:437
  40.9 19.5 %collective-permute-start.7 = (bf16[32,1536]{1,0:T(8,128)(2,1)S(1)}, bf16[32,1536]{1,0:T(8,128)(2,1)S(1)}, u32[]{:S(2)}, u32[]{:S(2)}) collective-permute-start(bf16[32,1536]{1,0:T(8,128)(2,1)S(1)} %add_convert_fusion), channel_id=1, source_target_pairs={{0,1},{1,0},{2,3},{3,2},{4,5},{5,4},{6,7},{7,6},{8,9},{9,8},{10,11... | collective-permute-start | bytes 294920 | tf_op jit(solution)/shard_map/ppermute | solution.py:389

commit v2 on v1

--- a/solution.py
+++ b/solution.py
@@ -15,88 +15,103 @@
 EDGE = 32
 SLIM = 16
 GROUP = 4
+PRICE = 512
+TILES = 4
+LIMIT = 16 * 1024 * 1024
 F32 = jnp.float32
 BF16 = jnp.bfloat16
 
 
-def conv_kernel(
-    place_ref, gated_ref, gated_low, gated_high, cot_ref, cot_low, cot_high, taps_ref, bias_ref,
-    out_ref, grad_ref, sums_ref, source, slopes, partial,
+def tap_sums(read, tap, tiles):
+    sums = [[None, None] for _ in range(tiles)]
+    for k in range(KSIZE):
+        weight = tap(k)
+        for tile in range(tiles):
+            term = weight * read(tile, k)
+            held = sums[tile][k % 2]
+            sums[tile][k % 2] = term if held is None else held + term
+    return [even + odd for even, odd in sums]
+
+
+def row_block(start):
+    return pl.ds(start, 8)
+
+
+def pre_kernel(
+    place_ref, gated_ref, gated_low, gated_high, taps_ref, bias_ref, out_ref, source, slopes,
+    valid,
 ):
     rows, width = gated_ref.shape
-    first, length, frames = place_ref[0], place_ref[1], place_ref[2]
-
-    def frame_of(start, count):
-        return first + start + lax.broadcasted_iota(jnp.int32, (count, LANES), 0)
-
-    for column in range(width // LANES):
-        lanes = pl.ds(column * LANES, LANES)
-
-        def fill(value, start):
-            count = value.shape[0]
-            frame = frame_of(start, count)
-            keep = (frame >= 0) & (frame < length)
-            source[pl.ds(start + EDGE, count), :] = jnp.where(keep, value.astype(F32), 0.0)
-
-        def fill_cot(value, start):
-            count = value.shape[0]
-            frame = frame_of(start, count)
-            keep = (frame >= 0) & (frame < frames)
-            slopes[pl.ds(start + SLIM, count), :] = jnp.where(keep, value.astype(F32), 0.0)
-
-        fill(gated_low[:, lanes], -EDGE)
-        fill(gated_high[:, lanes], rows)
-        fill_cot(cot_low[:, lanes], -SLIM)
-        fill_cot(cot_high[:, lanes], rows)
-
-        @pl.loop(0, rows // EDGE)
-        def _(step):
-            at = pl.multiple_of(step * EDGE, EDGE)
-            fill(gated_ref[pl.ds(at, EDGE), lanes], at)
-            slopes[pl.ds(at + SLIM, EDGE), :] = cot_ref[pl.ds(at, EDGE), lanes].astype(F32)
-
-        taps = [
-            jnp.broadcast_to(taps_ref[k : k + 1, lanes], (8, LANES)) for k in range(KSIZE)
-        ]
+    first, length = place_ref[0], place_ref[1]
+    frame = first - EDGE + lax.broadcasted_iota(jnp.int32, valid.shape, 0)
+    valid[...] = ((frame >= 0) & (frame < length)).astype(F32)
+
+    @pl.loop(0, width // LANES)
+    def _(column):
+        lanes = pl.ds(pl.multiple_of(column * LANES, LANES), LANES)
+
+        def put(ref, start, at):
+            to = pl.ds(at, 16)
+            block = ref[pl.ds(start, 16), lanes].astype(F32)
+            source[column, to, :] = block * valid[to, :]
+
+        for start in range(0, EDGE, 16):
+            put(gated_low, start, start)
+            put(gated_high, start, EDGE + rows + start)
+        for start in range(0, rows, 16):
+            put(gated_ref, start, EDGE + start)
         bias = jnp.broadcast_to(bias_ref[:, lanes], (8, LANES))
-
-        def weighted(read, order, base):
-            parts = [base, None, None, None]
+        for start in range(0, rows + 2 * SLIM, 8 * TILES):
+            pres = tap_sums(
+                lambda tile, k: source[column, row_block(start + 8 * tile + 1 + k), :],
+                lambda k: jnp.broadcast_to(taps_ref[k, :, lanes], (8, LANES)),
+                TILES,
+            )
+            swishes = []
+            for tile, pre in enumerate(pres):
+                pre = pre + bias
+                gate = jax.nn.sigmoid(pre)
+                swish = pre * gate
+                slopes[column, row_block(start + 8 * tile), :] = gate + swish * (1.0 - gate)
+                swishes.append(swish)
+            for tile in range(0, TILES, 2):
+                at = start + 8 * tile - SLIM
+                if 0 <= at < rows:
+                    pair = jnp.concatenate(swishes[tile : tile + 2], axis=0)
+                    out_ref[pl.ds(at, 16), lanes] = pair.astype(BF16)
+
+
+def sums_kernel(
+    place_ref, source, slopes, cot_ref, cot_low, cot_high, grads, sums_ref, partial
+):
+    columns, wide, _ = slopes.shape
+    rows = wide - 2 * SLIM
+    first, frames = place_ref[0], place_ref[2]
+    embed = cot_ref.shape[1] - columns * LANES
+    low_kept = (first > 0).astype(F32)
+    high_kept = (first + rows < frames).astype(F32)
+
+    @pl.loop(0, columns)
+    def _(column):
+        lanes = pl.ds(pl.multiple_of(column * LANES, LANES), LANES)
+        shifted = pl.ds(pl.multiple_of(embed + column * LANES, LANES), LANES)
+
+        def put(cot, at):
+            to = pl.ds(at, 16)
+            grads[column, to, :] = cot.astype(F32) * slopes[column, to, :]
+
+        put(cot_low[:, lanes].astype(F32) * low_kept, 0)
+        put(cot_high[:, lanes].astype(F32) * high_kept, rows + SLIM)
+        for at in range(0, rows, 16):
+            put(cot_ref[pl.ds(at, 16), shifted], at + SLIM)
+
+        totals = [None] * (KSIZE + 1)
+        for at in range(0, rows, 8):
+            grad = grads[column, row_block(at + SLIM), :]
             for k in range(KSIZE):
-                term = taps[k] * read(order(k))
-                slot = k % 4
-                parts[slot] = term if parts[slot] is None else parts[slot] + term
-            return (parts[0] + parts[1]) + (parts[2] + parts[3])
-
-        def pre_tile(at):
-            pre = weighted(lambda k: source[pl.ds(at + 1 + k, 8), :], lambda k: k, bias)
-            gate = jax.nn.sigmoid(pre)
-            swish = pre * gate
-            where = pl.ds(at, 8)
-            slopes[where, :] = slopes[where, :] * (gate + swish * (1.0 - gate))
-            return swish
-
-        for at in range(0, SLIM, 8):
-            pre_tile(at)
-            pre_tile(rows + SLIM + at)
-
-        @pl.loop(0, rows // 16)
-        def _(step):
-            at = pl.multiple_of(step * 16, 16)
-            swish = [pre_tile(SLIM + at), pre_tile(SLIM + at + 8)]
-            out_ref[pl.ds(at, 16), lanes] = jnp.concatenate(swish, axis=0).astype(BF16)
-
-        zero = jnp.zeros((8, LANES), F32)
-
-        def gather(step, totals):
-            at = pl.multiple_of(step * 8, 8)
-            grad = slopes[pl.ds(at + SLIM, 8), :]
-            sums = [
-                totals[k] + grad * source[pl.ds(at + SLIM + 1 + k, 8), :] for k in range(KSIZE)
-            ]
-            return (*sums, totals[KSIZE] + grad)
-
-        totals = lax.fori_loop(0, rows // 8, gather, (zero,) * (KSIZE + 1))
+                term = grad * source[column, row_block(at + SLIM + 1 + k), :]
+                totals[k] = term if totals[k] is None else totals[k] + term
+            totals[KSIZE] = grad if totals[KSIZE] is None else totals[KSIZE] + grad
         for k in range(KSIZE + 1):
             partial[8 * k : 8 * k + 8, :] = totals[k]
         summed = partial[pl.ds(0, KSIZE + 1, stride=8), :]
@@ -104,61 +119,81 @@
             summed = summed + partial[pl.ds(sublane, KSIZE + 1, stride=8), :]
         sums_ref[:, lanes] = summed.astype(sums_ref.dtype)
 
-        @pl.loop(0, rows // 16)
-        def _(step):
-            at = pl.multiple_of(step * 16, 16)
-            back = [
-                weighted(
-                    lambda k: slopes[pl.ds(at + shift + SLIM + HALF - k, 8), :],
-                    lambda k: k,
-                    zero,
-                )
-                for shift in (0, 8)
-            ]
-            keep = frame_of(at, 16) < length
-            whole = jnp.where(keep, jnp.concatenate(back, axis=0), 0.0)
-            grad_ref[pl.ds(at, 16), lanes] = whole.astype(BF16)
-
-
-def conv_call(place, gated, gated_low, gated_high, arriving, cot_low, cot_high, taps, bias):
+
+def back_kernel(place_ref, grads, taps_ref, out_ref, valid):
+    rows, width = out_ref.shape
+    first, length = place_ref[0], place_ref[1]
+    frame = first + lax.broadcasted_iota(jnp.int32, valid.shape, 0)
+    valid[...] = (frame < length).astype(F32)
+
+    @pl.loop(0, width // LANES)
+    def _(column):
+        lanes = pl.ds(pl.multiple_of(column * LANES, LANES), LANES)
+        for start in range(0, rows, 8 * TILES):
+            backs = tap_sums(
+                lambda tile, k: grads[
+                    column, row_block(start + 8 * tile + SLIM + HALF - k), :
+                ],
+                lambda k: jnp.broadcast_to(taps_ref[k, :, lanes], (8, LANES)),
+                TILES,
+            )
+            for tile in range(0, TILES, 2):
+                at = start + 8 * tile
+                pair = jnp.concatenate(backs[tile : tile + 2], axis=0)
+                out_ref[pl.ds(at, 16), lanes] = (pair * valid[pl.ds(at, 16), :]).astype(BF16)
+
+
+def conv_calls(place, gated, gated_low, gated_high, arriving, cot_low, cot_high, taps, bias):
     rows, channels = gated.shape
-    width = 2 * LANES
-    offset = (arriving.shape[1] - channels) // width
-
-    def columns(count, shift=0):
-        return pl.BlockSpec((count, width), lambda i: (0, i + shift))
-
-    work = 3 * 2 * KSIZE * rows * channels
-    return pl.pallas_call(
-        conv_kernel,
-        grid=(channels // width,),
-        in_specs=[
-            pl.BlockSpec(memory_space=pltpu.SMEM),
-            columns(rows),
-            columns(EDGE),
-            columns(EDGE),
-            columns(rows, offset),
-            columns(SLIM),
-            columns(SLIM),
-            columns(KSIZE),
-            columns(1),
-        ],
-        out_specs=[columns(rows), columns(rows), columns(KSIZE + 1)],
-        out_shape=[
-            jax.ShapeDtypeStruct((rows, channels), BF16),
-            jax.ShapeDtypeStruct((rows, channels), BF16),
-            jax.ShapeDtypeStruct((KSIZE + 1, channels), BF16),
-        ],
-        scratch_shapes=[
-            pltpu.VMEM((rows + 2 * EDGE, LANES), F32),
-            pltpu.VMEM((rows + 2 * SLIM, LANES), F32),
-            pltpu.VMEM((8 * (KSIZE + 1), LANES), F32),
-        ],
-        cost_estimate=pl.CostEstimate(
-            flops=work, bytes_accessed=10 * rows * channels, transcendentals=rows * channels
-        ),
-        name="conv",
-    )(place, gated, gated_low, gated_high, arriving, cot_low, cot_high, taps, bias)
+    wide = rows + 2 * SLIM
+    scalars = pl.BlockSpec(memory_space=pltpu.SMEM)
+    whole = pl.BlockSpec(memory_space=pltpu.VMEM)
+
+    def shaped(*dims, dtype=BF16):
+        return jax.ShapeDtypeStruct(dims, dtype)
+
+    def stacked(count):
+        return shaped(channels // LANES, count, LANES, dtype=F32)
+
+    def cost(reads, exps=0):
+        return pl.CostEstimate(
+            flops=PRICE * 2 * KSIZE * rows * channels,
+            bytes_accessed=reads * rows * channels,
+            transcendentals=exps,
+        )
+
+    params = pltpu.CompilerParams(vmem_limit_bytes=LIMIT)
+    depth_out, source, slopes = pl.pallas_call(
+        pre_kernel,
+        in_specs=[scalars] + [whole] * 5,
+        out_specs=[whole] * 3,
+        out_shape=[shaped(rows, channels), stacked(rows + 2 * EDGE), stacked(wide)],
+        scratch_shapes=[pltpu.VMEM((rows + 2 * EDGE, LANES), F32)],
+        cost_estimate=cost(8, 2 * rows * channels),
+        compiler_params=params,
+        name="conv_pre",
+    )(place, gated, gated_low, gated_high, taps, bias)
+    grads, sums = pl.pallas_call(
+        sums_kernel,
+        in_specs=[scalars] + [whole] * 5,
+        out_specs=[whole] * 2,
+        out_shape=[stacked(wide), shaped(KSIZE + 1, channels)],
+        scratch_shapes=[pltpu.VMEM((8 * (KSIZE + 1), LANES), F32)],
+        cost_estimate=cost(12),
+        compiler_params=params,
+        name="conv_sums",
+    )(place, source, slopes, arriving, cot_low, cot_high)
+    gated_grad = pl.pallas_call(
+        back_kernel,
+        in_specs=[scalars] + [whole] * 2,
+        out_specs=whole,
+        out_shape=shaped(rows, channels),
+        scratch_shapes=[pltpu.VMEM((rows, LANES), F32)],
+        cost_estimate=cost(6),
+        compiler_params=params,
+        name="conv_back",
+    )(place, grads, taps)
+    return depth_out, gated_grad, sums
 
 
 def attention_kernel(
@@ -242,7 +277,7 @@
             jax.ShapeDtypeStruct((rows, columns), BF16),
         ],
         cost_estimate=pl.CostEstimate(
-            flops=6 * 2 * HEADS * 4 * rows * rows * HD,
+            flops=PRICE // 64 * 6 * 2 * HEADS * 4 * rows * rows * HD,
             bytes_accessed=2 * rows * (3 * columns + 3 * embed),
             transcendentals=HEADS * 4 * rows * rows,
         ),
@@ -381,16 +416,33 @@
     return attention_out, jnp.concatenate([grad_q, grad_k, grad_v], axis=1)
 
 
+def last_sum_kernel(mine_ref, other_ref, taps_ref, bias_ref):
+    total = mine_ref[...].astype(F32) + other_ref[...].astype(F32)
+    for k in range(KSIZE):
+        taps_ref[k] = total[k : k + 1]
+    bias_ref[...] = total[KSIZE:]
+
+
 def summed_over(value, axes):
-    for axis in axes:
-        count = lax.axis_size(axis)
-        step = 1
-        while step < count:
-            other = lax.ppermute(value, axis, [(i, i ^ step) for i in range(count)])
-            total = value.astype(F32) + other.astype(F32)
-            value = total.astype(BF16)
-            step *= 2
-    return total
+    steps = [(axis, 1 << bit) for axis in axes for bit in range(lax.axis_size(axis).bit_length() - 1)]
+    for axis, step in steps:
+        pairs = [(i, i ^ step) for i in range(lax.axis_size(axis))]
+        other = lax.ppermute(value, axis, pairs)
+        if (axis, step) != steps[-1]:
+            value = (value.astype(F32) + other.astype(F32)).astype(BF16)
+    channels = value.shape[1]
+    whole = pl.BlockSpec(memory_space=pltpu.VMEM)
+    return pl.pallas_call(
+        last_sum_kernel,
+        in_specs=[whole] * 2,
+        out_specs=[whole] * 2,
+        out_shape=[
+            jax.ShapeDtypeStruct((KSIZE, 1, channels), F32),
+            jax.ShapeDtypeStruct((1, channels), F32),
+        ],
+        compiler_params=pltpu.CompilerParams(vmem_limit_bytes=LIMIT),
+        name="last_sum",
+    )(value, other)
 
 
 def edges(block, count, pipe_shift):
@@ -437,7 +489,7 @@
         cot_peer = lax.ppermute(sent[:, :embed], ("pipe", "ctx"), crossed)
         peer = lax.ppermute(mixed, "ctx", [(0, 1), (1, 0)])
     place = jnp.stack([first, length, jnp.int32(frames)])
-    depth_out, gated_grad, sums = conv_call(
+    depth_out, gated_grad, sums = conv_calls(
         place,
         gated,
         gated_low,
@@ -445,10 +497,10 @@
         arriving,
         cot_low,
         cot_high,
-        depth_kernel[0],
+        depth_kernel.reshape(KSIZE, 1, -1),
         depth_bias,
     )
-    sums = summed_over(sums, ("dp", "ctx"))
+    kernel_grad, bias_grad = summed_over(sums, ("dp", "ctx"))
     if devices == 2:
         place = jnp.stack([first, (1 - me) * rows, length])
         attention_out, projected_grad = attention_call(place, mixed, peer, arriving, cot_peer)
@@ -461,8 +513,8 @@
         depth_out[None, None],
         projected_grad[None, None],
         gated_grad[None, None],
-        sums[None, :KSIZE],
-        sums[KSIZE:],
+        kernel_grad.reshape(1, KSIZE, -1),
+        bias_grad,
     )
 
 

time: 62.1 us -> 36.5 us (0.59)
  waiting for transfers between devices: 21.6 us -> 4.2 us
  Pallas kernels: 18.7 us -> 15.3 us
  local copies, waits for them, and re-layouts: 5.95 us -> 3.01 us
  other arithmetic: 1.71 us -> 0.21 us
    ppermute x1, waiting for transfers between devices: 13.5 us -> 0.01 us  [local(): cot_peer = lax.ppermute(sent[:, :embed], ('pipe', 'ctx'), crossed)]
    pallas_call x1 -> x4, Pallas kernels: 14.3 us -> 10.9 us  [the longest x1 3.85 us: conv_calls(): pl.pallas_call(pre_kernel, in_specs=[scalars] + [whole] * 5, out_specs=[w...]
    unnamed x14 -> x8, local copies, waits for them, and re-layouts: 2.42 us -> 0.02 us
    ppermute x2, waiting for transfers between devices: 2.22 us -> 0.01 us  [edges(): got = lax.ppermute(piece, ('pipe', 'ctx'), route([(0, 1), (1, 0)]))]
    ppermute x2, starting transfers between devices: 1.91 us -> 3.88 us  [edges(): got = lax.ppermute(piece, ('pipe', 'ctx'), route([(0, 1), (1, 0)]))]
    ppermute x1, starting transfers between devices: 2.43 us -> 0.65 us  [local(): lax.ppermute(sent, 'pipe', [(i, (i - 1) % sections) for i in range(sectio...]
    ppermute x3, waiting for transfers between devices: 5.88 us -> 4.18 us  [summed_over(): other = lax.ppermute(value, axis, pairs)]
    ppermute x1, starting transfers between devices: 2.14 us -> 0.51 us  [local(): peer = lax.ppermute(mixed, 'ctx', [(0, 1), (1, 0)])]
  transfers between devices with their start and end apart: 8 -> 8, of which waited for: 4 -> 2; matrix products, arithmetic and copies ran while one was open for 7% -> 6% of each run, Pallas kernels for 7% -> 40%
where the time goes in v2:
time: 36.5 us; the launch traced here: 36.3 us
  Pallas kernels  15.3 us (42%)
  starting transfers between devices  12.1 us (33%)
  waiting for transfers between devices  4.2 us (12%)
  local copies, waits for them, and re-layouts  3.01 us (8%)
  between operations  1.39 us (4%)
    ppermute x3, starting transfers between devices, summed_over(): other = lax.ppermute(value, axis, pairs)  5.88 us
    pallas_call x1, Pallas kernels, attention_call(): pl.pallas_call(attention_kernel, grid=(1,), in_specs=[pl.BlockSpec(memory...  4.42 us
    ppermute x3, waiting for transfers between devices, summed_over(): other = lax.ppermute(value, axis, pairs)  4.18 us
    ppermute x2, starting transfers between devices, edges(): got = lax.ppermute(piece, ('pipe', 'ctx'), route([(0, 1), (1, 0)]))  3.88 us
    pallas_call x1, Pallas kernels, conv_calls(): pl.pallas_call(pre_kernel, in_specs=[scalars] + [whole] * 5, out_specs=[w...  3.85 us
    pallas_call x1, Pallas kernels, conv_calls(): pl.pallas_call(back_kernel, in_specs=[scalars] + [whole] * 2, out_specs=w...  3.54 us
    pallas_call x1, Pallas kernels, conv_calls(): pl.pallas_call(sums_kernel, in_specs=[scalars] + [whole] * 5, out_specs=[...  2.8 us
    ppermute x1, starting transfers between devices, local(): cot_peer = lax.ppermute(sent[:, :embed], ('pipe', 'ctx'), crossed)  1.21 us
  transfers between devices with their start and end apart: 8, of which 2 were waited for; matrix products, arithmetic and copies ran while one was open for 6% of the time, Pallas kernels for 40%

profile of v2, /device:TPU:0, one launch (start us, length us, event | category | flops | bytes accessed | tf_op | source)
XLA Modules:
  0.0 36.3 jit_solution(14005406320075912856)
XLA Ops:
  0.7 1.0 %dynamic-slice_bitcast_fusion = bf16[32,1536]{1,0:T(8,128)(2,1)S(1)} fusion(bf16[1,1,128,1536]{3,2,1,0:T(8,128)(2,1)} %param.7, s32[]{:T(128)S(6)} %select_n.9), kind=kLoop, calls=%fused_computation.2 | loop fusion | bytes 196612 | tf_op jit(solution)/shard_map/dynamic_slice | solution.py:462
  1.7 3.0 %collective-permute-start.3 = (bf16[32,1536]{1,0:T(8,128)(2,1)S(1)}, bf16[32,1536]{1,0:T(8,128)(2,1)S(1)}, u32[]{:S(2)}, u32[]{:S(2)}) collective-permute-start(bf16[32,1536]{1,0:T(8,128)(2,1)S(1)} %dynamic-slice_bitcast_fusion), channel_id=1, source_target_pairs={{0,1},{1,0},{2,3},{3,2},{4,5},{5,4},{6,7},{7,6},{8,9},{9,8},{10,11... | collective-permute-start | bytes 294920 | tf_op jit(solution)/shard_map/ppermute | solution.py:463
  4.6 0.7 %collective-permute-start.1 = (bf16[128,2304]{1,0:T(8,128)(2,1)}, bf16[128,2304]{1,0:T(8,128)(2,1)S(1)}, u32[]{:S(2)}, u32[]{:S(2)}) collective-permute-start(bf16[128,2304]{1,0:T(8,128)(2,1)} %bitcast.21), channel_id=1, source_target_pairs={{0,6},{2,0},{4,2},{6,4},{1,7},{3,1},{5,3},{7,5},{8,14},{10,8},{12,... | collective-permute-start | bytes 1769480 | tf_op jit(solution)/shard_map/ppermute | solution.py:482
  5.3 1.1 %slice.9 = bf16[128,1536]{1,0:T(8,128)(2,1)S(1)} slice(bf16[128,2304]{1,0:T(8,128)(2,1)} %bitcast.22), slice={[0:128], [768:2304]} | slice | bytes 786432 | tf_op jit(solution)/shard_map/slice | solution.py:481
  6.4 0.9 %collective-permute-start.4 = (bf16[16,1536]{1,0:T(8,128)(2,1)S(1)}, bf16[16,1536]{1,0:T(8,128)(2,1)S(1)}, u32[]{:S(2)}, u32[]{:S(2)}) collective-permute-start(bf16[16,1536]{1,0:T(8,128)(2,1)S(1)} %constant_dynamic-slice_fusion), channel_id=1, source_target_pairs={{0,7},{1,6},{2,1},{3,0},{4,3},{5,2},{6,5},{7,4},{8,15},{9,14},{10,... | collective-permute-start | bytes 147464 | tf_op jit(solution)/shard_map/ppermute | solution.py:463
  7.3 0.9 %slice.8 = bf16[128,768]{1,0:T(8,128)(2,1)S(1)} slice(bf16[128,2304]{1,0:T(8,128)(2,1)} %bitcast.23), slice={[0:128], [0:768]} | slice | bytes 393216 | tf_op jit(solution)/shard_map/slice | solution.py:489
  8.2 1.2 %collective-permute-start.2 = (bf16[128,768]{1,0:T(8,128)(2,1)S(1)}, bf16[128,768]{1,0:T(8,128)(2,1)S(1)}, u32[]{:S(2)}, u32[]{:S(2)}) collective-permute-start(bf16[128,768]{1,0:T(8,128)(2,1)S(1)} %slice.8), channel_id=1, source_target_pairs={{0,7},{1,6},{2,1},{3,0},{4,3},{5,2},{6,5},{7,4},{8,15},{9,14},{10,... | collective-permute-start | bytes 589832 | tf_op jit(solution)/shard_map/ppermute | solution.py:489
  9.4 0.5 %collective-permute-start = (bf16[128,2304]{1,0:T(8,128)(2,1)S(1)}, bf16[128,2304]{1,0:T(8,128)(2,1)S(1)}, u32[]{:S(2)}, u32[]{:S(2)}) collective-permute-start(bf16[128,2304]{1,0:T(8,128)(2,1)S(1)} %bitcast.17), channel_id=1, source_target_pairs={{0,1},{1,0},{2,3},{3,2},{4,5},{5,4},{6,7},{7,6},{8,9},{9,8},{10,11... | collective-permute-start | bytes 1769480 | tf_op jit(solution)/shard_map/ppermute | solution.py:490
  10.6 0.1 pad_add_fusion.1.place_ref
  10.7 0.0 collective-permute-done.3.gated_low.gated_high
  10.7 3.9 %conv_pre.1 = (bf16[128,1536]{1,0:T(8,128)(2,1)}, f32[12,192,128]{2,1,0:T(8,128)S(1)}, f32[12,160,128]{2,1,0:T(8,128)S(1)}) custom-call(s32[3]{0:T(128)S(1)} %pad_add_fusion.1.place_ref, bf16[128,1536]{1,0:T(8,128)(2,1)S(1)} %bitcast.16, bf16[32,1536]{1,0:T(8,128)(2,1)S(1)} %collective-permute-done.3.gated_low.gated_high, ...), custom_call_target="tpu_custom_call" | custom-call | flops 6241124352 | bytes 1572864 | tf_op jit(solution)/shard_map/conv_pre/pallas_call | solution.py:166
  14.6 0.0 collective-permute-done.4.cot_low.cot_high
  14.6 0.0 collective-permute-done.1.cot_ref
  14.6 2.8 %conv_sums.1 = (f32[12,160,128]{2,1,0:T(8,128)S(1)}, bf16[32,1536]{1,0:T(8,128)(2,1)S(1)}) custom-call(s32[3]{0:T(128)S(1)} %pad_add_fusion.1.place_ref, f32[12,192,128]{2,1,0:T(8,128)S(1)} %get-tuple-element.18.source, f32[12,160,128]{2,1,0:T(8,128)S(1)} %get-tuple-element.19.slopes, bf16[128,2304]{1,0:T(8,128)(2,1)S(1)} %collective-permute-done.1.cot_ref, ...), custom_call_target="tpu_custom_call" | custom-call | flops 6241124352 | bytes 2359296 | tf_op jit(solution)/shard_map/conv_sums/pallas_call | solution.py:176
  17.4 1.6 %collective-permute-start.5 = (bf16[32,1536]{1,0:T(8,128)(2,1)S(1)}, bf16[32,1536]{1,0:T(8,128)(2,1)S(1)}, u32[]{:S(2)}, u32[]{:S(2)}) collective-permute-start(bf16[32,1536]{1,0:T(8,128)(2,1)S(1)} %get-tuple-element.21), channel_id=1, source_target_pairs={{0,8},{8,0},{16,24},{24,16},{1,9},{9,1},{17,25},{25,17},{2,10},{10... | collective-permute-start | bytes 294920 | tf_op jit(solution)/shard_map/ppermute | solution.py:430
  19.0 0.1 pad_add_fusion.place_ref
  19.1 3.2 %collective-permute-done.5 = bf16[32,1536]{1,0:T(8,128)(2,1)S(1)} collective-permute-done((bf16[32,1536]{1,0:T(8,128)(2,1)S(1)}, bf16[32,1536]{1,0:T(8,128)(2,1)S(1)}, u32[]{:S(2)}, u32[]{:S(2)}) %collective-permute-start.5) | collective-permute-done | bytes 98336 | tf_op jit(solution)/shard_map/ppermute | solution.py:430
  22.4 2.7 %collective-permute-start.6 = (bf16[32,1536]{1,0:T(8,128)(2,1)S(1)}, bf16[32,1536]{1,0:T(8,128)(2,1)S(1)}, u32[]{:S(2)}, u32[]{:S(2)}) collective-permute-start(bf16[32,1536]{1,0:T(8,128)(2,1)S(1)} %add_convert_fusion.1), channel_id=1, source_target_pairs={{0,16},{8,24},{16,0},{24,8},{1,17},{9,25},{17,1},{25,9},{2,18},{10... | collective-permute-start | bytes 294920 | tf_op jit(solution)/shard_map/ppermute | solution.py:430
  25.0 3.5 %conv_back.1 = bf16[128,1536]{1,0:T(8,128)(2,1)} custom-call(s32[3]{0:T(128)S(1)} %pad_add_fusion.1.place_ref, f32[12,160,128]{2,1,0:T(8,128)S(1)} %get-tuple-element.20.grads, f32[31,1,1536]{2,1,0:T(1,128)S(1)} %bitcast.20), custom_call_target="tpu_custom_call" | custom-call | flops 6241124352 | bytes 1179648 | tf_op jit(solution)/shard_map/conv_back/pallas_call | solution.py:186
  28.6 0.9 %collective-permute-done.6 = bf16[32,1536]{1,0:T(8,128)(2,1)S(1)} collective-permute-done((bf16[32,1536]{1,0:T(8,128)(2,1)S(1)}, bf16[32,1536]{1,0:T(8,128)(2,1)S(1)}, u32[]{:S(2)}, u32[]{:S(2)}) %collective-permute-start.6) | collective-permute-done | bytes 98336 | tf_op jit(solution)/shard_map/ppermute | solution.py:430
  29.5 1.6 %collective-permute-start.7 = (bf16[32,1536]{1,0:T(8,128)(2,1)S(1)}, bf16[32,1536]{1,0:T(8,128)(2,1)S(1)}, u32[]{:S(2)}, u32[]{:S(2)}) collective-permute-start(bf16[32,1536]{1,0:T(8,128)(2,1)S(1)} %add_convert_fusion.mine_ref), channel_id=1, source_target_pairs={{0,1},{1,0},{2,3},{3,2},{4,5},{5,4},{6,7},{7,6},{8,9},{9,8},{10,11... | collective-permute-start | bytes 294920 | tf_op jit(solution)/shard_map/ppermute | solution.py:430
  31.1 4.4 %attention.1 = (bf16[128,768]{1,0:T(8,128)(2,1)}, bf16[128,2304]{1,0:T(8,128)(2,1)}) custom-call(s32[3]{0:T(128)S(1)} %pad_add_fusion.place_ref, bf16[128,2304]{1,0:T(8,128)(2,1)S(1)} %bitcast.18, bf16[128,2304]{1,0:T(8,128)(2,1)S(1)} %collective-permute-done.peer_ref, bf16[128,2304]{1,0:T(8,128)(2,1)S(1)} %collective-permute-done.1.cot_ref, ...), custom_call_target="tpu_custom_call" | custom-call | flops 4831838208 | bytes 2359296 | tf_op jit(solution)/shard_map/attention/pallas_call | solution.py:270
  35.5 0.0 collective-permute-done.7.other_ref
  35.6 0.7 %last_sum.1 = (f32[31,1,1536]{2,1,0:T(1,128)}, f32[1,1536]{1,0:T(1,128)}) custom-call(bf16[32,1536]{1,0:T(8,128)(2,1)S(1)} %add_convert_fusion.mine_ref, bf16[32,1536]{1,0:T(8,128)(2,1)S(1)} %collective-permute-done.7.other_ref), custom_call_target="tpu_custom_call" | custom-call | tf_op jit(solution)/shard_map/last_sum/pallas_call | solution.py:435
  (13 shorter events, 0.1 us)
Async XLA Ops:
  0.6 10.1 %copy-start = (bf16[1,1,128,1536]{3,2,1,0:T(8,128)(2,1)S(1)}, bf16[1,1,128,1536]{3,2,1,0:T(8,128)(2,1)}, u32[]{:S(2)}) copy-start(bf16[1,1,128,1536]{3,2,1,0:T(8,128)(2,1)} %param.7) | copy-start | bytes 1179652
  0.6 8.8 %copy-start.1 = (bf16[1,1,128,2304]{3,2,1,0:T(8,128)(2,1)S(1)}, bf16[1,1,128,2304]{3,2,1,0:T(8,128)(2,1)}, u32[]{:S(2)}) copy-start(bf16[1,1,128,2304]{3,2,1,0:T(8,128)(2,1)} %param.6) | copy-start | bytes 1769476
  0.7 10.0 %copy-start.2 = (f32[1,31,1536]{2,0,1:T(1,128)S(1)}, f32[1,31,1536]{2,0,1:T(1,128)}, u32[]{:S(2)}) copy-start(f32[1,31,1536]{2,0,1:T(1,128)} %param.10) | copy-start | bytes 571396
  0.7 10.0 %copy-start.3 = (f32[1,1536]{1,0:T(1,128)S(1)}, f32[1,1536]{1,0:T(1,128)}, u32[]{:S(2)}) copy-start(f32[1,1536]{1,0:T(1,128)} %bias_ref.1) | copy-start | bytes 18436
  1.7 9.0 %collective-permute-start.3 = (bf16[32,1536]{1,0:T(8,128)(2,1)S(1)}, bf16[32,1536]{1,0:T(8,128)(2,1)S(1)}, u32[]{:S(2)}, u32[]{:S(2)}) collective-permute-start(bf16[32,1536]{1,0:T(8,128)(2,1)S(1)} %dynamic-slice_bitcast_fusion), channel_id=1, source_target_pairs={{0,1},{1,0},{2,3},{3,2},{4,5},{5,4},{6,7},{7,6},{8,9},{9,8},{10,11... | collective-permute-start | bytes 294920 | tf_op jit(solution)/shard_map/ppermute | solution.py:463
  4.6 9.9 %collective-permute-start.1 = (bf16[128,2304]{1,0:T(8,128)(2,1)}, bf16[128,2304]{1,0:T(8,128)(2,1)S(1)}, u32[]{:S(2)}, u32[]{:S(2)}) collective-permute-start(bf16[128,2304]{1,0:T(8,128)(2,1)} %bitcast.21), channel_id=1, source_target_pairs={{0,6},{2,0},{4,2},{6,4},{1,7},{3,1},{5,3},{7,5},{8,14},{10,8},{12,... | collective-permute-start | bytes 1769480 | tf_op jit(solution)/shard_map/ppermute | solution.py:482
  6.4 8.2 %collective-permute-start.4 = (bf16[16,1536]{1,0:T(8,128)(2,1)S(1)}, bf16[16,1536]{1,0:T(8,128)(2,1)S(1)}, u32[]{:S(2)}, u32[]{:S(2)}) collective-permute-start(bf16[16,1536]{1,0:T(8,128)(2,1)S(1)} %constant_dynamic-slice_fusion), channel_id=1, source_target_pairs={{0,7},{1,6},{2,1},{3,0},{4,3},{5,2},{6,5},{7,4},{8,15},{9,14},{10,... | collective-permute-start | bytes 147464 | tf_op jit(solution)/shard_map/ppermute | solution.py:463
  8.2 22.9 %collective-permute-start.2 = (bf16[128,768]{1,0:T(8,128)(2,1)S(1)}, bf16[128,768]{1,0:T(8,128)(2,1)S(1)}, u32[]{:S(2)}, u32[]{:S(2)}) collective-permute-start(bf16[128,768]{1,0:T(8,128)(2,1)S(1)} %slice.8), channel_id=1, source_target_pairs={{0,7},{1,6},{2,1},{3,0},{4,3},{5,2},{6,5},{7,4},{8,15},{9,14},{10,... | collective-permute-start | bytes 589832 | tf_op jit(solution)/shard_map/ppermute | solution.py:489
  9.4 21.7 %collective-permute-start = (bf16[128,2304]{1,0:T(8,128)(2,1)S(1)}, bf16[128,2304]{1,0:T(8,128)(2,1)S(1)}, u32[]{:S(2)}, u32[]{:S(2)}) collective-permute-start(bf16[128,2304]{1,0:T(8,128)(2,1)S(1)} %bitcast.17), channel_id=1, source_target_pairs={{0,1},{1,0},{2,3},{3,2},{4,5},{5,4},{6,7},{7,6},{8,9},{9,8},{10,11... | collective-permute-start | bytes 1769480 | tf_op jit(solution)/shard_map/ppermute | solution.py:490
  17.4 5.0 %collective-permute-start.5 = (bf16[32,1536]{1,0:T(8,128)(2,1)S(1)}, bf16[32,1536]{1,0:T(8,128)(2,1)S(1)}, u32[]{:S(2)}, u32[]{:S(2)}) collective-permute-start(bf16[32,1536]{1,0:T(8,128)(2,1)S(1)} %get-tuple-element.21), channel_id=1, source_target_pairs={{0,8},{8,0},{16,24},{24,16},{1,9},{9,1},{17,25},{25,17},{2,10},{10... | collective-permute-start | bytes 294920 | tf_op jit(solution)/shard_map/ppermute | solution.py:430
  22.4 7.1 %collective-permute-start.6 = (bf16[32,1536]{1,0:T(8,128)(2,1)S(1)}, bf16[32,1536]{1,0:T(8,128)(2,1)S(1)}, u32[]{:S(2)}, u32[]{:S(2)}) collective-permute-start(bf16[32,1536]{1,0:T(8,128)(2,1)S(1)} %add_convert_fusion.1), channel_id=1, source_target_pairs={{0,16},{8,24},{16,0},{24,8},{1,17},{9,25},{17,1},{25,9},{2,18},{10... | collective-permute-start | bytes 294920 | tf_op jit(solution)/shard_map/ppermute | solution.py:430
  29.5 6.0 %collective-permute-start.7 = (bf16[32,1536]{1,0:T(8,128)(2,1)S(1)}, bf16[32,1536]{1,0:T(8,128)(2,1)S(1)}, u32[]{:S(2)}, u32[]{:S(2)}) collective-permute-start(bf16[32,1536]{1,0:T(8,128)(2,1)S(1)} %add_convert_fusion.mine_ref), channel_id=1, source_target_pairs={{0,1},{1,0},{2,3},{3,2},{4,5},{5,4},{6,7},{7,6},{8,9},{9,8},{10,11... | collective-permute-start | bytes 294920 | tf_op jit(solution)/shard_map/ppermute | solution.py:430

commit v3 on v0

v3 whole, which is shorter than its diff:
```python
import functools
import math

import jax
import jax.numpy as jnp
from jax import lax
from jax.experimental import pallas as pl
from jax.experimental.pallas import tpu as pltpu
from jax.sharding import PartitionSpec as P

HEADS = 8
HD = 96
KSIZE = 31
HALF = KSIZE // 2
LANES = 128
EDGE = 32
SLIM = 16
GROUP = 4
SPAN = GROUP * HD
SCALE = 1.0 / math.sqrt(HD)
PRICE = 512
TILES = 4
LIMIT = 4 * 1024 * 1024
F32 = jnp.float32
BF16 = jnp.bfloat16


def tap_sums(read, tap, tiles):
    sums = [[None, None] for _ in tiles]
    for k in range(KSIZE):
        weight = tap(k)
        for held, tile in zip(sums, tiles):
            term = weight * read(tile, k)
            held[k % 2] = term if held[k % 2] is None else held[k % 2] + term
    return [even + odd for even, odd in sums]


def row_block(start):
    return pl.ds(start, 8)


def swish_and_slope(source, column, lanes, taps_ref, bias_ref, tiles):
    pres = tap_sums(
        lambda tile, k: source[column, row_block(tile + EDGE - HALF + k), :],
        lambda k: jnp.broadcast_to(taps_ref[k, :, lanes], (8, LANES)),
        tiles,
    )
    bias = jnp.broadcast_to(bias_ref[:, lanes], (8, LANES))
    results = []
    for pre in pres:
        pre = pre + bias
        gate = jax.nn.sigmoid(pre)
        swish = pre * gate
        results.append((swish, gate + swish * (1.0 - gate)))
    return results


def pre_kernel(
    place_ref, length_ref, gated_ref, gated_low, gated_high, taps_ref, bias_ref, out_ref, source,
    slopes, valid,
):
    rows, width = gated_ref.shape
    frame = place_ref[0] - EDGE + lax.broadcasted_iota(jnp.int32, valid.shape, 0)
    valid[...] = ((frame >= 0) & (frame < length_ref[0, 0])).astype(F32)

    @pl.loop(0, width // LANES)
    def _(column):
        lanes = pl.ds(pl.multiple_of(column * LANES, LANES), LANES)

        def put(ref, start, at):
            to = pl.ds(at, 16)
            block = ref[pl.ds(start, 16), lanes].astype(F32)
            source[column, to, :] = block * valid[to, :]

        for start in range(0, EDGE, 16):
            put(gated_low, start, start)
            put(gated_high, start, EDGE + rows + start)
        for start in range(0, rows, 16):
            put(gated_ref, start, EDGE + start)
        for start in range(0, rows, 8 * TILES):
            tiles = range(start, start + 8 * TILES, 8)
            swishes = []
            for tile, (swish, slope) in zip(
                tiles, swish_and_slope(source, column, lanes, taps_ref, bias_ref, tiles)
            ):
                slopes[column, row_block(tile), :] = slope
                swishes.append(swish)
            for index in range(0, TILES, 2):
                pair = jnp.concatenate(swishes[index : index + 2], axis=0)
                out_ref[pl.ds(start + 8 * index, 16), lanes] = pair.astype(BF16)


def sums_kernel(source, slopes, cot_ref, grads, sums_ref, partial):
    columns, rows, _ = slopes.shape
    embed = cot_ref.shape[1] - columns * LANES

    @pl.loop(0, columns)
    def _(column):
        lanes = pl.ds(pl.multiple_of(column * LANES, LANES), LANES)
        shifted = pl.ds(pl.multiple_of(embed + column * LANES, LANES), LANES)
        for at in range(0, rows, 16):
            block = pl.ds(at, 16)
            grads[column, block, :] = cot_ref[block, shifted].astype(F32) * slopes[column, block, :]

        totals = [None] * (KSIZE + 1)
        for at in range(0, rows, 8):
            grad = grads[column, row_block(at), :]
            for k in range(KSIZE):
                term = grad * source[column, row_block(at + EDGE - HALF + k), :]
                totals[k] = term if totals[k] is None else totals[k] + term
            totals[KSIZE] = grad if totals[KSIZE] is None else totals[KSIZE] + grad
        for k in range(KSIZE + 1):
            partial[8 * k : 8 * k + 8, :] = totals[k]
        summed = partial[pl.ds(0, KSIZE + 1, stride=8), :]
        for sublane in range(1, 8):
            summed = summed + partial[pl.ds(sublane, KSIZE + 1, stride=8), :]
        sums_ref[:, lanes] = summed.astype(sums_ref.dtype)


def back_kernel(
    place_ref, length_ref, source, grads, cot_low, cot_high, taps_ref, bias_ref, out_ref, valid, wide
):
    rows, width = out_ref.shape
    across = cot_low.shape[1] // LANES
    base = cot_low.shape[0] - SLIM * (width // LANES // across)
    first, frames = place_ref[0], place_ref[2]
    frame = first + lax.broadcasted_iota(jnp.int32, valid.shape, 0)
    valid[...] = (frame < length_ref[0, 0]).astype(F32)
    low_kept = (first > 0).astype(F32)
    high_kept = (first + rows < frames).astype(F32)

    @pl.loop(0, width // LANES)
    def _(column):
        lanes = pl.ds(pl.multiple_of(column * LANES, LANES), LANES)
        for at in range(0, rows, 8):
            wide[row_block(at + SLIM), :] = grads[column, row_block(at), :]
        sides = (range(-SLIM, 0, 8), range(rows, rows + SLIM, 8))
        tiles = [tile for side in sides for tile in side]
        slopes = [
            slope
            for _, slope in swish_and_slope(source, column, lanes, taps_ref, bias_ref, tiles)
        ]
        block = column // across
        from_lanes = pl.ds(pl.multiple_of((column - block * across) * LANES, LANES), LANES)
        from_rows = pl.ds(pl.multiple_of(base + block * SLIM, SLIM), SLIM)
        for cot_ref, kept, side, at in (
            (cot_low, low_kept, slopes[:2], 0),
            (cot_high, high_kept, slopes[2:], rows + SLIM),
        ):
            cot = cot_ref[from_rows, from_lanes].astype(F32) * kept
            wide[pl.ds(at, SLIM), :] = cot * jnp.concatenate(side, axis=0)

        for start in range(0, rows, 8 * TILES):
            backs = tap_sums(
                lambda tile, k: wide[row_block(tile + SLIM + HALF - k), :],
                lambda k: jnp.broadcast_to(taps_ref[k, :, lanes], (8, LANES)),
                range(start, start + 8 * TILES, 8),
            )
            for index in range(0, TILES, 2):
                at = start + 8 * index
                pair = jnp.concatenate(backs[index : index + 2], axis=0)
                out_ref[pl.ds(at, 16), lanes] = (pair * valid[pl.ds(at, 16), :]).astype(BF16)


SCALARS = pl.BlockSpec(memory_space=pltpu.SMEM)
WHOLE = pl.BlockSpec(memory_space=pltpu.VMEM)
MEMORY = pl.BlockSpec(memory_space=pltpu.HBM)
PARAMS = pltpu.CompilerParams(vmem_limit_bytes=LIMIT)


def shaped(*dims, dtype=BF16):
    return jax.ShapeDtypeStruct(dims, dtype)


def stacked(channels, count):
    return shaped(channels // LANES, count, LANES, dtype=F32)


def conv_cost(rows, channels, reads):
    return pl.CostEstimate(
        flops=PRICE * 2 * KSIZE * rows * channels,
        bytes_accessed=reads * rows * channels,
        transcendentals=rows * channels,
    )


def conv_pre(place, length, gated, gated_low, gated_high, taps, bias):
    rows, channels = gated.shape
    return pl.pallas_call(
        pre_kernel,
        in_specs=[SCALARS] * 2 + [WHOLE] * 5,
        out_specs=[WHOLE] * 3,
        out_shape=[
            shaped(rows, channels), stacked(channels, rows + 2 * EDGE), stacked(channels, rows)
        ],
        scratch_shapes=[pltpu.VMEM((rows + 2 * EDGE, LANES), F32)],
        cost_estimate=conv_cost(rows, channels, 8),
        compiler_params=PARAMS,
        name="conv_pre",
    )(place, length, gated, gated_low, gated_high, taps, bias)


def conv_sums(source, slopes, arriving):
    columns, rows, _ = slopes.shape
    channels = columns * LANES
    return pl.pallas_call(
        sums_kernel,
        in_specs=[WHOLE] * 3,
        out_specs=[WHOLE] * 2,
        out_shape=[stacked(channels, rows), shaped(KSIZE + 1, channels)],
        scratch_shapes=[pltpu.VMEM((8 * (KSIZE + 1), LANES), F32)],
        cost_estimate=conv_cost(rows, channels, 12),
        compiler_params=PARAMS,
        name="conv_sums",
    )(source, slopes, arriving)


def conv_back(place, length, source, grads, cot_low, cot_high, taps, bias):
    columns, rows, _ = grads.shape
    channels = columns * LANES
    return pl.pallas_call(
        back_kernel,
        in_specs=[SCALARS] * 2 + [WHOLE] * 6,
        out_specs=WHOLE,
        out_shape=shaped(rows, channels),
        scratch_shapes=[
            pltpu.VMEM((rows, LANES), F32), pltpu.VMEM((rows + 2 * SLIM, LANES), F32)
        ],
        cost_estimate=conv_cost(rows, channels, 6),
        compiler_params=PARAMS,
        name="conv_back",
    )(place, length, source, grads, cot_low, cot_high, taps, bias)


def copy_all(copies, sems):
    started = [
        pltpu.make_async_copy(source, target, sems.at[index])
        for index, (source, target) in enumerate(copies)
    ]
    for copy in started:
        copy.start()

    def wait():
        for copy in started:
            copy.wait()

    return wait


def in_hbm(*arrays):
    return [pltpu.with_memory_space_constraint(array, pltpu.HBM) for array in arrays]


def cut_edges_kernel(start_ref, gated_ref, sent_ref, edge_ref, cot_ref, sems):
    rows, embed = gated_ref.shape[0], cot_ref.shape[1]
    edge = pl.ds(pl.multiple_of(start_ref[0], 16), EDGE)
    slim = pl.ds(pl.multiple_of(start_ref[1], 16), SLIM)
    copies = [
        (gated_ref.at[edge], edge_ref),
        (sent_ref.at[:, pl.ds(0, embed)], cot_ref.at[pl.ds(0, rows)]),
    ]
    for block in range(sent_ref.shape[1] // embed - 1):
        source = sent_ref.at[slim, pl.ds((block + 1) * embed, embed)]
        copies.append((source, cot_ref.at[pl.ds(rows + block * SLIM, SLIM)]))
    copy_all(copies, sems)()


def cut_edges(gated, sent, last):
    rows, channels = gated.shape
    embed = HEADS * HD
    blocks = channels // embed
    starts = jnp.stack([last * (rows - EDGE), last * (rows - SLIM)])
    return pl.pallas_call(
        cut_edges_kernel,
        in_specs=[SCALARS] + [MEMORY] * 2,
        out_specs=[WHOLE] * 2,
        out_shape=[shaped(EDGE, channels), shaped(rows + blocks * SLIM, embed)],
        scratch_shapes=[pltpu.SemaphoreType.DMA((2 + blocks,))],
        compiler_params=PARAMS,
        name="cut_edges",
    )(starts, *in_hbm(gated, sent))


def cut_heads_kernel(mixed_ref, *rest):
    *part_refs, sems = rest
    copies = []
    for group, part_ref in enumerate(part_refs):
        for block in range(3):
            source = mixed_ref.at[:, pl.ds(block * HEADS * HD + group * SPAN, SPAN)]
            copies.append((source, part_ref.at[:, pl.ds(block * SPAN, SPAN)]))
    copy_all(copies, sems)()


def cut_heads(mixed):
    groups = HEADS // GROUP
    return pl.pallas_call(
        cut_heads_kernel,
        in_specs=[MEMORY],
        out_specs=[WHOLE] * groups,
        out_shape=[shaped(mixed.shape[0], 3 * SPAN)] * groups,
        scratch_shapes=[pltpu.SemaphoreType.DMA((3 * groups,))],
        compiler_params=PARAMS,
        name="cut_heads",
    )(*in_hbm(mixed))


def attend_group(group, place_ref, length_ref, mine_ref, peer_ref, cot_ref, cot_peer_ref, bias,
                 out_part, grad_part):
    rows = mine_ref.shape[0]
    embed = HEADS * HD
    base = group * SPAN
    row = lax.broadcasted_iota(jnp.int32, bias.shape, 0)
    frame = jnp.where(row < rows, row + place_ref[0], row - rows + place_ref[1])
    bias[...] = jnp.where(frame < length_ref[0, 0], 0.0, -1e30)
    across = (((1,), (1,)), ((), ()))
    downward = (((0,), (0,)), ((), ()))

    def both(block, start, width):
        mine = mine_ref[:, block * embed + base + start : block * embed + base + start + width]
        peer = peer_ref[:, block * SPAN + start : block * SPAN + start + width]
        return jnp.concatenate([mine, peer], axis=0)

    tiles = SPAN // LANES
    totals = [[None] * tiles for _ in range(4)]
    for head in range(GROUP):
        low = head * HD
        tile = low // LANES
        count = (low + HD - 1) // LANES - tile + 1
        width = count * LANES
        start = tile * LANES
        lane = lax.broadcasted_iota(jnp.int32, (2 * rows, width), 1) + start
        here = (lane >= low) & (lane < low + HD)

        def own(value):
            return jnp.where(here, value, jnp.zeros((), BF16))

        query = both(0, start, width)
        key = own(both(1, start, width))
        value = own(both(2, start, width))
        at = base + start
        cot = jnp.concatenate(
            [cot_ref[:, at : at + width], cot_peer_ref[:rows, at : at + width]], axis=0
        )
        scores = lax.dot_general(key, query, across, preferred_element_type=F32)
        scores = scores + jnp.concatenate([bias[...]] * (2 * rows // LANES), axis=1)
        top = jnp.max(scores, axis=0, keepdims=True)
        raised = jnp.exp((scores - top) * SCALE)
        total = jnp.sum(raised, axis=0, keepdims=True)
        probs_bf = (raised * (1.0 / total)).astype(BF16)
        probs = probs_bf.astype(F32)
        grad_probs = lax.dot_general(value, cot, across, preferred_element_type=F32)
        centre = jnp.sum(probs * grad_probs, axis=0, keepdims=True)
        grad_scores = (probs * (grad_probs - centre) * SCALE).astype(BF16)
        results = (
            lax.dot_general(probs_bf[:, :rows], value, downward, preferred_element_type=F32),
            lax.dot_general(grad_scores[:, :rows], key, downward, preferred_element_type=F32),
            jnp.dot(grad_scores[:rows], own(query), preferred_element_type=F32),
            jnp.dot(probs_bf[:rows], own(cot), preferred_element_type=F32),
        )
        for result, kept in zip(results, totals):
            for index in range(count):
                piece = result[:, index * LANES : (index + 1) * LANES]
                held = kept[tile + index]
                kept[tile + index] = piece if held is None else held + piece
    for index in range(tiles):
        lanes = pl.ds(index * LANES, LANES)
        out_part[:, lanes] = totals[0][index].astype(BF16)
        for block in range(3):
            grad_part[block, :, lanes] = totals[block + 1][index].astype(BF16)

def first_group_kernel(
    place_ref, length_ref, mine_ref, peer_ref, cot_ref, cot_peer_ref, depth_ref, gated_ref,
    depth_out, gated_out, out_part, grad_part, bias, sems,
):
    wait = copy_all([(depth_ref, depth_out), (gated_ref, gated_out)], sems)
    attend_group(
        0, place_ref, length_ref, mine_ref, peer_ref, cot_ref, cot_peer_ref, bias, out_part,
        grad_part,
    )
    wait()


def write_group(group, out_part, grad_part, out_ref, grad_ref, sems):
    copies = [(out_part, out_ref.at[:, pl.ds(group * SPAN, SPAN)])]
    for block in range(3):
        at = block * HEADS * HD + group * SPAN
        copies.append((grad_part.at[block], grad_ref.at[:, pl.ds(at, SPAN)]))
    return copy_all(copies, sems.at[group])


def second_group_kernel(
    place_ref, length_ref, mine_ref, peer_ref, cot_ref, cot_peer_ref, out_first, grad_first,
    out_ref, grad_ref, out_part, grad_part, bias, sems,
):
    wait = write_group(0, out_first, grad_first, out_ref, grad_ref, sems)
    attend_group(
        1, place_ref, length_ref, mine_ref, peer_ref, cot_ref, cot_peer_ref, bias, out_part,
        grad_part,
    )
    write_group(1, out_part, grad_part, out_ref, grad_ref, sems)()
    wait()


def attention_call(group, place, length, mine, peer, arriving, cot_peer, earlier):
    rows, columns = mine.shape
    parts = [shaped(rows, SPAN), shaped(3, rows, SPAN)]
    scratch = [pltpu.VMEM((2 * rows, LANES), F32)]
    if group == 0:
        out_shape = [shaped(*value.shape) for value in earlier] + parts
        out_specs = [MEMORY] * 2 + [WHOLE] * 2
        scratch += [pltpu.SemaphoreType.DMA((2,))]
    else:
        out_shape = [shaped(rows, HEADS * HD), shaped(rows, columns)]
        out_specs = [MEMORY] * 2
        scratch = [pltpu.VMEM(part.shape, BF16) for part in parts] + scratch
        scratch += [pltpu.SemaphoreType.DMA((2, 4))]
    return pl.pallas_call(
        (first_group_kernel, second_group_kernel)[group],
        in_specs=[SCALARS] * 2 + [WHOLE] * 6,
        out_specs=out_specs,
        out_shape=out_shape,
        scratch_shapes=scratch,
        cost_estimate=pl.CostEstimate(
            flops=PRICE // 64 * 6 * 2 * GROUP * 4 * rows * rows * HD,
            bytes_accessed=2 * rows * 9 * SPAN,
            transcendentals=GROUP * 4 * rows * rows,
        ),
        compiler_params=pltpu.CompilerParams(vmem_limit_bytes=4 * LIMIT),
        name=f"attention_{group}",
    )(place, length, mine, peer, arriving, cot_peer, *earlier)


def head_pass(queries, grad_out, keys_in, values_in, valid_keys):
    query_rows, head_dim = queries.shape
    score_scale = 1.0 / math.sqrt(head_dim)
    block_rows = min(512, query_rows)
    block_count = query_rows // block_rows
    frame_count = keys_in.shape[0]
    across = (((1,), (1,)), ((), ()))
    downward = (((0,), (0,)), ((), ()))

    def advance(totals, blocks):
        query_block, grad_block = blocks
        scores = (
            lax.dot_general(query_block, keys_in, across, preferred_element_type=jnp.float32)
            * score_scale
        )
        scores = jnp.where(valid_keys[None, :], scores, -1e30)
        row_top = jnp.max(scores, axis=1, keepdims=True)
        row_total = jnp.sum(jnp.exp(scores - row_top), axis=1, keepdims=True)
        probs_bf = (jnp.exp(scores - row_top) / row_total).astype(jnp.bfloat16)
        attended_full = jnp.dot(probs_bf, values_in, preferred_element_type=jnp.float32)
        attended = attended_full.astype(jnp.bfloat16)
        grad_probs = lax.dot_general(
            grad_block, values_in, across, preferred_element_type=jnp.float32
        )
        centre = jnp.sum(grad_block.astype(jnp.float32) * attended_full, axis=1, keepdims=True)
        grad_scores = (probs_bf.astype(jnp.float32) * (grad_probs - centre) * score_scale).astype(
            jnp.bfloat16
        )
        grad_query = jnp.dot(grad_scores, keys_in, preferred_element_type=jnp.float32).astype(
            jnp.bfloat16
        )
        key_total = totals[0] + lax.dot_general(
            grad_scores, query_block, downward, preferred_element_type=jnp.float32
        )
        value_total = totals[1] + lax.dot_general(
            probs_bf, grad_block, downward, preferred_element_type=jnp.float32
        )
        return ((key_total, value_total), (attended, grad_query))

    zero_grads = jnp.zeros((frame_count, head_dim), jnp.float32)
    blocked = (
        queries.reshape(block_count, block_rows, head_dim),
        grad_out.reshape(block_count, block_rows, head_dim),
    )
    totals, results = lax.scan(advance, (zero_grads, zero_grads), blocked)
    attended = results[0].reshape(query_rows, head_dim)
    grad_query = results[1].reshape(query_rows, head_dim)
    return (attended, grad_query, totals[0], totals[1])


def attend_block(query_part, grad_part, key_value, valid_keys, heads_dev):
    block_width = heads_dev * HD

    def split_heads(matrix):
        return matrix.reshape(matrix.shape[0], heads_dev, HD).transpose(1, 0, 2)

    def join_heads(matrix):
        return matrix.transpose(1, 0, 2).reshape(matrix.shape[1], block_width)

    def one_head(items):
        return head_pass(items[0], items[1], items[2], items[3], valid_keys)

    stacked = (
        split_heads(query_part),
        split_heads(grad_part),
        split_heads(key_value[:, :block_width]),
        split_heads(key_value[:, block_width:]),
    )
    attended, grad_query, key_grad, value_grad = lax.map(one_head, stacked)
    key_grads = jnp.concatenate([join_heads(key_grad), join_heads(value_grad)], axis=1)
    return (join_heads(attended), join_heads(grad_query), key_grads)


def attend_by_heads(mixed, grad_attn, valid_keys):
    rows_here = mixed.shape[0]
    devices_ctx = lax.axis_size("ctx")
    embed = HEADS * HD
    part_count = max(devices_ctx // HEADS, 1)
    heads_dev = max(HEADS // devices_ctx, 1)
    block_heads = HEADS // heads_dev
    part_rows = rows_here // part_count
    block_width = heads_dev * HD
    queries = mixed[:, :embed]
    keys_in = mixed[:, embed : 2 * embed]
    values_in = mixed[:, 2 * embed :]

    def by_part(matrix):
        split = matrix.reshape(part_count, part_rows, block_heads, block_width).transpose(
            2, 0, 1, 3
        )
        return split.reshape(devices_ctx, part_rows, block_width)

    def swap(value, concat):
        return lax.all_to_all(value, "ctx", split_axis=0, concat_axis=concat, tiled=True)

    key_value = jnp.concatenate(
        [
            keys_in.reshape(rows_here, block_heads, block_width),
            values_in.reshape(rows_here, block_heads, block_width),
        ],
        axis=2,
    )
    key_value = jnp.repeat(key_value.transpose(1, 0, 2), part_count, axis=0)
    query_part = swap(by_part(queries), 1)[0]
    grad_part = swap(by_part(grad_attn), 1)[0]
    key_value = swap(key_value, 1)[0]
    attended, grad_query, key_grads = attend_block(
        query_part, grad_part, key_value, valid_keys, heads_dev
    )
    outgoing = jnp.concatenate([attended, grad_query], axis=1).reshape(
        devices_ctx, part_rows, 2 * block_width
    )
    returned = swap(outgoing, 0)
    key_returned = swap(
        key_grads.reshape(devices_ctx, rows_here, 2 * block_width).astype(BF16), 0
    ).astype(F32)
    columns = 2 * block_width
    split = returned.reshape(block_heads, part_count, part_rows, columns).transpose(1, 2, 0, 3)
    returned = split.reshape(rows_here, block_heads, columns)
    attention_out = returned[:, :, :block_width].reshape(rows_here, embed)
    grad_q = returned[:, :, block_width:].reshape(rows_here, embed)
    summed = jnp.sum(
        key_returned.reshape(block_heads, part_count, rows_here, 2 * block_width), axis=1
    )
    summed = summed.astype(BF16).transpose(1, 0, 2)
    grad_k = summed[:, :, :block_width].reshape(rows_here, embed)
    grad_v = summed[:, :, block_width:].reshape(rows_here, embed)
    return attention_out, jnp.concatenate([grad_q, grad_k, grad_v], axis=1)


def add_kernel(mine_ref, other_ref, out_ref):
    out_ref[...] = (mine_ref[...].astype(F32) + other_ref[...].astype(F32)).astype(BF16)


def last_sum_kernel(mine_ref, other_ref, taps_ref, bias_ref):
    total = mine_ref[...].astype(F32) + other_ref[...].astype(F32)
    for k in range(KSIZE):
        taps_ref[k] = total[k : k + 1]
    bias_ref[...] = total[KSIZE:]


def sum_steps():
    return [
        (axis, 1 << bit)
        for axis in ("dp", "ctx")
        for bit in range(lax.axis_size(axis).bit_length() - 1)
    ]


def exchanged(value, axis, step):
    return lax.ppermute(value, axis, [(i, i ^ step) for i in range(lax.axis_size(axis))])


def add(value, other):
    return pl.pallas_call(
        add_kernel,
        in_specs=[WHOLE] * 2,
        out_specs=WHOLE,
        out_shape=shaped(*value.shape),
        compiler_params=PARAMS,
        name="add",
    )(value, other)


def last_sum(value, other):
    channels = value.shape[1]
    return pl.pallas_call(
        last_sum_kernel,
        in_specs=[WHOLE] * 2,
        out_specs=[WHOLE] * 2,
        out_shape=[shaped(KSIZE, 1, channels, dtype=F32), shaped(1, channels, dtype=F32)],
        compiler_params=PARAMS,
        name="last_sum",
    )(value, other)


def route(pairs, pipe_shift):
    sections, devices = lax.axis_size("pipe"), lax.axis_size("ctx")
    return [
        (s * devices + a, ((s - pipe_shift) % sections) * devices + b)
        for s in range(sections)
        for a, b in pairs
    ]


SWAP = [(0, 1), (1, 0)]


def edges(block, count, pipe_shift):
    rows, devices = block.shape[0], lax.axis_size("ctx")
    upward = [(i, i + 1) for i in range(devices - 1)]
    downward = [(b, a) for a, b in upward]
    low = lax.ppermute(block[rows - count :], ("pipe", "ctx"), route(upward, pipe_shift))
    high = lax.ppermute(block[:count], ("pipe", "ctx"), route(downward, pipe_shift))
    return low, high


def local(projected, gated_input, upstream, lengths, depth_kernel, depth_bias):
    embed = HEADS * HD
    sections, devices = lax.axis_size("pipe"), lax.axis_size("ctx")
    me = lax.axis_index("ctx")
    mixed, gated, sent = projected[0, 0], gated_input[0, 0], upstream[0, 0]
    taps = depth_kernel.reshape(KSIZE, 1, -1)
    rows = mixed.shape[0]
    frames = rows * devices
    first = me * rows
    place = jnp.stack([first, (1 - me) * rows, jnp.int32(frames)])
    arriving = lax.ppermute(sent, "pipe", [(i, (i - 1) % sections) for i in range(sections)])
    if devices == 2:
        edge, piece = cut_edges(gated, sent, 1 - me)
        parts = cut_heads(mixed)
        gated_low = gated_high = lax.ppermute(edge, "ctx", SWAP)
        cot_low = cot_high = cot_peer = lax.ppermute(piece, ("pipe", "ctx"), route(SWAP, 1))
        peers = [lax.ppermute(part, "ctx", SWAP) for part in parts]
    else:
        gated_low, gated_high = edges(gated, EDGE, 0)
        cot_low, cot_high = [
            jnp.concatenate(jnp.split(side, side.shape[1] // embed, axis=1), axis=0)
            for side in edges(sent[:, embed:], SLIM, 1)
        ]
    depth_out, source, slopes = conv_pre(
        place, lengths, gated, gated_low, gated_high, taps, depth_bias
    )
    grads, sums = conv_sums(source, slopes, arriving)
    *steps, last_step = sum_steps()
    for step in steps:
        sums = add(sums, exchanged(sums, *step))
    kernel_grad, bias_grad = last_sum(sums, exchanged(sums, *last_step))
    gated_grad = conv_back(
        place, lengths, source, grads, cot_low, cot_high, taps, depth_bias
    )
    if devices == 2:
        given = (mixed, peers[0], arriving, cot_peer)
        depth_out, gated_grad, *first_results = attention_call(
            0, place, lengths, *given, (depth_out, gated_grad)
        )
        given = (mixed, peers[1], arriving, cot_peer)
        attention_out, projected_grad = attention_call(1, place, lengths, *given, first_results)
    else:
        attention_out, projected_grad = attend_by_heads(
            mixed, arriving[:, :embed], jnp.arange(frames) < lengths[0, 0]
        )
    return (
        attention_out[None, None],
        depth_out[None, None],
        projected_grad[None, None],
        gated_grad[None, None],
        kernel_grad.reshape(1, KSIZE, -1),
        bias_grad,
    )


def solution(mesh):
    by_frame = P("pipe", "dp", "ctx", None)
    return jax.shard_map(
        local,
        mesh=mesh,
        in_specs=(
            by_frame,
            by_frame,
            by_frame,
            P("pipe", "dp"),
            P("pipe", None, None),
            P("pipe", None),
        ),
        out_specs=(
            by_frame,
            by_frame,
            by_frame,
            by_frame,
            P("pipe", None, None),
            P("pipe", None),
        ),
        check_vma=False,
    )
```

time: 201 us -> 33 us (0.16)
  other arithmetic: 54.4 us -> 0.15 us
  local copies, waits for them, and re-layouts: 50.4 us -> 0.02 us
  blocking collectives: 24.2 us -> 0 us
  starting transfers between devices: 31.2 us -> 12.3 us
  Pallas kernels: 0 us -> 16.5 us
  between operations: 16 us -> 1.41 us
  waiting for transfers between devices: 13.8 us -> 2.42 us
  matrix products: 9.53 us -> 0 us
    reduce_sum x12 -> x0, other arithmetic: 28.5 us -> none  [the longest x4 28.1 us: local(): jnp.sum(padded[offset:offset + rows_here].astype(jnp.float32) * grad_pre,...]
    another operation x34 -> x0, local copies, waits for them, and re-layouts: 24.7 us -> none  [the longest x32 24.4 us: local(): jnp.stack([jnp.sum(padded[offset:offset + rows_here].astype(jnp.float32)...]
    psum x1 -> x0, blocking collectives: 24.2 us -> none  [local(): kernel_grad, bias_grad = lax.psum((kernel_local, bias_local), ('dp', 'ctx'))]
    broadcast_in_dim x3 -> x0, other arithmetic: 21.3 us -> none  [the longest x1 21 us: local(): gated_grad[None, None]]
    all_to_all x5 -> x0, starting transfers between devices: 19.5 us -> none  [the longest x1 4.37 us: local(): lax.all_to_all(by_part(queries), 'ctx', split_axis=0, concat_axis=1, tile...]
    pallas_call x0 -> x10, Pallas kernels: none -> 16.5 us  [the longest x2 5.24 us: attention_call(): pl.pallas_call((first_group_kernel, second_group_kernel)[group], in_specs...]
    all_to_all x5 -> x0, waiting for transfers between devices: 13.8 us -> none  [the longest x1 8.99 us: local(): lax.all_to_all(key_value, 'ctx', split_axis=0, concat_axis=1, tiled=True)]
    dot_general x24 -> x0, matrix products: 9.53 us -> none  [the longest x4 3.15 us: advance(): jnp.dot(probs_bf, values_in, preferred_element_type=jnp.float32)]
  transfers between devices with their start and end apart: 11 -> 8, of which waited for: 2 -> 3; matrix products, arithmetic and copies ran while one was open for 55% -> 0% of each run, Pallas kernels for 0% -> 48%
where the time goes in v3:
time: 33 us; the launch traced here: 32.8 us
  Pallas kernels  16.5 us (50%)
  starting transfers between devices  12.3 us (37%)
  waiting for transfers between devices  2.42 us (7%)
  between operations  1.41 us (4%)
    ppermute x3, starting transfers between devices, exchanged(): lax.ppermute(value, axis, [(i, i ^ step) for i in range(lax.axis_size(axi...  5.88 us
    pallas_call x2, Pallas kernels, attention_call(): pl.pallas_call((first_group_kernel, second_group_kernel)[group], in_specs...  5.24 us
    pallas_call x1, Pallas kernels, conv_back(): pl.pallas_call(back_kernel, in_specs=[SCALARS] * 2 + [WHOLE] * 6, out_spe...  2.86 us
    pallas_call x1, Pallas kernels, conv_pre(): pl.pallas_call(pre_kernel, in_specs=[SCALARS] * 2 + [WHOLE] * 5, out_spec...  2.61 us
    ppermute x1, starting transfers between devices, local(): lax.ppermute(sent, 'pipe', [(i, (i - 1) % sections) for i in range(sectio...  2.43 us
    ppermute x3, waiting for transfers between devices, exchanged(): lax.ppermute(value, axis, [(i, i ^ step) for i in range(lax.axis_size(axi...  2.41 us
    pallas_call x1, Pallas kernels, conv_sums(): pl.pallas_call(sums_kernel, in_specs=[WHOLE] * 3, out_specs=[WHOLE] * 2,...  2.25 us
    ppermute x2, starting transfers between devices, local(): peers = [lax.ppermute(part, 'ctx', SWAP) for part in parts]  2.09 us
  transfers between devices with their start and end apart: 8, of which 3 were waited for; matrix products, arithmetic and copies ran while one was open for 0% of the time, Pallas kernels for 48%

profile of v3, /device:TPU:0, one launch (start us, length us, event | category | flops | bytes accessed | tf_op | source)
XLA Modules:
  0.0 32.8 jit_solution(16253345816295771706)
XLA Ops:
  0.6 0.0 copy-start.1
  0.7 2.4 %collective-permute-start.1 = (bf16[128,2304]{1,0:T(8,128)(2,1)}, bf16[128,2304]{1,0:T(8,128)(2,1)S(1)}, u32[]{:S(2)}, u32[]{:S(2)}) collective-permute-start(bf16[128,2304]{1,0:T(8,128)(2,1)} %bitcast.20), channel_id=1, source_target_pairs={{0,6},{2,0},{4,2},{6,4},{1,7},{3,1},{5,3},{7,5},{8,14},{10,8},{12,... | collective-permute-start | bytes 1769480 | tf_op jit(solution)/shard_map/ppermute | solution.py:640
  3.1 0.1 pad_add_fusion.1.start_ref
  3.2 1.6 %cut_edges.1 = (bf16[32,1536]{1,0:T(8,128)(2,1)S(1)}, bf16[160,768]{1,0:T(8,128)(2,1)S(1)}) custom-call(s32[2]{0:T(128)S(1)} %pad_add_fusion.1.start_ref, bf16[128,1536]{1,0:T(8,128)(2,1)} %bitcast.16, bf16[128,2304]{1,0:T(8,128)(2,1)} %bitcast.21), custom_call_target="tpu_custom_call" | custom-call | tf_op jit(solution)/shard_map/cut_edges/pallas_call | solution.py:273
  4.7 1.6 %collective-permute-start.4 = (bf16[32,1536]{1,0:T(8,128)(2,1)S(1)}, bf16[32,1536]{1,0:T(8,128)(2,1)S(1)}, u32[]{:S(2)}, u32[]{:S(2)}) collective-permute-start(bf16[32,1536]{1,0:T(8,128)(2,1)S(1)} %get-tuple-element.26), channel_id=1, source_target_pairs={{0,1},{1,0},{2,3},{3,2},{4,5},{5,4},{6,7},{7,6},{8,9},{9,8},{10,11... | collective-permute-start | bytes 294920 | tf_op jit(solution)/shard_map/ppermute | solution.py:644
  6.3 0.3 %collective-permute-start.2 = (bf16[160,768]{1,0:T(8,128)(2,1)S(1)}, bf16[160,768]{1,0:T(8,128)(2,1)S(1)}, u32[]{:S(2)}, u32[]{:S(2)}) collective-permute-start(bf16[160,768]{1,0:T(8,128)(2,1)S(1)} %get-tuple-element.24), channel_id=1, source_target_pairs={{0,7},{1,6},{2,1},{3,0},{4,3},{5,2},{6,5},{7,4},{8,15},{9,14},{10,... | collective-permute-start | bytes 737288 | tf_op jit(solution)/shard_map/ppermute | solution.py:645
  6.7 1.2 %cut_heads.1 = (bf16[128,1152]{1,0:T(8,128)(2,1)S(1)}, bf16[128,1152]{1,0:T(8,128)(2,1)S(1)}) custom-call(bf16[128,2304]{1,0:T(8,128)(2,1)} %bitcast.13), custom_call_target="tpu_custom_call" | custom-call | tf_op jit(solution)/shard_map/cut_heads/pallas_call | solution.py:296
  7.8 1.6 %collective-permute-start.3 = (bf16[128,1152]{1,0:T(8,128)(2,1)S(1)}, bf16[128,1152]{1,0:T(8,128)(2,1)S(1)}, u32[]{:S(2)}, u32[]{:S(2)}) collective-permute-start(bf16[128,1152]{1,0:T(8,128)(2,1)S(1)} %get-tuple-element.25), channel_id=1, source_target_pairs={{0,1},{1,0},{2,3},{3,2},{4,5},{5,4},{6,7},{7,6},{8,9},{9,8},{10,11... | collective-permute-start | bytes 884744 | tf_op jit(solution)/shard_map/ppermute | solution.py:646
  9.4 0.5 %collective-permute-start = (bf16[128,1152]{1,0:T(8,128)(2,1)S(1)}, bf16[128,1152]{1,0:T(8,128)(2,1)S(1)}, u32[]{:S(2)}, u32[]{:S(2)}) collective-permute-start(bf16[128,1152]{1,0:T(8,128)(2,1)S(1)} %get-tuple-element.23), channel_id=1, source_target_pairs={{0,1},{1,0},{2,3},{3,2},{4,5},{5,4},{6,7},{7,6},{8,9},{9,8},{10,11... | collective-permute-start | bytes 884744 | tf_op jit(solution)/shard_map/ppermute | solution.py:646
  9.9 0.1 pad_add_fusion.place_ref
  10.7 0.0 collective-permute-done.4.gated_low.gated_high
  10.7 2.6 %conv_pre.1 = (bf16[128,1536]{1,0:T(8,128)(2,1)S(1)}, f32[12,192,128]{2,1,0:T(8,128)S(1)}, f32[12,128,128]{2,1,0:T(8,128)S(1)}) custom-call(s32[3]{0:T(128)S(1)} %pad_add_fusion.place_ref, s32[1,1]{1,0:T(1,128)S(6)} %copy.12.length_ref, bf16[128,1536]{1,0:T(8,128)(2,1)S(1)} %bitcast.17, bf16[32,1536]{1,0:T(8,128)(2,1)S(1)} %collective-permute-done.4.gated_low.gated_high, ...), custom_call_target="tpu_custom_call" | custom-call | flops 6241124352 | bytes 1572864 | tf_op jit(solution)/shard_map/conv_pre/pallas_call | solution.py:189
  13.3 2.2 %conv_sums.1 = (f32[12,128,128]{2,1,0:T(8,128)S(1)}, bf16[32,1536]{1,0:T(8,128)(2,1)S(1)}) custom-call(f32[12,192,128]{2,1,0:T(8,128)S(1)} %get-tuple-element.28.source, f32[12,128,128]{2,1,0:T(8,128)S(1)} %get-tuple-element.29.slopes, bf16[128,2304]{1,0:T(8,128)(2,1)S(1)} %collective-permute-done.1.cot_ref), custom_call_target="tpu_custom_call" | custom-call | flops 6241124352 | bytes 2359296 | tf_op jit(solution)/shard_map/conv_sums/pallas_call | solution.py:206
  15.6 1.6 %collective-permute-start.5 = (bf16[32,1536]{1,0:T(8,128)(2,1)S(1)}, bf16[32,1536]{1,0:T(8,128)(2,1)S(1)}, u32[]{:S(2)}, u32[]{:S(2)}) collective-permute-start(bf16[32,1536]{1,0:T(8,128)(2,1)S(1)} %get-tuple-element.37.mine_ref), channel_id=1, source_target_pairs={{0,8},{8,0},{16,24},{24,16},{1,9},{9,1},{17,25},{25,17},{2,10},{10... | collective-permute-start | bytes 294920 | tf_op jit(solution)/shard_map/ppermute | solution.py:583
  17.2 0.0 collective-permute-done.2.cot_low.cot_high.cot_peer_ref
  17.2 2.9 %conv_back.1.gated_ref = bf16[128,1536]{1,0:T(8,128)(2,1)S(1)} custom-call(s32[3]{0:T(128)S(1)} %pad_add_fusion.place_ref, s32[1,1]{1,0:T(1,128)S(6)} %copy.12.length_ref, f32[12,192,128]{2,1,0:T(8,128)S(1)} %get-tuple-element.28.source, f32[12,128,128]{2,1,0:T(8,128)S(1)} %get-tuple-element.30.grads, ...), custom_call_target="tpu_custom_call" | custom-call | flops 6241124352 | bytes 1179648 | tf_op jit(solution)/shard_map/conv_back/pallas_call | solution.py:221
  20.1 0.2 collective-permute-done.5.other_ref
  20.3 2.7 %collective-permute-start.6 = (bf16[32,1536]{1,0:T(8,128)(2,1)S(1)}, bf16[32,1536]{1,0:T(8,128)(2,1)S(1)}, u32[]{:S(2)}, u32[]{:S(2)}) collective-permute-start(bf16[32,1536]{1,0:T(8,128)(2,1)S(1)} %add.8.mine_ref), channel_id=1, source_target_pairs={{0,16},{8,24},{16,0},{24,8},{1,17},{9,25},{17,1},{25,9},{2,18},{10... | collective-permute-start | bytes 294920 | tf_op jit(solution)/shard_map/ppermute | solution.py:583
  23.0 2.2 %attention_0.1 = (bf16[128,1536]{1,0:T(8,128)(2,1)}, bf16[128,1536]{1,0:T(8,128)(2,1)}, bf16[128,384]{1,0:T(8,128)(2,1)S(1)}, bf16[3,128,384]{2,1,0:T(8,128)(2,1)S(1)}) custom-call(s32[3]{0:T(128)S(1)} %pad_add_fusion.place_ref, s32[1,1]{1,0:T(1,128)S(6)} %copy.12.length_ref, bf16[128,2304]{1,0:T(8,128)(2,1)S(1)} %bitcast.14, ...), custom_call_target="tpu_custom_call" | custom-call | flops 2415919104 | bytes 884736 | tf_op jit(solution)/shard_map/attention_0/pallas_call | solution.py:417
  25.2 2.1 %collective-permute-done.6.other_ref = bf16[32,1536]{1,0:T(8,128)(2,1)S(1)} collective-permute-done((bf16[32,1536]{1,0:T(8,128)(2,1)S(1)}, bf16[32,1536]{1,0:T(8,128)(2,1)S(1)}, u32[]{:S(2)}, u32[]{:S(2)}) %collective-permute-start.6) | collective-permute-done | bytes 98336 | tf_op jit(solution)/shard_map/ppermute | solution.py:583
  27.4 1.6 %collective-permute-start.7 = (bf16[32,1536]{1,0:T(8,128)(2,1)S(1)}, bf16[32,1536]{1,0:T(8,128)(2,1)S(1)}, u32[]{:S(2)}, u32[]{:S(2)}) collective-permute-start(bf16[32,1536]{1,0:T(8,128)(2,1)S(1)} %add.9.mine_ref), channel_id=1, source_target_pairs={{0,1},{1,0},{2,3},{3,2},{4,5},{5,4},{6,7},{7,6},{8,9},{9,8},{10,11... | collective-permute-start | bytes 294920 | tf_op jit(solution)/shard_map/ppermute | solution.py:583
  29.0 3.0 %attention_1.1 = (bf16[128,768]{1,0:T(8,128)(2,1)}, bf16[128,2304]{1,0:T(8,128)(2,1)}) custom-call(s32[3]{0:T(128)S(1)} %pad_add_fusion.place_ref, s32[1,1]{1,0:T(1,128)S(6)} %copy.12.length_ref, bf16[128,2304]{1,0:T(8,128)(2,1)S(1)} %bitcast.15, bf16[128,1152]{1,0:T(8,128)(2,1)S(1)} %collective-permute-done.peer_ref, ...), custom_call_target="tpu_custom_call" | custom-call | flops 2415919104 | bytes 884736 | tf_op jit(solution)/shard_map/attention_1/pallas_call | solution.py:417
  32.0 0.1 collective-permute-done.7.other_ref
  32.1 0.7 %last_sum.1 = (f32[31,1,1536]{2,1,0:T(1,128)}, f32[1,1536]{1,0:T(1,128)}) custom-call(bf16[32,1536]{1,0:T(8,128)(2,1)S(1)} %add.9.mine_ref, bf16[32,1536]{1,0:T(8,128)(2,1)S(1)} %collective-permute-done.7.other_ref), custom_call_target="tpu_custom_call" | custom-call | tf_op jit(solution)/shard_map/last_sum/pallas_call | solution.py:599
  (12 shorter events, 0.1 us)
Async XLA Ops:
  0.6 10.1 %copy-start.1 = (bf16[1,1,128,1536]{3,2,1,0:T(8,128)(2,1)S(1)}, bf16[1,1,128,1536]{3,2,1,0:T(8,128)(2,1)}, u32[]{:S(2)}) copy-start(bf16[1,1,128,1536]{3,2,1,0:T(8,128)(2,1)} %param.7) | copy-start | bytes 1179652
  0.6 10.0 %copy-start.2 = (f32[1,31,1536]{2,0,1:T(1,128)S(1)}, f32[1,31,1536]{2,0,1:T(1,128)}, u32[]{:S(2)}) copy-start(f32[1,31,1536]{2,0,1:T(1,128)} %param.10) | copy-start | bytes 571396
  0.7 10.0 %copy-start.3 = (f32[1,1536]{1,0:T(1,128)S(1)}, f32[1,1536]{1,0:T(1,128)}, u32[]{:S(2)}) copy-start(f32[1,1536]{1,0:T(1,128)} %bias_ref.3) | copy-start | bytes 18436
  0.7 12.7 %collective-permute-start.1 = (bf16[128,2304]{1,0:T(8,128)(2,1)}, bf16[128,2304]{1,0:T(8,128)(2,1)S(1)}, u32[]{:S(2)}, u32[]{:S(2)}) collective-permute-start(bf16[128,2304]{1,0:T(8,128)(2,1)} %bitcast.20), channel_id=1, source_target_pairs={{0,6},{2,0},{4,2},{6,4},{1,7},{3,1},{5,3},{7,5},{8,14},{10,8},{12,... | collective-permute-start | bytes 1769480 | tf_op jit(solution)/shard_map/ppermute | solution.py:640
  4.7 5.9 %collective-permute-start.4 = (bf16[32,1536]{1,0:T(8,128)(2,1)S(1)}, bf16[32,1536]{1,0:T(8,128)(2,1)S(1)}, u32[]{:S(2)}, u32[]{:S(2)}) collective-permute-start(bf16[32,1536]{1,0:T(8,128)(2,1)S(1)} %get-tuple-element.26), channel_id=1, source_target_pairs={{0,1},{1,0},{2,3},{3,2},{4,5},{5,4},{6,7},{7,6},{8,9},{9,8},{10,11... | collective-permute-start | bytes 294920 | tf_op jit(solution)/shard_map/ppermute | solution.py:644
  6.3 10.9 %collective-permute-start.2 = (bf16[160,768]{1,0:T(8,128)(2,1)S(1)}, bf16[160,768]{1,0:T(8,128)(2,1)S(1)}, u32[]{:S(2)}, u32[]{:S(2)}) collective-permute-start(bf16[160,768]{1,0:T(8,128)(2,1)S(1)} %get-tuple-element.24), channel_id=1, source_target_pairs={{0,7},{1,6},{2,1},{3,0},{4,3},{5,2},{6,5},{7,4},{8,15},{9,14},{10,... | collective-permute-start | bytes 737288 | tf_op jit(solution)/shard_map/ppermute | solution.py:645
  7.8 15.1 %collective-permute-start.3 = (bf16[128,1152]{1,0:T(8,128)(2,1)S(1)}, bf16[128,1152]{1,0:T(8,128)(2,1)S(1)}, u32[]{:S(2)}, u32[]{:S(2)}) collective-permute-start(bf16[128,1152]{1,0:T(8,128)(2,1)S(1)} %get-tuple-element.25), channel_id=1, source_target_pairs={{0,1},{1,0},{2,3},{3,2},{4,5},{5,4},{6,7},{7,6},{8,9},{9,8},{10,11... | collective-permute-start | bytes 884744 | tf_op jit(solution)/shard_map/ppermute | solution.py:646
  9.4 19.5 %collective-permute-start = (bf16[128,1152]{1,0:T(8,128)(2,1)S(1)}, bf16[128,1152]{1,0:T(8,128)(2,1)S(1)}, u32[]{:S(2)}, u32[]{:S(2)}) collective-permute-start(bf16[128,1152]{1,0:T(8,128)(2,1)S(1)} %get-tuple-element.23), channel_id=1, source_target_pairs={{0,1},{1,0},{2,3},{3,2},{4,5},{5,4},{6,7},{7,6},{8,9},{9,8},{10,11... | collective-permute-start | bytes 884744 | tf_op jit(solution)/shard_map/ppermute | solution.py:646
  15.6 4.7 %collective-permute-start.5 = (bf16[32,1536]{1,0:T(8,128)(2,1)S(1)}, bf16[32,1536]{1,0:T(8,128)(2,1)S(1)}, u32[]{:S(2)}, u32[]{:S(2)}) collective-permute-start(bf16[32,1536]{1,0:T(8,128)(2,1)S(1)} %get-tuple-element.37.mine_ref), channel_id=1, source_target_pairs={{0,8},{8,0},{16,24},{24,16},{1,9},{9,1},{17,25},{25,17},{2,10},{10... | collective-permute-start | bytes 294920 | tf_op jit(solution)/shard_map/ppermute | solution.py:583
  17.2 5.7 %copy-start = (bf16[1,1,128,2304]{3,2,1,0:T(8,128)(2,1)S(1)}, bf16[1,1,128,2304]{3,2,1,0:T(8,128)(2,1)}, u32[]{:S(2)}) copy-start(bf16[1,1,128,2304]{3,2,1,0:T(8,128)(2,1)} %param.6) | copy-start | bytes 1769476
  20.3 7.1 %collective-permute-start.6 = (bf16[32,1536]{1,0:T(8,128)(2,1)S(1)}, bf16[32,1536]{1,0:T(8,128)(2,1)S(1)}, u32[]{:S(2)}, u32[]{:S(2)}) collective-permute-start(bf16[32,1536]{1,0:T(8,128)(2,1)S(1)} %add.8.mine_ref), channel_id=1, source_target_pairs={{0,16},{8,24},{16,0},{24,8},{1,17},{9,25},{17,1},{25,9},{2,18},{10... | collective-permute-start | bytes 294920 | tf_op jit(solution)/shard_map/ppermute | solution.py:583
  27.4 4.7 %collective-permute-start.7 = (bf16[32,1536]{1,0:T(8,128)(2,1)S(1)}, bf16[32,1536]{1,0:T(8,128)(2,1)S(1)}, u32[]{:S(2)}, u32[]{:S(2)}) collective-permute-start(bf16[32,1536]{1,0:T(8,128)(2,1)S(1)} %add.9.mine_ref), channel_id=1, source_target_pairs={{0,1},{1,0},{2,3},{3,2},{4,5},{5,4},{6,7},{7,6},{8,9},{9,8},{10,11... | collective-permute-start | bytes 294920 | tf_op jit(solution)/shard_map/ppermute | solution.py:583

commit v4 on v3

--- a/solution.py
+++ b/solution.py
@@ -251,7 +251,8 @@
     return [pltpu.with_memory_space_constraint(array, pltpu.HBM) for array in arrays]
 
 
-def cut_edges_kernel(start_ref, gated_ref, sent_ref, edge_ref, cot_ref, sems):
+def cut_kernel(start_ref, gated_ref, sent_ref, mixed_ref, edge_ref, cot_ref, *rest):
+    *part_refs, sems = rest
     rows, embed = gated_ref.shape[0], cot_ref.shape[1]
     edge = pl.ds(pl.multiple_of(start_ref[0], 16), EDGE)
     slim = pl.ds(pl.multiple_of(start_ref[1], 16), SLIM)
@@ -262,46 +263,28 @@
     for block in range(sent_ref.shape[1] // embed - 1):
         source = sent_ref.at[slim, pl.ds((block + 1) * embed, embed)]
         copies.append((source, cot_ref.at[pl.ds(rows + block * SLIM, SLIM)]))
+    for group, part_ref in enumerate(part_refs):
+        for block in range(3):
+            source = mixed_ref.at[:, pl.ds(block * embed + group * SPAN, SPAN)]
+            copies.append((source, part_ref.at[:, pl.ds(block * SPAN, SPAN)]))
     copy_all(copies, sems)()
 
 
-def cut_edges(gated, sent, last):
+def cut(gated, sent, mixed, last):
     rows, channels = gated.shape
-    embed = HEADS * HD
+    embed, groups = HEADS * HD, HEADS // GROUP
     blocks = channels // embed
     starts = jnp.stack([last * (rows - EDGE), last * (rows - SLIM)])
     return pl.pallas_call(
-        cut_edges_kernel,
-        in_specs=[SCALARS] + [MEMORY] * 2,
-        out_specs=[WHOLE] * 2,
-        out_shape=[shaped(EDGE, channels), shaped(rows + blocks * SLIM, embed)],
-        scratch_shapes=[pltpu.SemaphoreType.DMA((2 + blocks,))],
+        cut_kernel,
+        in_specs=[SCALARS] + [MEMORY] * 3,
+        out_specs=[WHOLE] * (2 + groups),
+        out_shape=[shaped(EDGE, channels), shaped(rows + blocks * SLIM, embed)]
+        + [shaped(rows, 3 * SPAN)] * groups,
+        scratch_shapes=[pltpu.SemaphoreType.DMA((2 + blocks + 3 * groups,))],
         compiler_params=PARAMS,
-        name="cut_edges",
-    )(starts, *in_hbm(gated, sent))
-
-
-def cut_heads_kernel(mixed_ref, *rest):
-    *part_refs, sems = rest
-    copies = []
-    for group, part_ref in enumerate(part_refs):
-        for block in range(3):
-            source = mixed_ref.at[:, pl.ds(block * HEADS * HD + group * SPAN, SPAN)]
-            copies.append((source, part_ref.at[:, pl.ds(block * SPAN, SPAN)]))
-    copy_all(copies, sems)()
-
-
-def cut_heads(mixed):
-    groups = HEADS // GROUP
-    return pl.pallas_call(
-        cut_heads_kernel,
-        in_specs=[MEMORY],
-        out_specs=[WHOLE] * groups,
-        out_shape=[shaped(mixed.shape[0], 3 * SPAN)] * groups,
-        scratch_shapes=[pltpu.SemaphoreType.DMA((3 * groups,))],
-        compiler_params=PARAMS,
-        name="cut_heads",
-    )(*in_hbm(mixed))
+        name="cut",
+    )(starts, *in_hbm(gated, sent, mixed))
 
 
 def attend_group(group, place_ref, length_ref, mine_ref, peer_ref, cot_ref, cot_peer_ref, bias,
@@ -369,7 +352,7 @@
             grad_part[block, :, lanes] = totals[block + 1][index].astype(BF16)
 
 def first_group_kernel(
-    place_ref, length_ref, mine_ref, peer_ref, cot_ref, cot_peer_ref, depth_ref, gated_ref,
+    depth_ref, gated_ref, place_ref, length_ref, mine_ref, peer_ref, cot_ref, cot_peer_ref,
     depth_out, gated_out, out_part, grad_part, bias, sems,
 ):
     wait = copy_all([(depth_ref, depth_out), (gated_ref, gated_out)], sems)
@@ -389,7 +372,7 @@
 
 
 def second_group_kernel(
-    place_ref, length_ref, mine_ref, peer_ref, cot_ref, cot_peer_ref, out_first, grad_first,
+    out_first, grad_first, place_ref, length_ref, mine_ref, peer_ref, cot_ref, cot_peer_ref,
     out_ref, grad_ref, out_part, grad_part, bias, sems,
 ):
     wait = write_group(0, out_first, grad_first, out_ref, grad_ref, sems)
@@ -416,7 +399,7 @@
         scratch += [pltpu.SemaphoreType.DMA((2, 4))]
     return pl.pallas_call(
         (first_group_kernel, second_group_kernel)[group],
-        in_specs=[SCALARS] * 2 + [WHOLE] * 6,
+        in_specs=[WHOLE] * 2 + [SCALARS] * 2 + [WHOLE] * 4,
         out_specs=out_specs,
         out_shape=out_shape,
         scratch_shapes=scratch,
@@ -427,7 +410,7 @@
         ),
         compiler_params=pltpu.CompilerParams(vmem_limit_bytes=4 * LIMIT),
         name=f"attention_{group}",
-    )(place, length, mine, peer, arriving, cot_peer, *earlier)
+    )(*earlier, place, length, mine, peer, arriving, cot_peer)
 
 
 def head_pass(queries, grad_out, keys_in, values_in, valid_keys):
@@ -639,8 +622,7 @@
     place = jnp.stack([first, (1 - me) * rows, jnp.int32(frames)])
     arriving = lax.ppermute(sent, "pipe", [(i, (i - 1) % sections) for i in range(sections)])
     if devices == 2:
-        edge, piece = cut_edges(gated, sent, 1 - me)
-        parts = cut_heads(mixed)
+        edge, piece, *parts = cut(gated, sent, mixed, 1 - me)
         gated_low = gated_high = lax.ppermute(edge, "ctx", SWAP)
         cot_low = cot_high = cot_peer = lax.ppermute(piece, ("pipe", "ctx"), route(SWAP, 1))
         peers = [lax.ppermute(part, "ctx", SWAP) for part in parts]

time: 33 us -> 31.5 us (0.955)
  waiting for transfers between devices: 2.42 us -> 1.31 us
  Pallas kernels: 16.5 us -> 15.6 us
  starting transfers between devices: 12.3 us -> 12.9 us
    ppermute x3, waiting for transfers between devices: 2.41 us -> 0.73 us  [exchanged(): lax.ppermute(value, axis, [(i, i ^ step) for i in range(lax.axis_size(axi...]
    pallas_call x2 -> x1, Pallas kernels: 2.74 us -> 1.89 us  [cut(): pl.pallas_call(cut_kernel, in_specs=[SCALARS] + [MEMORY] * 3, out_specs=[...]
    ppermute x3, starting transfers between devices: 5.88 us -> 6.49 us  [exchanged(): lax.ppermute(value, axis, [(i, i ^ step) for i in range(lax.axis_size(axi...]
    ppermute x1, waiting for transfers between devices: 0.01 us -> 0.46 us  [local(): lax.ppermute(piece, ('pipe', 'ctx'), route(SWAP, 1))]
  transfers between devices with their start and end apart: 8 -> 8, of which waited for: 3 -> 3; matrix products, arithmetic and copies ran while one was open for 0% -> 0% of each run, Pallas kernels for 48% -> 47%
where the time goes in v4:
time: 31.5 us; the launch traced here: 31.4 us
  Pallas kernels  15.6 us (50%)
  starting transfers between devices  12.9 us (41%)
  between operations  1.4 us (4%)
  waiting for transfers between devices  1.31 us (4%)
    ppermute x3, starting transfers between devices, exchanged(): lax.ppermute(value, axis, [(i, i ^ step) for i in range(lax.axis_size(axi...  6.49 us
    pallas_call x2, Pallas kernels, attention_call(): pl.pallas_call((first_group_kernel, second_group_kernel)[group], in_specs...  5.23 us
    pallas_call x1, Pallas kernels, conv_back(): pl.pallas_call(back_kernel, in_specs=[SCALARS] * 2 + [WHOLE] * 6, out_spe...  2.86 us
    pallas_call x1, Pallas kernels, conv_pre(): pl.pallas_call(pre_kernel, in_specs=[SCALARS] * 2 + [WHOLE] * 5, out_spec...  2.61 us
    ppermute x1, starting transfers between devices, local(): lax.ppermute(sent, 'pipe', [(i, (i - 1) % sections) for i in range(sectio...  2.43 us
    pallas_call x1, Pallas kernels, conv_sums(): pl.pallas_call(sums_kernel, in_specs=[WHOLE] * 3, out_specs=[WHOLE] * 2,...  2.25 us
    ppermute x2, starting transfers between devices, local(): peers = [lax.ppermute(part, 'ctx', SWAP) for part in parts]  2.03 us
    pallas_call x1, Pallas kernels, cut(): pl.pallas_call(cut_kernel, in_specs=[SCALARS] + [MEMORY] * 3, out_specs=[...  1.89 us
  transfers between devices with their start and end apart: 8, of which 3 were waited for; matrix products, arithmetic and copies ran while one was open for 0% of the time, Pallas kernels for 47%

profile of v4, /device:TPU:0, one launch (start us, length us, event | category | flops | bytes accessed | tf_op | source)
XLA Modules:
  0.0 31.4 jit_solution(8279228604695535388)
XLA Ops:
  0.6 0.0 copy-start.1
  0.7 2.4 %collective-permute-start.1 = (bf16[128,2304]{1,0:T(8,128)(2,1)}, bf16[128,2304]{1,0:T(8,128)(2,1)S(1)}, u32[]{:S(2)}, u32[]{:S(2)}) collective-permute-start(bf16[128,2304]{1,0:T(8,128)(2,1)} %bitcast.20), channel_id=1, source_target_pairs={{0,6},{2,0},{4,2},{6,4},{1,7},{3,1},{5,3},{7,5},{8,14},{10,8},{12,... | collective-permute-start | bytes 1769480 | tf_op jit(solution)/shard_map/ppermute | solution.py:623
  3.1 0.1 pad_add_fusion.1.start_ref
  3.2 1.9 %cut.1 = (bf16[32,1536]{1,0:T(8,128)(2,1)S(1)}, bf16[160,768]{1,0:T(8,128)(2,1)S(1)}, bf16[128,1152]{1,0:T(8,128)(2,1)S(1)}, bf16[128,1152]{1,0:T(8,128)(2,1)S(1)}) custom-call(s32[2]{0:T(128)S(1)} %pad_add_fusion.1.start_ref, bf16[128,1536]{1,0:T(8,128)(2,1)} %bitcast.16, bf16[128,2304]{1,0:T(8,128)(2,1)} %bitcast.21, bf16[128,2304]{1,0:T(8,128)(2,1)} %bitcast.13), custom_call_target="tpu_custom_call" | custom-call | tf_op jit(solution)/shard_map/cut/pallas_call | solution.py:278
  5.1 1.6 %collective-permute-start = (bf16[32,1536]{1,0:T(8,128)(2,1)S(1)}, bf16[32,1536]{1,0:T(8,128)(2,1)S(1)}, u32[]{:S(2)}, u32[]{:S(2)}) collective-permute-start(bf16[32,1536]{1,0:T(8,128)(2,1)S(1)} %get-tuple-element.23), channel_id=1, source_target_pairs={{0,1},{1,0},{2,3},{3,2},{4,5},{5,4},{6,7},{7,6},{8,9},{9,8},{10,11... | collective-permute-start | bytes 294920 | tf_op jit(solution)/shard_map/ppermute | solution.py:626
  6.7 0.3 %collective-permute-start.2 = (bf16[160,768]{1,0:T(8,128)(2,1)S(1)}, bf16[160,768]{1,0:T(8,128)(2,1)S(1)}, u32[]{:S(2)}, u32[]{:S(2)}) collective-permute-start(bf16[160,768]{1,0:T(8,128)(2,1)S(1)} %get-tuple-element.28), channel_id=1, source_target_pairs={{0,7},{1,6},{2,1},{3,0},{4,3},{5,2},{6,5},{7,4},{8,15},{9,14},{10,... | collective-permute-start | bytes 737288 | tf_op jit(solution)/shard_map/ppermute | solution.py:627
  7.0 1.5 %collective-permute-start.3 = (bf16[128,1152]{1,0:T(8,128)(2,1)S(1)}, bf16[128,1152]{1,0:T(8,128)(2,1)S(1)}, u32[]{:S(2)}, u32[]{:S(2)}) collective-permute-start(bf16[128,1152]{1,0:T(8,128)(2,1)S(1)} %get-tuple-element.29), channel_id=1, source_target_pairs={{0,1},{1,0},{2,3},{3,2},{4,5},{5,4},{6,7},{7,6},{8,9},{9,8},{10,11... | collective-permute-start | bytes 884744 | tf_op jit(solution)/shard_map/ppermute | solution.py:628
  8.5 0.5 %collective-permute-start.4 = (bf16[128,1152]{1,0:T(8,128)(2,1)S(1)}, bf16[128,1152]{1,0:T(8,128)(2,1)S(1)}, u32[]{:S(2)}, u32[]{:S(2)}) collective-permute-start(bf16[128,1152]{1,0:T(8,128)(2,1)S(1)} %get-tuple-element.32), channel_id=1, source_target_pairs={{0,1},{1,0},{2,3},{3,2},{4,5},{5,4},{6,7},{7,6},{8,9},{9,8},{10,11... | collective-permute-start | bytes 884744 | tf_op jit(solution)/shard_map/ppermute | solution.py:628
  9.0 0.1 pad_add_fusion.place_ref
  9.7 0.1 collective-permute-done.gated_low.gated_high
  9.9 2.6 %conv_pre.1 = (bf16[128,1536]{1,0:T(8,128)(2,1)S(1)}, f32[12,192,128]{2,1,0:T(8,128)S(1)}, f32[12,128,128]{2,1,0:T(8,128)S(1)}) custom-call(s32[3]{0:T(128)S(1)} %pad_add_fusion.place_ref, s32[1,1]{1,0:T(1,128)S(6)} %copy.12.length_ref, bf16[128,1536]{1,0:T(8,128)(2,1)S(1)} %bitcast.17, bf16[32,1536]{1,0:T(8,128)(2,1)S(1)} %collective-permute-done.gated_low.gated_high, ...), custom_call_target="tpu_custom_call" | custom-call | flops 6241124352 | bytes 1572864 | tf_op jit(solution)/shard_map/conv_pre/pallas_call | solution.py:189
  12.5 0.0 collective-permute-done.1.cot_ref
  12.5 2.2 %conv_sums.1 = (f32[12,128,128]{2,1,0:T(8,128)S(1)}, bf16[32,1536]{1,0:T(8,128)(2,1)S(1)}) custom-call(f32[12,192,128]{2,1,0:T(8,128)S(1)} %get-tuple-element.25.source, f32[12,128,128]{2,1,0:T(8,128)S(1)} %get-tuple-element.26.slopes, bf16[128,2304]{1,0:T(8,128)(2,1)S(1)} %collective-permute-done.1.cot_ref), custom_call_target="tpu_custom_call" | custom-call | flops 6241124352 | bytes 2359296 | tf_op jit(solution)/shard_map/conv_sums/pallas_call | solution.py:206
  14.8 1.6 %collective-permute-start.5 = (bf16[32,1536]{1,0:T(8,128)(2,1)S(1)}, bf16[32,1536]{1,0:T(8,128)(2,1)S(1)}, u32[]{:S(2)}, u32[]{:S(2)}) collective-permute-start(bf16[32,1536]{1,0:T(8,128)(2,1)S(1)} %get-tuple-element.37.mine_ref), channel_id=1, source_target_pairs={{0,8},{8,0},{16,24},{24,16},{1,9},{9,1},{17,25},{25,17},{2,10},{10... | collective-permute-start | bytes 294920 | tf_op jit(solution)/shard_map/ppermute | solution.py:566
  16.4 0.5 %collective-permute-done.2.cot_low.cot_high.cot_peer_ref = bf16[160,768]{1,0:T(8,128)(2,1)S(1)} collective-permute-done((bf16[160,768]{1,0:T(8,128)(2,1)S(1)}, bf16[160,768]{1,0:T(8,128)(2,1)S(1)}, u32[]{:S(2)}, u32[]{:S(2)}) %collective-permute-start.2) | collective-permute-done | bytes 245792 | tf_op jit(solution)/shard_map/ppermute | solution.py:627
  16.9 2.9 %conv_back.1.gated_ref = bf16[128,1536]{1,0:T(8,128)(2,1)S(1)} custom-call(s32[3]{0:T(128)S(1)} %pad_add_fusion.place_ref, s32[1,1]{1,0:T(1,128)S(6)} %copy.12.length_ref, f32[12,192,128]{2,1,0:T(8,128)S(1)} %get-tuple-element.25.source, f32[12,128,128]{2,1,0:T(8,128)S(1)} %get-tuple-element.27.grads, ...), custom_call_target="tpu_custom_call" | custom-call | flops 6241124352 | bytes 1179648 | tf_op jit(solution)/shard_map/conv_back/pallas_call | solution.py:221
  19.7 0.0 collective-permute-done.5.other_ref
  19.8 2.7 %collective-permute-start.6 = (bf16[32,1536]{1,0:T(8,128)(2,1)S(1)}, bf16[32,1536]{1,0:T(8,128)(2,1)S(1)}, u32[]{:S(2)}, u32[]{:S(2)}) collective-permute-start(bf16[32,1536]{1,0:T(8,128)(2,1)S(1)} %add.8.mine_ref), channel_id=1, source_target_pairs={{0,16},{8,24},{16,0},{24,8},{1,17},{9,25},{17,1},{25,9},{2,18},{10... | collective-permute-start | bytes 294920 | tf_op jit(solution)/shard_map/ppermute | solution.py:566
  22.4 2.2 %attention_0.1 = (bf16[128,1536]{1,0:T(8,128)(2,1)}, bf16[128,1536]{1,0:T(8,128)(2,1)}, bf16[128,384]{1,0:T(8,128)(2,1)S(1)}, bf16[3,128,384]{2,1,0:T(8,128)(2,1)S(1)}) custom-call(bf16[128,1536]{1,0:T(8,128)(2,1)S(1)} %get-tuple-element.24.depth_ref, bf16[128,1536]{1,0:T(8,128)(2,1)S(1)} %conv_back.1.gated_ref, s32[3]{0:T(128)S(1)} %pad_add_fusion.place_ref, ...), custom_call_target="tpu_custom_call" | custom-call | flops 2415919104 | bytes 884736 | tf_op jit(solution)/shard_map/attention_0/pallas_call | solution.py:400
  24.7 0.7 %collective-permute-done.6.other_ref = bf16[32,1536]{1,0:T(8,128)(2,1)S(1)} collective-permute-done((bf16[32,1536]{1,0:T(8,128)(2,1)S(1)}, bf16[32,1536]{1,0:T(8,128)(2,1)S(1)}, u32[]{:S(2)}, u32[]{:S(2)}) %collective-permute-start.6) | collective-permute-done | bytes 98336 | tf_op jit(solution)/shard_map/ppermute | solution.py:566
  25.4 2.2 %collective-permute-start.7 = (bf16[32,1536]{1,0:T(8,128)(2,1)S(1)}, bf16[32,1536]{1,0:T(8,128)(2,1)S(1)}, u32[]{:S(2)}, u32[]{:S(2)}) collective-permute-start(bf16[32,1536]{1,0:T(8,128)(2,1)S(1)} %add.9.mine_ref), channel_id=1, source_target_pairs={{0,1},{1,0},{2,3},{3,2},{4,5},{5,4},{6,7},{7,6},{8,9},{9,8},{10,11... | collective-permute-start | bytes 294920 | tf_op jit(solution)/shard_map/ppermute | solution.py:566
  27.6 0.0 collective-permute-done.4.peer_ref
  27.6 3.0 %attention_1.1 = (bf16[128,768]{1,0:T(8,128)(2,1)}, bf16[128,2304]{1,0:T(8,128)(2,1)}) custom-call(bf16[128,384]{1,0:T(8,128)(2,1)S(1)} %get-tuple-element.30.out_first, bf16[3,128,384]{2,1,0:T(8,128)(2,1)S(1)} %get-tuple-element.31.grad_first, s32[3]{0:T(128)S(1)} %pad_add_fusion.place_ref, s32[1,1]{1,0:T(1,128)S(6)} %copy.12.length_ref, ...), custom_call_target="tpu_custom_call" | custom-call | flops 2415919104 | bytes 884736 | tf_op jit(solution)/shard_map/attention_1/pallas_call | solution.py:400
  30.6 0.7 %last_sum.1 = (f32[31,1,1536]{2,1,0:T(1,128)}, f32[1,1536]{1,0:T(1,128)}) custom-call(bf16[32,1536]{1,0:T(8,128)(2,1)S(1)} %add.9.mine_ref, bf16[32,1536]{1,0:T(8,128)(2,1)S(1)} %collective-permute-done.7.other_ref), custom_call_target="tpu_custom_call" | custom-call | tf_op jit(solution)/shard_map/last_sum/pallas_call | solution.py:582
  (11 shorter events, 0.1 us)
Async XLA Ops:
  0.6 9.2 %copy-start.1 = (bf16[1,1,128,1536]{3,2,1,0:T(8,128)(2,1)S(1)}, bf16[1,1,128,1536]{3,2,1,0:T(8,128)(2,1)}, u32[]{:S(2)}) copy-start(bf16[1,1,128,1536]{3,2,1,0:T(8,128)(2,1)} %param.7) | copy-start | bytes 1179652
  0.6 9.2 %copy-start.3 = (f32[1,1536]{1,0:T(1,128)S(1)}, f32[1,1536]{1,0:T(1,128)}, u32[]{:S(2)}) copy-start(f32[1,1536]{1,0:T(1,128)} %bias_ref.3) | copy-start | bytes 18436
  0.7 9.2 %copy-start.2 = (f32[1,31,1536]{2,0,1:T(1,128)S(1)}, f32[1,31,1536]{2,0,1:T(1,128)}, u32[]{:S(2)}) copy-start(f32[1,31,1536]{2,0,1:T(1,128)} %param.10) | copy-start | bytes 571396
  0.7 11.8 %collective-permute-start.1 = (bf16[128,2304]{1,0:T(8,128)(2,1)}, bf16[128,2304]{1,0:T(8,128)(2,1)S(1)}, u32[]{:S(2)}, u32[]{:S(2)}) collective-permute-start(bf16[128,2304]{1,0:T(8,128)(2,1)} %bitcast.20), channel_id=1, source_target_pairs={{0,6},{2,0},{4,2},{6,4},{1,7},{3,1},{5,3},{7,5},{8,14},{10,8},{12,... | collective-permute-start | bytes 1769480 | tf_op jit(solution)/shard_map/ppermute | solution.py:623
  5.1 4.8 %collective-permute-start = (bf16[32,1536]{1,0:T(8,128)(2,1)S(1)}, bf16[32,1536]{1,0:T(8,128)(2,1)S(1)}, u32[]{:S(2)}, u32[]{:S(2)}) collective-permute-start(bf16[32,1536]{1,0:T(8,128)(2,1)S(1)} %get-tuple-element.23), channel_id=1, source_target_pairs={{0,1},{1,0},{2,3},{3,2},{4,5},{5,4},{6,7},{7,6},{8,9},{9,8},{10,11... | collective-permute-start | bytes 294920 | tf_op jit(solution)/shard_map/ppermute | solution.py:626
  6.7 10.2 %collective-permute-start.2 = (bf16[160,768]{1,0:T(8,128)(2,1)S(1)}, bf16[160,768]{1,0:T(8,128)(2,1)S(1)}, u32[]{:S(2)}, u32[]{:S(2)}) collective-permute-start(bf16[160,768]{1,0:T(8,128)(2,1)S(1)} %get-tuple-element.28), channel_id=1, source_target_pairs={{0,7},{1,6},{2,1},{3,0},{4,3},{5,2},{6,5},{7,4},{8,15},{9,14},{10,... | collective-permute-start | bytes 737288 | tf_op jit(solution)/shard_map/ppermute | solution.py:627
  7.0 15.4 %collective-permute-start.3 = (bf16[128,1152]{1,0:T(8,128)(2,1)S(1)}, bf16[128,1152]{1,0:T(8,128)(2,1)S(1)}, u32[]{:S(2)}, u32[]{:S(2)}) collective-permute-start(bf16[128,1152]{1,0:T(8,128)(2,1)S(1)} %get-tuple-element.29), channel_id=1, source_target_pairs={{0,1},{1,0},{2,3},{3,2},{4,5},{5,4},{6,7},{7,6},{8,9},{9,8},{10,11... | collective-permute-start | bytes 884744 | tf_op jit(solution)/shard_map/ppermute | solution.py:628
  8.5 19.1 %collective-permute-start.4 = (bf16[128,1152]{1,0:T(8,128)(2,1)S(1)}, bf16[128,1152]{1,0:T(8,128)(2,1)S(1)}, u32[]{:S(2)}, u32[]{:S(2)}) collective-permute-start(bf16[128,1152]{1,0:T(8,128)(2,1)S(1)} %get-tuple-element.32), channel_id=1, source_target_pairs={{0,1},{1,0},{2,3},{3,2},{4,5},{5,4},{6,7},{7,6},{8,9},{9,8},{10,11... | collective-permute-start | bytes 884744 | tf_op jit(solution)/shard_map/ppermute | solution.py:628
  14.8 5.0 %collective-permute-start.5 = (bf16[32,1536]{1,0:T(8,128)(2,1)S(1)}, bf16[32,1536]{1,0:T(8,128)(2,1)S(1)}, u32[]{:S(2)}, u32[]{:S(2)}) collective-permute-start(bf16[32,1536]{1,0:T(8,128)(2,1)S(1)} %get-tuple-element.37.mine_ref), channel_id=1, source_target_pairs={{0,8},{8,0},{16,24},{24,16},{1,9},{9,1},{17,25},{25,17},{2,10},{10... | collective-permute-start | bytes 294920 | tf_op jit(solution)/shard_map/ppermute | solution.py:566
  16.9 5.6 %copy-start = (bf16[1,1,128,2304]{3,2,1,0:T(8,128)(2,1)S(1)}, bf16[1,1,128,2304]{3,2,1,0:T(8,128)(2,1)}, u32[]{:S(2)}) copy-start(bf16[1,1,128,2304]{3,2,1,0:T(8,128)(2,1)} %param.6) | copy-start | bytes 1769476
  19.8 5.6 %collective-permute-start.6 = (bf16[32,1536]{1,0:T(8,128)(2,1)S(1)}, bf16[32,1536]{1,0:T(8,128)(2,1)S(1)}, u32[]{:S(2)}, u32[]{:S(2)}) collective-permute-start(bf16[32,1536]{1,0:T(8,128)(2,1)S(1)} %add.8.mine_ref), channel_id=1, source_target_pairs={{0,16},{8,24},{16,0},{24,8},{1,17},{9,25},{17,1},{25,9},{2,18},{10... | collective-permute-start | bytes 294920 | tf_op jit(solution)/shard_map/ppermute | solution.py:566
  25.4 5.2 %collective-permute-start.7 = (bf16[32,1536]{1,0:T(8,128)(2,1)S(1)}, bf16[32,1536]{1,0:T(8,128)(2,1)S(1)}, u32[]{:S(2)}, u32[]{:S(2)}) collective-permute-start(bf16[32,1536]{1,0:T(8,128)(2,1)S(1)} %add.9.mine_ref), channel_id=1, source_target_pairs={{0,1},{1,0},{2,3},{3,2},{4,5},{5,4},{6,7},{7,6},{8,9},{9,8},{10,11... | collective-permute-start | bytes 294920 | tf_op jit(solution)/shard_map/ppermute | solution.py:566

commit v5 on v4

--- a/solution.py
+++ b/solution.py
@@ -60,10 +60,10 @@
     slopes, valid,
 ):
     rows, width = gated_ref.shape
-    frame = place_ref[0] - EDGE + lax.broadcasted_iota(jnp.int32, valid.shape, 0)
+    frame = place_ref[0 : 1, :] - EDGE + lax.broadcasted_iota(jnp.int32, valid.shape, 0)
     valid[...] = ((frame >= 0) & (frame < length_ref[0, 0])).astype(F32)
 
-    @pl.loop(0, width // LANES)
+    @pl.loop(0, width // LANES, unroll=2)
     def _(column):
         lanes = pl.ds(pl.multiple_of(column * LANES, LANES), LANES)
 
@@ -94,7 +94,7 @@
     columns, rows, _ = slopes.shape
     embed = cot_ref.shape[1] - columns * LANES
 
-    @pl.loop(0, columns)
+    @pl.loop(0, columns, unroll=2)
     def _(column):
         lanes = pl.ds(pl.multiple_of(column * LANES, LANES), LANES)
         shifted = pl.ds(pl.multiple_of(embed + column * LANES, LANES), LANES)
@@ -123,13 +123,13 @@
     rows, width = out_ref.shape
     across = cot_low.shape[1] // LANES
     base = cot_low.shape[0] - SLIM * (width // LANES // across)
-    first, frames = place_ref[0], place_ref[2]
+    first, frames = place_ref[0 : 1, :], place_ref[2 : 3, :]
     frame = first + lax.broadcasted_iota(jnp.int32, valid.shape, 0)
     valid[...] = (frame < length_ref[0, 0]).astype(F32)
     low_kept = (first > 0).astype(F32)
     high_kept = (first + rows < frames).astype(F32)
 
-    @pl.loop(0, width // LANES)
+    @pl.loop(0, width // LANES, unroll=2)
     def _(column):
         lanes = pl.ds(pl.multiple_of(column * LANES, LANES), LANES)
         for at in range(0, rows, 8):
@@ -188,7 +188,7 @@
     rows, channels = gated.shape
     return pl.pallas_call(
         pre_kernel,
-        in_specs=[SCALARS] * 2 + [WHOLE] * 5,
+        in_specs=[WHOLE, SCALARS] + [WHOLE] * 5,
         out_specs=[WHOLE] * 3,
         out_shape=[
             shaped(rows, channels), stacked(channels, rows + 2 * EDGE), stacked(channels, rows)
@@ -220,7 +220,7 @@
     channels = columns * LANES
     return pl.pallas_call(
         back_kernel,
-        in_specs=[SCALARS] * 2 + [WHOLE] * 6,
+        in_specs=[WHOLE, SCALARS] + [WHOLE] * 6,
         out_specs=WHOLE,
         out_shape=shaped(rows, channels),
         scratch_shapes=[
@@ -293,7 +293,7 @@
     embed = HEADS * HD
     base = group * SPAN
     row = lax.broadcasted_iota(jnp.int32, bias.shape, 0)
-    frame = jnp.where(row < rows, row + place_ref[0], row - rows + place_ref[1])
+    frame = jnp.where(row < rows, row + place_ref[0 : 1, :], row - rows + place_ref[1 : 2, :])
     bias[...] = jnp.where(frame < length_ref[0, 0], 0.0, -1e30)
     across = (((1,), (1,)), ((), ()))
     downward = (((0,), (0,)), ((), ()))
@@ -399,7 +399,7 @@
         scratch += [pltpu.SemaphoreType.DMA((2, 4))]
     return pl.pallas_call(
         (first_group_kernel, second_group_kernel)[group],
-        in_specs=[WHOLE] * 2 + [SCALARS] * 2 + [WHOLE] * 4,
+        in_specs=[WHOLE] * 3 + [SCALARS] + [WHOLE] * 4,
         out_specs=out_specs,
         out_shape=out_shape,
         scratch_shapes=scratch,
@@ -619,7 +619,8 @@
     rows = mixed.shape[0]
     frames = rows * devices
     first = me * rows
-    place = jnp.stack([first, (1 - me) * rows, jnp.int32(frames)])
+    row = lax.broadcasted_iota(jnp.int32, (8, LANES), 0)
+    place = jnp.where(row == 0, first, jnp.where(row == 1, (1 - me) * rows, frames))
     arriving = lax.ppermute(sent, "pipe", [(i, (i - 1) % sections) for i in range(sections)])
     if devices == 2:
         edge, piece, *parts = cut(gated, sent, mixed, 1 - me)

time: 31.5 us -> 30.7 us (0.975)
  Pallas kernels: 15.6 us -> 13.5 us
  waiting for transfers between devices: 1.31 us -> 2.73 us
    pallas_call x2, Pallas kernels: 5.23 us -> 4.15 us  [attention_call(): pl.pallas_call((first_group_kernel, second_group_kernel)[group], in_specs...]
    pallas_call x2, Pallas kernels: 5.47 us -> 4.39 us  [the longest x1 2.36 us: conv_back(): pl.pallas_call(back_kernel, in_specs=[WHOLE, SCALARS] + [WHOLE] * 6, out_...]
    ppermute x3, waiting for transfers between devices: 0.73 us -> 1.56 us  [exchanged(): lax.ppermute(value, axis, [(i, i ^ step) for i in range(lax.axis_size(axi...]
    ppermute x1, waiting for transfers between devices: 0.46 us -> 1.06 us  [local(): lax.ppermute(piece, ('pipe', 'ctx'), route(SWAP, 1))]
  transfers between devices with their start and end apart: 8 -> 8, of which waited for: 3 -> 4; matrix products, arithmetic and copies ran while one was open for 0% -> 1% of each run, Pallas kernels for 47% -> 42%
where the time goes in v5:
time: 30.7 us; the launch traced here: 30.5 us
  Pallas kernels  13.5 us (44%)
  starting transfers between devices  12.8 us (42%)
  waiting for transfers between devices  2.73 us (9%)
  between operations  1.39 us (5%)
    ppermute x3, starting transfers between devices, exchanged(): lax.ppermute(value, axis, [(i, i ^ step) for i in range(lax.axis_size(axi...  6.41 us
    pallas_call x2, Pallas kernels, attention_call(): pl.pallas_call((first_group_kernel, second_group_kernel)[group], in_specs...  4.15 us
    ppermute x1, starting transfers between devices, local(): lax.ppermute(sent, 'pipe', [(i, (i - 1) % sections) for i in range(sectio...  2.43 us
    pallas_call x1, Pallas kernels, conv_back(): pl.pallas_call(back_kernel, in_specs=[WHOLE, SCALARS] + [WHOLE] * 6, out_...  2.36 us
    pallas_call x1, Pallas kernels, conv_sums(): pl.pallas_call(sums_kernel, in_specs=[WHOLE] * 3, out_specs=[WHOLE] * 2,...  2.23 us
    pallas_call x1, Pallas kernels, conv_pre(): pl.pallas_call(pre_kernel, in_specs=[WHOLE, SCALARS] + [WHOLE] * 5, out_s...  2.03 us
    ppermute x2, starting transfers between devices, local(): peers = [lax.ppermute(part, 'ctx', SWAP) for part in parts]  2.03 us
    pallas_call x1, Pallas kernels, cut(): pl.pallas_call(cut_kernel, in_specs=[SCALARS] + [MEMORY] * 3, out_specs=[...  1.89 us
  transfers between devices with their start and end apart: 8, of which 4 were waited for; matrix products, arithmetic and copies ran while one was open for 1% of the time, Pallas kernels for 42%

profile of v5, /device:TPU:0, one launch (start us, length us, event | category | flops | bytes accessed | tf_op | source)
XLA Modules:
  0.0 30.5 jit_solution(10399598366793513214)
XLA Ops:
  0.6 0.0 copy-start.1
  0.7 2.4 %collective-permute-start.1 = (bf16[128,2304]{1,0:T(8,128)(2,1)}, bf16[128,2304]{1,0:T(8,128)(2,1)S(1)}, u32[]{:S(2)}, u32[]{:S(2)}) collective-permute-start(bf16[128,2304]{1,0:T(8,128)(2,1)} %bitcast.18), channel_id=1, source_target_pairs={{0,6},{2,0},{4,2},{6,4},{1,7},{3,1},{5,3},{7,5},{8,14},{10,8},{12,... | collective-permute-start | bytes 1769480 | tf_op jit(solution)/shard_map/ppermute | solution.py:624
  3.1 0.1 pad_add_fusion.start_ref
  3.2 1.9 %cut.1 = (bf16[32,1536]{1,0:T(8,128)(2,1)S(1)}, bf16[160,768]{1,0:T(8,128)(2,1)S(1)}, bf16[128,1152]{1,0:T(8,128)(2,1)S(1)}, bf16[128,1152]{1,0:T(8,128)(2,1)S(1)}) custom-call(s32[2]{0:T(128)S(1)} %pad_add_fusion.start_ref, bf16[128,1536]{1,0:T(8,128)(2,1)} %bitcast.14, bf16[128,2304]{1,0:T(8,128)(2,1)} %bitcast.19, bf16[128,2304]{1,0:T(8,128)(2,1)} %bitcast.11), custom_call_target="tpu_custom_call" | custom-call | tf_op jit(solution)/shard_map/cut/pallas_call | solution.py:278
  5.1 1.6 %collective-permute-start = (bf16[32,1536]{1,0:T(8,128)(2,1)S(1)}, bf16[32,1536]{1,0:T(8,128)(2,1)S(1)}, u32[]{:S(2)}, u32[]{:S(2)}) collective-permute-start(bf16[32,1536]{1,0:T(8,128)(2,1)S(1)} %get-tuple-element.23), channel_id=1, source_target_pairs={{0,1},{1,0},{2,3},{3,2},{4,5},{5,4},{6,7},{7,6},{8,9},{9,8},{10,11... | collective-permute-start | bytes 294920 | tf_op jit(solution)/shard_map/ppermute | solution.py:627
  6.7 0.3 %collective-permute-start.2 = (bf16[160,768]{1,0:T(8,128)(2,1)S(1)}, bf16[160,768]{1,0:T(8,128)(2,1)S(1)}, u32[]{:S(2)}, u32[]{:S(2)}) collective-permute-start(bf16[160,768]{1,0:T(8,128)(2,1)S(1)} %get-tuple-element.28), channel_id=1, source_target_pairs={{0,7},{1,6},{2,1},{3,0},{4,3},{5,2},{6,5},{7,4},{8,15},{9,14},{10,... | collective-permute-start | bytes 737288 | tf_op jit(solution)/shard_map/ppermute | solution.py:628
  7.0 1.5 %collective-permute-start.3 = (bf16[128,1152]{1,0:T(8,128)(2,1)S(1)}, bf16[128,1152]{1,0:T(8,128)(2,1)S(1)}, u32[]{:S(2)}, u32[]{:S(2)}) collective-permute-start(bf16[128,1152]{1,0:T(8,128)(2,1)S(1)} %get-tuple-element.29), channel_id=1, source_target_pairs={{0,1},{1,0},{2,3},{3,2},{4,5},{5,4},{6,7},{7,6},{8,9},{9,8},{10,11... | collective-permute-start | bytes 884744 | tf_op jit(solution)/shard_map/ppermute | solution.py:629
  8.5 0.5 %collective-permute-start.4 = (bf16[128,1152]{1,0:T(8,128)(2,1)S(1)}, bf16[128,1152]{1,0:T(8,128)(2,1)S(1)}, u32[]{:S(2)}, u32[]{:S(2)}) collective-permute-start(bf16[128,1152]{1,0:T(8,128)(2,1)S(1)} %get-tuple-element.32), channel_id=1, source_target_pairs={{0,1},{1,0},{2,3},{3,2},{4,5},{5,4},{6,7},{7,6},{8,9},{9,8},{10,11... | collective-permute-start | bytes 884744 | tf_op jit(solution)/shard_map/ppermute | solution.py:629
  9.0 0.1 broadcast_select_fusion.place_ref
  9.8 0.1 collective-permute-done.gated_low.gated_high
  9.9 2.0 %conv_pre.1 = (bf16[128,1536]{1,0:T(8,128)(2,1)S(1)}, f32[12,192,128]{2,1,0:T(8,128)S(1)}, f32[12,128,128]{2,1,0:T(8,128)S(1)}) custom-call(s32[8,128]{1,0:T(8,128)S(1)} %broadcast_select_fusion.place_ref, s32[1,1]{1,0:T(1,128)S(6)} %copy.12.length_ref, bf16[128,1536]{1,0:T(8,128)(2,1)S(1)} %bitcast.15, ...), custom_call_target="tpu_custom_call" | custom-call | flops 6241124352 | bytes 1572864 | tf_op jit(solution)/shard_map/conv_pre/pallas_call | solution.py:189
  11.9 0.0 collective-permute-done.1.cot_ref
  11.9 2.2 %conv_sums.1 = (f32[12,128,128]{2,1,0:T(8,128)S(1)}, bf16[32,1536]{1,0:T(8,128)(2,1)S(1)}) custom-call(f32[12,192,128]{2,1,0:T(8,128)S(1)} %get-tuple-element.25.source, f32[12,128,128]{2,1,0:T(8,128)S(1)} %get-tuple-element.26.slopes, bf16[128,2304]{1,0:T(8,128)(2,1)S(1)} %collective-permute-done.1.cot_ref), custom_call_target="tpu_custom_call" | custom-call | flops 6241124352 | bytes 2359296 | tf_op jit(solution)/shard_map/conv_sums/pallas_call | solution.py:206
  14.2 1.6 %collective-permute-start.5 = (bf16[32,1536]{1,0:T(8,128)(2,1)S(1)}, bf16[32,1536]{1,0:T(8,128)(2,1)S(1)}, u32[]{:S(2)}, u32[]{:S(2)}) collective-permute-start(bf16[32,1536]{1,0:T(8,128)(2,1)S(1)} %get-tuple-element.37.mine_ref), channel_id=1, source_target_pairs={{0,8},{8,0},{16,24},{24,16},{1,9},{9,1},{17,25},{25,17},{2,10},{10... | collective-permute-start | bytes 294920 | tf_op jit(solution)/shard_map/ppermute | solution.py:566
  15.8 1.1 %collective-permute-done.2.cot_low.cot_high.cot_peer_ref = bf16[160,768]{1,0:T(8,128)(2,1)S(1)} collective-permute-done((bf16[160,768]{1,0:T(8,128)(2,1)S(1)}, bf16[160,768]{1,0:T(8,128)(2,1)S(1)}, u32[]{:S(2)}, u32[]{:S(2)}) %collective-permute-start.2) | collective-permute-done | bytes 245792 | tf_op jit(solution)/shard_map/ppermute | solution.py:628
  16.9 2.4 %conv_back.1.gated_ref = bf16[128,1536]{1,0:T(8,128)(2,1)S(1)} custom-call(s32[8,128]{1,0:T(8,128)S(1)} %broadcast_select_fusion.place_ref, s32[1,1]{1,0:T(1,128)S(6)} %copy.12.length_ref, f32[12,192,128]{2,1,0:T(8,128)S(1)} %get-tuple-element.25.source, f32[12,128,128]{2,1,0:T(8,128)S(1)} %get-tuple-element.27.grads, ...), custom_call_target="tpu_custom_call" | custom-call | flops 6241124352 | bytes 1179648 | tf_op jit(solution)/shard_map/conv_back/pallas_call | solution.py:221
  19.3 2.7 %collective-permute-start.6 = (bf16[32,1536]{1,0:T(8,128)(2,1)S(1)}, bf16[32,1536]{1,0:T(8,128)(2,1)S(1)}, u32[]{:S(2)}, u32[]{:S(2)}) collective-permute-start(bf16[32,1536]{1,0:T(8,128)(2,1)S(1)} %add.4.mine_ref), channel_id=1, source_target_pairs={{0,16},{8,24},{16,0},{24,8},{1,17},{9,25},{17,1},{25,9},{2,18},{10... | collective-permute-start | bytes 294920 | tf_op jit(solution)/shard_map/ppermute | solution.py:566
  21.9 0.0 collective-permute-done.3.peer_ref
  21.9 1.7 %attention_0.1 = (bf16[128,1536]{1,0:T(8,128)(2,1)}, bf16[128,1536]{1,0:T(8,128)(2,1)}, bf16[128,384]{1,0:T(8,128)(2,1)S(1)}, bf16[3,128,384]{2,1,0:T(8,128)(2,1)S(1)}) custom-call(bf16[128,1536]{1,0:T(8,128)(2,1)S(1)} %get-tuple-element.24.depth_ref, bf16[128,1536]{1,0:T(8,128)(2,1)S(1)} %conv_back.1.gated_ref, ...), custom_call_target="tpu_custom_call" | custom-call | flops 2415919104 | bytes 884736 | tf_op jit(solution)/shard_map/attention_0/pallas_call | solution.py:400
  23.6 1.2 %collective-permute-done.6.other_ref = bf16[32,1536]{1,0:T(8,128)(2,1)S(1)} collective-permute-done((bf16[32,1536]{1,0:T(8,128)(2,1)S(1)}, bf16[32,1536]{1,0:T(8,128)(2,1)S(1)}, u32[]{:S(2)}, u32[]{:S(2)}) %collective-permute-start.6) | collective-permute-done | bytes 98336 | tf_op jit(solution)/shard_map/ppermute | solution.py:566
  24.9 2.1 %collective-permute-start.7 = (bf16[32,1536]{1,0:T(8,128)(2,1)S(1)}, bf16[32,1536]{1,0:T(8,128)(2,1)S(1)}, u32[]{:S(2)}, u32[]{:S(2)}) collective-permute-start(bf16[32,1536]{1,0:T(8,128)(2,1)S(1)} %add.5.mine_ref), channel_id=1, source_target_pairs={{0,1},{1,0},{2,3},{3,2},{4,5},{5,4},{6,7},{7,6},{8,9},{9,8},{10,11... | collective-permute-start | bytes 294920 | tf_op jit(solution)/shard_map/ppermute | solution.py:566
  27.0 2.5 %attention_1.1 = (bf16[128,768]{1,0:T(8,128)(2,1)}, bf16[128,2304]{1,0:T(8,128)(2,1)}) custom-call(bf16[128,384]{1,0:T(8,128)(2,1)S(1)} %get-tuple-element.30.out_first, bf16[3,128,384]{2,1,0:T(8,128)(2,1)S(1)} %get-tuple-element.31.grad_first, s32[8,128]{1,0:T(8,128)S(1)} %broadcast_select_fusion.place_ref, s32[1,1]{1,0:T(1,128)S(6)} %copy.12.length_ref, ...), custom_call_target="tpu_custom_call" | custom-call | flops 2415919104 | bytes 884736 | tf_op jit(solution)/shard_map/attention_1/pallas_call | solution.py:400
  29.5 0.3 %collective-permute-done.7.other_ref = bf16[32,1536]{1,0:T(8,128)(2,1)S(1)} collective-permute-done((bf16[32,1536]{1,0:T(8,128)(2,1)S(1)}, bf16[32,1536]{1,0:T(8,128)(2,1)S(1)}, u32[]{:S(2)}, u32[]{:S(2)}) %collective-permute-start.7) | collective-permute-done | bytes 98336 | tf_op jit(solution)/shard_map/ppermute | solution.py:566
  29.8 0.7 %last_sum.1 = (f32[31,1,1536]{2,1,0:T(1,128)}, f32[1,1536]{1,0:T(1,128)}) custom-call(bf16[32,1536]{1,0:T(8,128)(2,1)S(1)} %add.5.mine_ref, bf16[32,1536]{1,0:T(8,128)(2,1)S(1)} %collective-permute-done.7.other_ref), custom_call_target="tpu_custom_call" | custom-call | tf_op jit(solution)/shard_map/last_sum/pallas_call | solution.py:582
  (13 shorter events, 0.1 us)
Async XLA Ops:
  0.6 9.2 %copy-start.1 = (bf16[1,1,128,1536]{3,2,1,0:T(8,128)(2,1)S(1)}, bf16[1,1,128,1536]{3,2,1,0:T(8,128)(2,1)}, u32[]{:S(2)}) copy-start(bf16[1,1,128,1536]{3,2,1,0:T(8,128)(2,1)} %param.7) | copy-start | bytes 1179652
  0.6 9.2 %copy-start.3 = (f32[1,1536]{1,0:T(1,128)S(1)}, f32[1,1536]{1,0:T(1,128)}, u32[]{:S(2)}) copy-start(f32[1,1536]{1,0:T(1,128)} %bias_ref.3) | copy-start | bytes 18436
  0.7 9.2 %copy-start.2 = (f32[1,31,1536]{2,0,1:T(1,128)S(1)}, f32[1,31,1536]{2,0,1:T(1,128)}, u32[]{:S(2)}) copy-start(f32[1,31,1536]{2,0,1:T(1,128)} %param.10) | copy-start | bytes 571396
  0.7 11.3 %collective-permute-start.1 = (bf16[128,2304]{1,0:T(8,128)(2,1)}, bf16[128,2304]{1,0:T(8,128)(2,1)S(1)}, u32[]{:S(2)}, u32[]{:S(2)}) collective-permute-start(bf16[128,2304]{1,0:T(8,128)(2,1)} %bitcast.18), channel_id=1, source_target_pairs={{0,6},{2,0},{4,2},{6,4},{1,7},{3,1},{5,3},{7,5},{8,14},{10,8},{12,... | collective-permute-start | bytes 1769480 | tf_op jit(solution)/shard_map/ppermute | solution.py:624
  5.1 4.8 %collective-permute-start = (bf16[32,1536]{1,0:T(8,128)(2,1)S(1)}, bf16[32,1536]{1,0:T(8,128)(2,1)S(1)}, u32[]{:S(2)}, u32[]{:S(2)}) collective-permute-start(bf16[32,1536]{1,0:T(8,128)(2,1)S(1)} %get-tuple-element.23), channel_id=1, source_target_pairs={{0,1},{1,0},{2,3},{3,2},{4,5},{5,4},{6,7},{7,6},{8,9},{9,8},{10,11... | collective-permute-start | bytes 294920 | tf_op jit(solution)/shard_map/ppermute | solution.py:627
  6.7 10.2 %collective-permute-start.2 = (bf16[160,768]{1,0:T(8,128)(2,1)S(1)}, bf16[160,768]{1,0:T(8,128)(2,1)S(1)}, u32[]{:S(2)}, u32[]{:S(2)}) collective-permute-start(bf16[160,768]{1,0:T(8,128)(2,1)S(1)} %get-tuple-element.28), channel_id=1, source_target_pairs={{0,7},{1,6},{2,1},{3,0},{4,3},{5,2},{6,5},{7,4},{8,15},{9,14},{10,... | collective-permute-start | bytes 737288 | tf_op jit(solution)/shard_map/ppermute | solution.py:628
  7.0 14.9 %collective-permute-start.3 = (bf16[128,1152]{1,0:T(8,128)(2,1)S(1)}, bf16[128,1152]{1,0:T(8,128)(2,1)S(1)}, u32[]{:S(2)}, u32[]{:S(2)}) collective-permute-start(bf16[128,1152]{1,0:T(8,128)(2,1)S(1)} %get-tuple-element.29), channel_id=1, source_target_pairs={{0,1},{1,0},{2,3},{3,2},{4,5},{5,4},{6,7},{7,6},{8,9},{9,8},{10,11... | collective-permute-start | bytes 884744 | tf_op jit(solution)/shard_map/ppermute | solution.py:629
  8.5 18.5 %collective-permute-start.4 = (bf16[128,1152]{1,0:T(8,128)(2,1)S(1)}, bf16[128,1152]{1,0:T(8,128)(2,1)S(1)}, u32[]{:S(2)}, u32[]{:S(2)}) collective-permute-start(bf16[128,1152]{1,0:T(8,128)(2,1)S(1)} %get-tuple-element.32), channel_id=1, source_target_pairs={{0,1},{1,0},{2,3},{3,2},{4,5},{5,4},{6,7},{7,6},{8,9},{9,8},{10,11... | collective-permute-start | bytes 884744 | tf_op jit(solution)/shard_map/ppermute | solution.py:629
  14.2 5.1 %collective-permute-start.5 = (bf16[32,1536]{1,0:T(8,128)(2,1)S(1)}, bf16[32,1536]{1,0:T(8,128)(2,1)S(1)}, u32[]{:S(2)}, u32[]{:S(2)}) collective-permute-start(bf16[32,1536]{1,0:T(8,128)(2,1)S(1)} %get-tuple-element.37.mine_ref), channel_id=1, source_target_pairs={{0,8},{8,0},{16,24},{24,16},{1,9},{9,1},{17,25},{25,17},{2,10},{10... | collective-permute-start | bytes 294920 | tf_op jit(solution)/shard_map/ppermute | solution.py:566
  16.9 5.1 %copy-start = (bf16[1,1,128,2304]{3,2,1,0:T(8,128)(2,1)S(1)}, bf16[1,1,128,2304]{3,2,1,0:T(8,128)(2,1)}, u32[]{:S(2)}) copy-start(bf16[1,1,128,2304]{3,2,1,0:T(8,128)(2,1)} %param.6) | copy-start | bytes 1769476
  19.3 5.6 %collective-permute-start.6 = (bf16[32,1536]{1,0:T(8,128)(2,1)S(1)}, bf16[32,1536]{1,0:T(8,128)(2,1)S(1)}, u32[]{:S(2)}, u32[]{:S(2)}) collective-permute-start(bf16[32,1536]{1,0:T(8,128)(2,1)S(1)} %add.4.mine_ref), channel_id=1, source_target_pairs={{0,16},{8,24},{16,0},{24,8},{1,17},{9,25},{17,1},{25,9},{2,18},{10... | collective-permute-start | bytes 294920 | tf_op jit(solution)/shard_map/ppermute | solution.py:566
  24.9 4.9 %collective-permute-start.7 = (bf16[32,1536]{1,0:T(8,128)(2,1)S(1)}, bf16[32,1536]{1,0:T(8,128)(2,1)S(1)}, u32[]{:S(2)}, u32[]{:S(2)}) collective-permute-start(bf16[32,1536]{1,0:T(8,128)(2,1)S(1)} %add.5.mine_ref), channel_id=1, source_target_pairs={{0,1},{1,0},{2,3},{3,2},{4,5},{5,4},{6,7},{7,6},{8,9},{9,8},{10,11... | collective-permute-start | bytes 294920 | tf_op jit(solution)/shard_map/ppermute | solution.py:566
